TPU v7x, 32 devices: a whole 2x2x4 slice. The times are simulated.
32 devices in a mesh: gx: 4 (over z), gz: 8 (over y, x, core).
Axes of the slice: x: 2, y: 2, z: 4, core: 2. Of those that a mesh axis runs over, the one named last changes fastest.
Arguments:
- velocity: float32 [256, 64, 256], P('gx', 'gz'), may hold values from -6 to 6
- viscosity: float32 [256, 64, 256], P('gx', 'gz'), may hold values from 0.5 to 5
- force: float32 [256, 64, 256], P('gx', 'gz'), may hold values from -30 to 30
Outputs:
- increment: float32 [256, 64, 256], P('gx', 'gz')
All inputs are finite; a program needn't handle non-finite values.
Results may differ from a plain program's by a relative error of at most 0.0005.
Values sent between devices are 32-bit elements; how exact they have to be, the bound alone decides.
No kernel may reach another device: no remote copies, remote signals or barrier semaphores. Data moves between devices by JAX's collectives and lax.ppermute only.
A program may use at most 128 MiB of HBM per device.

v0:
```python
import jax
import jax.numpy as jnp
from jax import lax
from jax.experimental import pallas as pl
from jax.experimental.pallas import tpu as pltpu
from jax.sharding import PartitionSpec as P

HALF_X = 0.5 * 1600.0 * 0.5
HALF_Y = 0.5 * 0.5 * 0.5
HALF_Z = 0.5 * 400.0 * 0.5

F32 = jnp.float32
VMEM = pl.BlockSpec(memory_space=pltpu.VMEM)
SMEM = pl.BlockSpec(memory_space=pltpu.SMEM)


def call(kernel, outs, n_in, scratch=(), cost=None):
    return pl.pallas_call(
        kernel,
        out_shape=tuple(jax.ShapeDtypeStruct(s, F32) for s in outs),
        in_specs=[SMEM] + [VMEM] * (n_in - 1),
        out_specs=tuple(VMEM for _ in outs),
        scratch_shapes=list(scratch),
        compiler_params=pltpu.CompilerParams(vmem_limit_bytes=48 << 20),
        cost_estimate=cost,
    )


def cost(elements, ops, touched):
    return pl.CostEstimate(flops=elements * ops, bytes_accessed=touched * 4, transcendentals=0)


def iota(shape, dim):
    return lax.broadcasted_iota(jnp.int32, shape, dim)


def shift(x, s, axis):
    return pltpu.roll(x, s % x.shape[axis], axis)


def x_factor_kernel(pos, visc, vel, force, c_out, n_out, gf_out, gl_out, coef, rhs, cf, cb):
    rows, depth, width = visc.shape
    mid = rows // 2
    lo_wall = jnp.where(pos[0] == 0, HALF_X, 0.0)
    hi_wall = jnp.where(pos[0] == pos[1] - 1, HALF_X, 0.0)
    s = 1.0 + lo_wall * visc[0]
    t = 1.0 + hi_wall * visc[rows - 1]
    lo_term = s - 1.0
    hi_term = t - 1.0
    for i in range(rows - 1):
        e = HALF_X * (visc[i] + visc[i + 1])
        r = 1.0 / (s + e)
        c = e * r
        cf[i] = c
        if i < mid:
            c_out[i] = c
            n_out[i] = r
        s = 1.0 + c * s
        if i + 1 == mid:
            s_mid = s
        j = rows - 1 - i
        e = HALF_X * (visc[j] + visc[j - 1])
        r = 1.0 / (t + e)
        c = e * r
        cb[j] = c
        if j > mid:
            c_out[j] = c
            n_out[j] = r
        t = 1.0 + c * t
        if j - 1 == mid:
            t_mid = t
    n_out[mid] = 1.0 / (s_mid + t_mid - 1.0)
    c_out[mid] = jnp.zeros_like(s)
    gl = 1.0 / (s + hi_term)
    gf = 1.0 / (t + lo_term)
    coef[0] = gf
    coef[2] = gl
    coef[3] = visc[0]
    coef[4] = visc[rows - 1]
    gl_out[rows - 1] = gl
    gf_out[0] = gf
    for i in range(rows - 1):
        gl = cf[rows - 2 - i] * gl
        gl_out[rows - 2 - i] = gl
        gf = cb[i + 1] * gf
        gf_out[i + 1] = gf
    coef[1] = gl

    lane = iota((depth, width), 1)
    sub = iota((depth, width), 0)
    for i in range(rows):
        v = vel[i]
        nu = visc[i]
        vn = jnp.where(lane == width - 1, 0.0, shift(v, -1, 1))
        nn = jnp.where(lane == width - 1, 0.0, shift(nu, -1, 1))
        fy = (2.0 * HALF_Y) * (nu + nn) * (vn - v)
        fl = jnp.where(lane == 0, (2.0 * HALF_Y) * nu * v, shift(fy, 1, 1))
        fz = (2.0 * HALF_Z) * (nu + shift(nu, -1, 0)) * (shift(v, -1, 0) - v)
        fz = jnp.where(sub == depth - 1, 0.0, fz)
        rhs[i] = force[i] + 2.0 * v + (fy - fl) + (fz - shift(fz, 1, 0))


def z_factor_kernel(pos, visc, al, ga, inv, gf_out, gl_out, planes):
    rows, depth, width = visc.shape
    lo_wall = jnp.where(pos[2] == 0, HALF_Z, 0.0)
    hi_wall = jnp.where(pos[2] == pos[3] - 1, HALF_Z, 0.0)
    sub = iota((depth, width), 0)
    wall = jnp.where(sub == 0, lo_wall, jnp.where(sub == depth - 1, hi_wall, 0.0))
    first = jnp.where(sub == 0, 1.0, 0.0)
    last = jnp.where(sub == depth - 1, 1.0, 0.0)
    for i in range(rows):
        nu = visc[i]
        e = jnp.where(sub == depth - 1, 0.0, HALF_Z * (nu + shift(nu, -1, 0)))
        sigma = 1.0 + wall * nu
        b = sigma + e + shift(e, 1, 0)
        gf, gl = first, last
        s, k = 1, 0
        while s < depth:
            r = 1.0 / b
            a = shift(e * r, s, 0)
            g = e * shift(r, -s, 0)
            al[k, i] = a
            ga[k, i] = g
            e = g * shift(e, -s, 0)
            sigma = sigma + a * shift(sigma, s, 0) + g * shift(sigma, -s, 0)
            gf = gf + a * shift(gf, s, 0) + g * shift(gf, -s, 0)
            gl = gl + a * shift(gl, s, 0) + g * shift(gl, -s, 0)
            s *= 2
            k += 1
            b = sigma + e + shift(e, s, 0) if s < depth else sigma
        r = 1.0 / b
        gf = gf * r
        gl = gl * r
        inv[i] = r
        gf_out[i] = gf
        gl_out[i] = gl
        planes[0, i] = gf[0]
        planes[1, i] = gf[depth - 1]
        planes[2, i] = gl[depth - 1]


def y_factor_kernel(pos, visc, al, ga, inv):
    rows, depth, width = visc.shape
    block = 4
    shape = (block, depth, width)
    lane = iota(shape, 2)

    def body(i, carry):
        at = pl.ds(i * block, block)
        nu = visc[at]
        wall = jnp.where((lane == 0) | (lane == width - 1), HALF_Y, 0.0) * nu
        e = jnp.where(lane == width - 1, 0.0, HALF_Y * (nu + shift(nu, -1, 2)))
        b = 1.0 + wall + e + shift(e, 1, 2)
        s, k = 1, 0
        while s < width:
            r = 1.0 / b
            er = e * r
            a = shift(er, s, 2)
            g = e * shift(r, -s, 2)
            al[k, at] = a
            ga[k, at] = g
            b = b - g * e - shift(er * e, s, 2)
            e = g * shift(e, -s, 2)
            s *= 2
            k += 1
        inv[at] = 1.0 / b
        return carry

    lax.fori_loop(0, rows // block, body, 0)


def x_solve_kernel(pos, visc, vel, rhs0, c_in, n_in, coef, pair, cross, w_out, payload):
    rows, depth, width = visc.shape
    mid = rows // 2
    sub = iota((depth, width), 0)
    upper = lax.rem(pos[2], 2)
    from_pair = (sub >= depth // 2) == (upper == 0)
    edge = (sub == 0) | (sub == depth - 1)

    def rhs(i):
        n_vel = jnp.where(from_pair, pair[0, pl.ds(i, 1)], cross[0, pl.ds(i, 1)])
        n_visc = jnp.where(from_pair, pair[1, pl.ds(i, 1)], cross[1, pl.ds(i, 1)])
        extra = (2.0 * HALF_Z) * (visc[i] + n_visc) * (n_vel - vel[i])
        return rhs0[i] + jnp.where(edge, extra, 0.0)

    d = rhs(0)
    w_out[0] = d
    u = rhs(rows - 1)
    w_out[rows - 1] = u
    for i in range(1, mid):
        d = rhs(i) + c_in[i - 1] * d
        w_out[i] = d
        j = rows - 1 - i
        if j > mid:
            u = rhs(j) + c_in[j + 1] * u
            w_out[j] = u
    d = rhs(mid) + c_in[mid - 1] * d + c_in[mid + 1] * u
    d = d * n_in[mid]
    w_out[mid] = d
    u = d
    for i in range(1, mid + 1):
        j = mid - i
        d = w_out[j] * n_in[j] + c_in[j] * d
        w_out[j] = d
        j = mid + i
        if j < rows:
            u = w_out[j] * n_in[j] + c_in[j] * u
            w_out[j] = u
    payload[0] = d
    payload[1] = u
    for k in range(5):
        payload[2 + k] = coef[k]


def make_middle_kernel(n):
    def kernel(pos, *refs):
        parts = refs[:n]
        (w, gf, gl, vel, yal, yga, yinv, zal, zga, zinv, dz, ends, slots, flux) = refs[n:]
        rows, depth, width = w.shape
        me = pos[0]
        for k in range(n):
            slots[jnp.bitwise_xor(me, k)] = parts[k][...]
        zero = jnp.zeros((depth, width), F32)
        flux[0] = zero
        flux[n] = zero
        lower, source = [], []
        for f in range(n - 1):
            e = HALF_X * (slots[f, 6] + slots[f + 1, 5])
            pivot = 1.0 / e + slots[f, 4] + slots[f + 1, 2]
            right = slots[f + 1, 0] - slots[f, 1]
            if f:
                pivot = pivot - slots[f, 3] * lower[-1]
                right = right + lower[-1] * source[-1]
            r = 1.0 / pivot
            lower.append(slots[f + 1, 3] * r)
            source.append(right)
            flux[f + 1] = right * r
        q = flux[n - 1] if n > 1 else zero
        for f in reversed(range(n - 2)):
            q = flux[f + 1] + lower[f] * q
            flux[f + 1] = q
        q_left = flux[me]
        q_right = flux[me + 1]
        block = 4
        steps_y = yal.shape[0]
        steps_z = zal.shape[0]

        def body(i, carry):
            at = pl.ds(i * block, block)
            d = w[at] + q_right * gl[at] - q_left * gf[at] - 2.0 * vel[at]
            for k in range(steps_y):
                d = d + yal[k, at] * shift(d, 1 << k, 2) + yga[k, at] * shift(d, -(1 << k), 2)
            d = d * yinv[at]
            for k in range(steps_z):
                d = d + zal[k, at] * shift(d, 1 << k, 1) + zga[k, at] * shift(d, -(1 << k), 1)
            d = d * zinv[at]
            dz[at] = d
            for j in range(block):
                ends[0, pl.ds(i * block + j, 1)] = d[j, 0:1]
                ends[1, pl.ds(i * block + j, 1)] = d[j, depth - 1:depth]
            return carry

        lax.fori_loop(0, rows // block, body, 0)

    return kernel


def final_kernel(pos, dz, gf, gl, q_left, q_right, out):
    rows = dz.shape[0]
    for i in range(rows):
        out[i] = dz[i] + q_right[pl.ds(i, 1)] * gl[i] - q_left[pl.ds(i, 1)] * gf[i]


def ordered(parts, me):
    bit = 1
    parts = list(parts)
    while bit < len(parts):
        odd = (me & bit) != 0
        parts = [jnp.where(odd, parts[i ^ bit], parts[i]) for i in range(len(parts))]
        bit *= 2
    return parts


def local(velocity, viscosity, force):
    rows, depth, width = velocity.shape
    nx, nz = lax.axis_size("gx"), lax.axis_size("gz")
    chips = nz // 2
    ix, iz = lax.axis_index("gx"), lax.axis_index("gz")
    upper = iz % 2
    chip = iz // 2
    pos = jnp.stack([ix, jnp.int32(nx), iz, jnp.int32(nz)]).astype(jnp.int32)
    volume = (rows, depth, width)
    size = rows * depth * width
    steps_y = (width - 1).bit_length()
    steps_z = (depth - 1).bit_length()

    pair_route = [(i, i ^ 1) for i in range(nz)]
    cross_route = [(i, i + 1 if i % 2 else i - 1) for i in range(1, nz - 1)]
    both = jnp.stack([velocity, viscosity])
    near_z = jnp.where(upper == 0, depth - 1, 0)
    far_z = jnp.where(upper == 0, 0, depth - 1)
    to_pair = lax.dynamic_index_in_dim(both, near_z, 2, keepdims=False)
    to_cross = lax.dynamic_index_in_dim(both, far_z, 2, keepdims=False)
    pair = lax.ppermute(to_pair, "gz", pair_route)
    cross = lax.ppermute(to_cross, "gz", cross_route)

    plane = (depth, width)
    slab = (rows, width)
    c_x, n_x, gf_x, gl_x, coef, rhs0 = call(
        x_factor_kernel,
        [volume] * 4 + [(5,) + plane, volume], 4,
        [pltpu.VMEM(volume, F32)] * 2, cost(size, 60, 9 * size),
    )(pos, viscosity, velocity, force)
    al_z, ga_z, inv_z, gf_z, gl_z, planes = call(
        z_factor_kernel,
        [(steps_z,) + volume] * 2 + [volume] * 3 + [(3,) + slab], 2, (), cost(size, 60, 10 * size),
    )(pos, viscosity)
    al_y, ga_y, inv_y = call(
        y_factor_kernel, [(steps_y,) + volume] * 2 + [volume], 2, (), cost(size, 200, 18 * size)
    )(pos, viscosity)

    w, payload = call(
        x_solve_kernel, [volume, (7,) + plane], 9, (), cost(size, 20, 6 * size)
    )(pos, viscosity, velocity, rhs0, c_x, n_x, coef, pair, cross)
    parts = [payload] + [
        lax.ppermute(payload, "gx", [(i, i ^ k) for i in range(nx)]) for k in range(1, nx)
    ]

    right_face = jnp.where(upper == 0, pair[1], cross[1])
    reach = 1.0 / (HALF_Z * (viscosity[:, depth - 1] + right_face))
    own_c = jnp.concatenate([planes, reach[None]])
    mate_c = lax.ppermute(own_c, "gz", pair_route)
    low_c = jnp.where(upper == 0, own_c, mate_c)
    high_c = jnp.where(upper == 0, mate_c, own_c)
    weight = 1.0 / (low_c[3] + low_c[2] + high_c[0])
    low_fl, high_fl = low_c[1], high_c[1]
    chip_c = jnp.stack([
        low_c[0] - weight * low_fl * low_fl,
        weight * low_fl * high_fl,
        high_c[2] - weight * high_fl * high_fl + high_c[3],
    ])
    groups = [[2 * c + p for c in range(chips)] for p in range(2)]
    all_c = lax.all_gather(chip_c, "gz", axis_index_groups=groups)

    dz, ends = call(
        make_middle_kernel(nx), [volume, (2,) + slab], 11 + nx,
        [pltpu.VMEM((nx, 7) + plane, F32), pltpu.VMEM((nx + 1,) + plane, F32)],
        cost(size, 100, 32 * size),
    )(pos, *parts, w, gf_x, gl_x, velocity, al_y, ga_y, inv_y, al_z, ga_z, inv_z)

    mate = lax.ppermute(ends, "gz", pair_route)
    low = jnp.where(upper == 0, ends, mate)
    high = jnp.where(upper == 0, mate, ends)
    jump = high[0] - low[1]
    q_mid = weight * jump
    chip_ends = jnp.stack([low[0] + low_fl * q_mid, high[1] - high_fl * q_mid])
    others = [chip_ends] + [
        lax.ppermute(chip_ends, "gz", [(i, i ^ (2 * k)) for i in range(nz)])
        for k in range(1, chips)
    ]
    by_chip = ordered(others, chip)
    lower, source, fluxes = [], [], []
    for f in range(chips - 1):
        pivot = all_c[f, 2] + all_c[f + 1, 0]
        right = by_chip[f + 1][0] - by_chip[f][1]
        if f:
            pivot = pivot - all_c[f, 1] * lower[-1]
            right = right + lower[-1] * source[-1]
        r = 1.0 / pivot
        lower.append(all_c[f + 1, 1] * r)
        source.append(right)
        fluxes.append(right * r)
    for f in reversed(range(chips - 2)):
        fluxes[f] = fluxes[f] + lower[f] * fluxes[f + 1]
    zero = jnp.zeros(slab, F32)
    chip_left, chip_right = zero, zero
    for f in range(chips - 1):
        chip_right = jnp.where(chip == f, fluxes[f], chip_right)
        chip_left = jnp.where(chip == f + 1, fluxes[f], chip_left)
    q_mid = weight * (jump + chip_right * high_fl + chip_left * low_fl)
    q_left = jnp.where(upper == 0, chip_left, q_mid)
    q_right = jnp.where(upper == 0, q_mid, chip_right)
    return call(final_kernel, [volume], 6, (), cost(size, 4, 4 * size))(
        pos, dz, gf_z, gl_z, q_left, q_right
    )[0]


def solution(mesh):
    return jax.shard_map(
        local,
        mesh=mesh,
        in_specs=(P("gx", "gz", None), P("gx", "gz", None), P("gx", "gz", None)),
        out_specs=P("gx", "gz", None),
        check_vma=False,
    )
```

profile of v0, /device:TPU:0, one launch (start us, length us, event | category | flops | bytes accessed | tf_op | source)
XLA Modules:
  0.0 81.2 jit_solution(10985336267703746102)
XLA Ops:
  0.0 0.0 copy-start.2
  0.0 1.8 %fusion = (f32[2,64,1,256]{3,2,1,0:T(1,128)S(1)}, f32[2,64,1,256]{3,2,1,0:T(1,128)S(1)}) fusion(s32[]{:T(128)S(6)} %select_n.134, f32[1,64,8,256]{3,2,1,0:T(8,128)} %bitcast.106, f32[1,64,8,256]{3,2,1,0:T(8,128)} %bitcast.105, s32[]{:T(128)S(6)} %select_n.133), kind=kLoop, calls=%fused_computation.6 | loop fusion | flops 65536 | bytes 1310728 | tf_op jit(solution)/shard_map/stack | solution.py:299
  1.8 0.5 collective-permute-start
  2.3 0.7 collective-permute-start.1
  3.0 1.1 %slice.90 = f32[64,1,256]{2,1,0:T(1,128)S(1)} slice(f32[64,8,256]{2,1,0:T(8,128)} %visc.7), slice={[0:64], [7:8], [0:256]} | slice | bytes 131072 | tf_op jit(solution)/shard_map/slice | solution.py:330
  4.1 0.1 pad_add_fusion.pos
  4.2 0.0 copy-start
  4.2 1.0 %copy-done = f32[64,8,256]{2,1,0:T(8,128)S(1)} copy-done((f32[64,8,256]{2,1,0:T(8,128)S(1)}, f32[64,8,256]{2,1,0:T(8,128)}, u32[]{:S(2)}) %copy-start) | copy-done | bytes 524312
  5.2 2.1 %shard_map.40 = (f32[3,64,8,256]{3,2,1,0:T(8,128)S(1)}, f32[3,64,8,256]{3,2,1,0:T(8,128)S(1)}, f32[64,8,256]{2,1,0:T(8,128)S(1)}, f32[64,8,256]{2,1,0:T(8,128)S(...) custom-call(s32[4]{0:T(128)S(1)} %pad_add_fusion.pos, f32[64,8,256]{2,1,0:T(8,128)S(1)} %copy-done), custom_call_target="tpu_custom_call" | custom-call | flops 7864320 | bytes 5242880 | tf_op jit(solution)/shard_map/pallas_call | solution.py:314
  7.3 0.0 copy-start.4
  7.3 1.2 %copy-done.4 = f32[3,64,8,256]{3,2,1,0:T(8,128)} copy-done((f32[3,64,8,256]{3,2,1,0:T(8,128)}, f32[3,64,8,256]{3,2,1,0:T(8,128)S(1)}, u32[]{:S(2)}) %copy-start.4) | copy-done | bytes 1572888
  8.5 0.0 copy-start.1
  8.5 1.0 %copy-done.1 = f32[64,8,256]{2,1,0:T(8,128)S(1)} copy-done((f32[64,8,256]{2,1,0:T(8,128)S(1)}, f32[64,8,256]{2,1,0:T(8,128)}, u32[]{:S(2)}) %copy-start.1) | copy-done | bytes 524312
  9.6 0.0 copy-start.5
  9.6 1.0 %copy-done.5 = f32[64,8,256]{2,1,0:T(8,128)S(1)} copy-done((f32[64,8,256]{2,1,0:T(8,128)S(1)}, f32[64,8,256]{2,1,0:T(8,128)}, u32[]{:S(2)}) %copy-start.5) | copy-done | bytes 524312
  10.6 3.9 %shard_map.37 = (f32[64,8,256]{2,1,0:T(8,128)S(1)}, f32[64,8,256]{2,1,0:T(8,128)S(1)}, f32[64,8,256]{2,1,0:T(8,128)S(1)}, f32[64,8,256]{2,1,0:T(8,128)S(1)}, f32...) custom-call(s32[4]{0:T(128)S(1)} %pad_add_fusion.pos, f32[64,8,256]{2,1,0:T(8,128)S(1)} %copy-done, ...), custom_call_target="tpu_custom_call" | custom-call | flops 7864320 | bytes 4718592 | tf_op jit(solution)/shard_map/pallas_call | solution.py:309
  14.5 15.2 %shard_map.39 = (f32[8,64,8,256]{3,2,1,0:T(8,128)S(1)}, f32[8,64,8,256]{3,2,1,0:T(8,128)}, f32[64,8,256]{2,1,0:T(8,128)S(1)}) custom-call(s32[4]{0:T(128)S(1)} %pad_add_fusion.pos, f32[64,8,256]{2,1,0:T(8,128)S(1)} %copy-done), custom_call_target="tpu_custom_call" | custom-call | flops 26214400 | bytes 9437184 | tf_op jit(solution)/shard_map/pallas_call | solution.py:318
  29.7 0.0 copy-start.3
  29.7 2.0 %copy-done.3 = f32[8,64,8,256]{3,2,1,0:T(8,128)} copy-done((f32[8,64,8,256]{3,2,1,0:T(8,128)}, f32[8,64,8,256]{3,2,1,0:T(8,128)S(1)}, u32[]{:S(2)}) %copy-start.3) | copy-done | bytes 4194328
  31.8 0.0 collective-permute-done.pair
  31.8 0.0 collective-permute-done.1.cross
  31.8 0.0 copy-done.2
  31.8 0.9 %shard_map.38 = (f32[64,8,256]{2,1,0:T(8,128)S(1)}, f32[7,8,256]{2,1,0:T(8,128)S(1)}) custom-call(s32[4]{0:T(128)S(1)} %pad_add_fusion.pos, f32[64,8,256]{2,1,0:T(8,128)S(1)} %copy-done, f32[64,8,256]{2,1,0:T(8,128)S(1)} %copy-done.2, f32[64,8,256]{2,1,0:T(8,128)S(1)} %get-tuple-element.24.rhs0, f32[64,8,256]{2,1,0:T(8,128)S(1)} %get-tuple-element.25.c_in, ...), custom_call_target="tpu_custom_call" | custom-call | flops 2621440 | bytes 3145728 | tf_op jit(solution)/shard_map/pallas_call | solution.py:322
  32.7 2.7 %collective-permute-start.2 = (f32[7,8,256]{2,1,0:T(8,128)S(1)}, f32[7,8,256]{2,1,0:T(8,128)S(1)}, u32[]{:S(2)}, u32[]{:S(2)}) collective-permute-start(f32[7,8,256]{2,1,0:T(8,128)S(1)} %get-tuple-element.28.refs_0_), channel_id=1, source_target_pairs={{0,8},{8,0},{16,24},{24,16},{1,9},{9,1},{17,25},{25,17},{2,10},{10... | collective-permute-start | bytes 172040 | tf_op jit(solution)/shard_map/ppermute | solution.py:326
  35.3 2.6 %collective-permute-start.3 = (f32[7,8,256]{2,1,0:T(8,128)S(1)}, f32[7,8,256]{2,1,0:T(8,128)S(1)}, u32[]{:S(2)}, u32[]{:S(2)}) collective-permute-start(f32[7,8,256]{2,1,0:T(8,128)S(1)} %get-tuple-element.28.refs_0_), channel_id=1, source_target_pairs={{0,16},{8,24},{16,0},{24,8},{1,17},{9,25},{17,1},{25,9},{2,18},{10... | collective-permute-start | bytes 172040 | tf_op jit(solution)/shard_map/ppermute | solution.py:326
  37.9 0.0 collective-permute-start.4
  37.9 0.0 collective-permute-done.2.refs_1_
  38.0 3.1 %collective-permute-done.3.refs_2_ = f32[7,8,256]{2,1,0:T(8,128)S(1)} collective-permute-done((f32[7,8,256]{2,1,0:T(8,128)S(1)}, f32[7,8,256]{2,1,0:T(8,128)S(1)}, u32[]{:S(2)}, u32[]{:S(2)}) %collective-permute-start.3) | collective-permute-done | bytes 57376 | tf_op jit(solution)/shard_map/ppermute | solution.py:326
  41.0 3.0 %collective-permute-done.4.refs_3_ = f32[7,8,256]{2,1,0:T(8,128)S(1)} collective-permute-done((f32[7,8,256]{2,1,0:T(8,128)S(1)}, f32[7,8,256]{2,1,0:T(8,128)S(1)}, u32[]{:S(2)}, u32[]{:S(2)}) %collective-permute-start.4) | collective-permute-done | bytes 57376 | tf_op jit(solution)/shard_map/ppermute | solution.py:326
  44.0 13.5 %shard_map.41 = (f32[64,8,256]{2,1,0:T(8,128)S(1)}, f32[2,64,256]{2,1,0:T(8,128)S(1)}) custom-call(s32[4]{0:T(128)S(1)} %pad_add_fusion.pos, f32[7,8,256]{2,1,0:T(8,128)S(1)} %get-tuple-element.28.refs_0_, f32[7,8,256]{2,1,0:T(8,128)S(1)} %collective-permute-done.2.refs_1_, f32[7,8,256]{2,1,0:T(8,128)S(1)} %collective-permute-done.3.refs_2_, ...), custom_call_target="tpu_custom_call" | custom-call | flops 13107200 | bytes 16777216 | tf_op jit(solution)/shard_map/pallas_call | solution.py:345
  57.5 1.1 %collective-permute-start.5 = (f32[2,64,256]{2,1,0:T(8,128)S(1)}, f32[2,64,256]{2,1,0:T(8,128)S(1)}, u32[]{:S(2)}, u32[]{:S(2)}) collective-permute-start(f32[2,64,256]{2,1,0:T(8,128)S(1)} %get-tuple-element.41), channel_id=1, source_target_pairs={{0,1},{1,0},{2,3},{3,2},{4,5},{5,4},{6,7},{7,6},{8,9},{9,8},{10,11... | collective-permute-start | bytes 393224 | tf_op jit(solution)/shard_map/ppermute | solution.py:351
  58.6 0.1 collective-permute-start.6
  58.7 0.9 %collective-permute-done.5 = f32[2,64,256]{2,1,0:T(8,128)S(1)} collective-permute-done((f32[2,64,256]{2,1,0:T(8,128)S(1)}, f32[2,64,256]{2,1,0:T(8,128)S(1)}, u32[]{:S(2)}, u32[]{:S(2)}) %collective-permute-start.5) | collective-permute-done | bytes 131104 | tf_op jit(solution)/shard_map/ppermute | solution.py:351
  59.6 0.6 collective-permute-done.6
  60.4 2.6 %collective-permute-start.7 = (f32[2,64,256]{2,1,0:T(8,128)S(1)}, f32[2,64,256]{2,1,0:T(8,128)S(1)}, u32[]{:S(2)}, u32[]{:S(2)}) collective-permute-start(f32[2,64,256]{2,1,0:T(8,128)S(1)} %pad_maximum_fusion.2), channel_id=1, source_target_pairs={{0,2},{1,3},{2,0},{3,1},{4,6},{5,7},{6,4},{7,5},{8,10},{9,11},{10,... | collective-permute-start | bytes 393224 | tf_op jit(solution)/shard_map/ppermute | solution.py:358
  63.0 1.3 %collective-permute-start.8 = (f32[2,64,256]{2,1,0:T(8,128)S(1)}, f32[2,64,256]{2,1,0:T(8,128)S(1)}, u32[]{:S(2)}, u32[]{:S(2)}) collective-permute-start(f32[2,64,256]{2,1,0:T(8,128)S(1)} %pad_maximum_fusion.2), channel_id=1, source_target_pairs={{0,4},{1,5},{2,6},{3,7},{4,0},{5,1},{6,2},{7,3},{8,12},{9,13},{10,... | collective-permute-start | bytes 393224 | tf_op jit(solution)/shard_map/ppermute | solution.py:358
  64.3 0.9 %collective-permute-start.9 = (f32[2,64,256]{2,1,0:T(8,128)S(1)}, f32[2,64,256]{2,1,0:T(8,128)S(1)}, u32[]{:S(2)}, u32[]{:S(2)}) collective-permute-start(f32[2,64,256]{2,1,0:T(8,128)S(1)} %pad_maximum_fusion.2), channel_id=1, source_target_pairs={{0,6},{1,7},{2,4},{3,5},{4,2},{5,3},{6,0},{7,1},{8,14},{9,15},{10,... | collective-permute-start | bytes 393224 | tf_op jit(solution)/shard_map/ppermute | solution.py:358
  65.2 14.1 %all-gather = f32[12,64,256]{2,1,0:T(8,128)S(1)} all-gather(f32[3,64,256]{2,1,0:T(8,128)S(1)} %pad_maximum_fusion.1), channel_id=2, replica_groups={{0,2,4,6},{1,3,5,7},{8,10,12,14},{9,11,13,15},{16,18,20,22},{17,19,21,2..., dimensions={0}, use_global_device_ids=true | all-gather | bytes 983040 | tf_op jit(solution)/shard_map/all_gather | solution.py:343
  79.4 0.0 collective-permute-done.7
  79.4 0.0 collective-permute-done.8
  79.4 0.0 collective-permute-done.9
  79.4 0.1 broadcast_select_fusion.8
  79.5 0.1 select_select_fusion
  79.6 0.1 broadcast_select_fusion.10
  79.7 1.5 %shard_map.42 = f32[64,8,256]{2,1,0:T(8,128)} custom-call(s32[4]{0:T(128)S(1)} %pad_add_fusion.pos, f32[64,8,256]{2,1,0:T(8,128)S(1)} %get-tuple-element.38.dz, f32[64,8,256]{2,1,0:T(8,128)S(1)} %get-tuple-element.39.gf, f32[64,8,256]{2,1,0:T(8,128)S(1)} %get-tuple-element.40.gl, f32[64,256]{1,0:T(8,128)S(1)} %broadcast_select_fusion.11.q_left, ...), custom_call_target="tpu_custom_call" | custom-call | flops 524288 | bytes 2097152 | tf_op jit(solution)/shard_map/pallas_call | solution.py:383
  (11 shorter events, 0.2 us)
Async XLA Ops:
  0.0 31.8 %copy-start.2 = (f32[64,8,256]{2,1,0:T(8,128)S(1)}, f32[64,8,256]{2,1,0:T(8,128)}, u32[]{:S(2)}) copy-start(f32[64,8,256]{2,1,0:T(8,128)} %refs_7_.1) | copy-start | bytes 1572868
  1.8 30.0 %collective-permute-start = (f32[2,64,256]{2,1,0:T(8,128)S(1)}, f32[2,64,256]{2,1,0:T(8,128)S(1)}, u32[]{:S(2)}, u32[]{:S(2)}) collective-permute-start(f32[2,64,256]{2,1,0:T(8,128)S(1)} %bitcast.109), channel_id=1, source_target_pairs={{0,1},{1,0},{2,3},{3,2},{4,5},{5,4},{6,7},{7,6},{8,9},{9,8},{10,11... | collective-permute-start | bytes 393224 | tf_op jit(solution)/shard_map/ppermute | solution.py:304
  2.3 29.4 %collective-permute-start.1 = (f32[2,64,256]{2,1,0:T(8,128)S(1)}, f32[2,64,256]{2,1,0:T(8,128)S(1)}, u32[]{:S(2)}, u32[]{:S(2)}) collective-permute-start(f32[2,64,256]{2,1,0:T(8,128)S(1)} %bitcast.110), channel_id=1, source_target_pairs={{1,2},{2,1},{3,4},{4,3},{5,6},{6,5},{9,10},{10,9},{11,12},{12,11},... | collective-permute-start | bytes 393224 | tf_op jit(solution)/shard_map/ppermute | solution.py:305
  4.2 1.0 %copy-start = (f32[64,8,256]{2,1,0:T(8,128)S(1)}, f32[64,8,256]{2,1,0:T(8,128)}, u32[]{:S(2)}) copy-start(f32[64,8,256]{2,1,0:T(8,128)} %visc.7) | copy-start | bytes 1572868
  7.3 1.2 %copy-start.4 = (f32[3,64,8,256]{3,2,1,0:T(8,128)}, f32[3,64,8,256]{3,2,1,0:T(8,128)S(1)}, u32[]{:S(2)}) copy-start(f32[3,64,8,256]{3,2,1,0:T(8,128)S(1)} %get-tuple-element.36.refs_12_) | copy-start | bytes 4718596
  8.5 1.0 %copy-start.1 = (f32[64,8,256]{2,1,0:T(8,128)S(1)}, f32[64,8,256]{2,1,0:T(8,128)}, u32[]{:S(2)}) copy-start(f32[64,8,256]{2,1,0:T(8,128)} %refs_7_.1) | copy-start | bytes 1572868
  9.6 1.0 %copy-start.5 = (f32[64,8,256]{2,1,0:T(8,128)S(1)}, f32[64,8,256]{2,1,0:T(8,128)}, u32[]{:S(2)}) copy-start(f32[64,8,256]{2,1,0:T(8,128)} %force.1) | copy-start | bytes 1572868
  29.7 2.0 %copy-start.3 = (f32[8,64,8,256]{3,2,1,0:T(8,128)}, f32[8,64,8,256]{3,2,1,0:T(8,128)S(1)}, u32[]{:S(2)}) copy-start(f32[8,64,8,256]{3,2,1,0:T(8,128)S(1)} %get-tuple-element.32.refs_8_) | copy-start | bytes 12582916
  32.7 5.3 %collective-permute-start.2 = (f32[7,8,256]{2,1,0:T(8,128)S(1)}, f32[7,8,256]{2,1,0:T(8,128)S(1)}, u32[]{:S(2)}, u32[]{:S(2)}) collective-permute-start(f32[7,8,256]{2,1,0:T(8,128)S(1)} %get-tuple-element.28.refs_0_), channel_id=1, source_target_pairs={{0,8},{8,0},{16,24},{24,16},{1,9},{9,1},{17,25},{25,17},{2,10},{10... | collective-permute-start | bytes 172040 | tf_op jit(solution)/shard_map/ppermute | solution.py:326
  35.3 5.7 %collective-permute-start.3 = (f32[7,8,256]{2,1,0:T(8,128)S(1)}, f32[7,8,256]{2,1,0:T(8,128)S(1)}, u32[]{:S(2)}, u32[]{:S(2)}) collective-permute-start(f32[7,8,256]{2,1,0:T(8,128)S(1)} %get-tuple-element.28.refs_0_), channel_id=1, source_target_pairs={{0,16},{8,24},{16,0},{24,8},{1,17},{9,25},{17,1},{25,9},{2,18},{10... | collective-permute-start | bytes 172040 | tf_op jit(solution)/shard_map/ppermute | solution.py:326
  37.9 6.1 %collective-permute-start.4 = (f32[7,8,256]{2,1,0:T(8,128)S(1)}, f32[7,8,256]{2,1,0:T(8,128)S(1)}, u32[]{:S(2)}, u32[]{:S(2)}) collective-permute-start(f32[7,8,256]{2,1,0:T(8,128)S(1)} %get-tuple-element.28.refs_0_), channel_id=1, source_target_pairs={{0,24},{8,16},{16,8},{24,0},{1,25},{9,17},{17,9},{25,1},{2,26},{10... | collective-permute-start | bytes 172040 | tf_op jit(solution)/shard_map/ppermute | solution.py:326
  57.5 2.1 %collective-permute-start.5 = (f32[2,64,256]{2,1,0:T(8,128)S(1)}, f32[2,64,256]{2,1,0:T(8,128)S(1)}, u32[]{:S(2)}, u32[]{:S(2)}) collective-permute-start(f32[2,64,256]{2,1,0:T(8,128)S(1)} %get-tuple-element.41), channel_id=1, source_target_pairs={{0,1},{1,0},{2,3},{3,2},{4,5},{5,4},{6,7},{7,6},{8,9},{9,8},{10,11... | collective-permute-start | bytes 393224 | tf_op jit(solution)/shard_map/ppermute | solution.py:351
  58.6 1.6 %collective-permute-start.6 = (f32[4,64,256]{2,1,0:T(8,128)S(1)}, f32[4,64,256]{2,1,0:T(8,128)S(1)}, u32[]{:S(2)}, u32[]{:S(2)}) collective-permute-start(f32[4,64,256]{2,1,0:T(8,128)S(1)} %pad_maximum_fusion), channel_id=1, source_target_pairs={{0,1},{1,0},{2,3},{3,2},{4,5},{5,4},{6,7},{7,6},{8,9},{9,8},{10,11... | collective-permute-start | bytes 786440 | tf_op jit(solution)/shard_map/ppermute | solution.py:332
  60.4 19.0 %collective-permute-start.7 = (f32[2,64,256]{2,1,0:T(8,128)S(1)}, f32[2,64,256]{2,1,0:T(8,128)S(1)}, u32[]{:S(2)}, u32[]{:S(2)}) collective-permute-start(f32[2,64,256]{2,1,0:T(8,128)S(1)} %pad_maximum_fusion.2), channel_id=1, source_target_pairs={{0,2},{1,3},{2,0},{3,1},{4,6},{5,7},{6,4},{7,5},{8,10},{9,11},{10,... | collective-permute-start | bytes 393224 | tf_op jit(solution)/shard_map/ppermute | solution.py:358
  63.0 16.4 %collective-permute-start.8 = (f32[2,64,256]{2,1,0:T(8,128)S(1)}, f32[2,64,256]{2,1,0:T(8,128)S(1)}, u32[]{:S(2)}, u32[]{:S(2)}) collective-permute-start(f32[2,64,256]{2,1,0:T(8,128)S(1)} %pad_maximum_fusion.2), channel_id=1, source_target_pairs={{0,4},{1,5},{2,6},{3,7},{4,0},{5,1},{6,2},{7,3},{8,12},{9,13},{10,... | collective-permute-start | bytes 393224 | tf_op jit(solution)/shard_map/ppermute | solution.py:358
  64.3 15.1 %collective-permute-start.9 = (f32[2,64,256]{2,1,0:T(8,128)S(1)}, f32[2,64,256]{2,1,0:T(8,128)S(1)}, u32[]{:S(2)}, u32[]{:S(2)}) collective-permute-start(f32[2,64,256]{2,1,0:T(8,128)S(1)} %pad_maximum_fusion.2), channel_id=1, source_target_pairs={{0,6},{1,7},{2,4},{3,5},{4,2},{5,3},{6,0},{7,1},{8,14},{9,15},{10,... | collective-permute-start | bytes 393224 | tf_op jit(solution)/shard_map/ppermute | solution.py:358
where the time goes:
time: 81.5 us; the launch traced here: 81.2 us
  Pallas kernels  37.1 us (46%)
  blocking collectives  14.1 us (17%)
  starting transfers between devices  12.4 us (15%)
  waiting for transfers between devices  7.53 us (9%)
  local copies, waits for them, and re-layouts  7.48 us (9%)
  other arithmetic  2.31 us (3%)
    pallas_call x1, Pallas kernels, local(): call(y_factor_kernel, [(steps_y,) + volume] * 2 + [volume], 2, (), cost(s...  15.2 us
    all_gather x1, blocking collectives, local(): all_c = lax.all_gather(chip_c, 'gz', axis_index_groups=groups)  14.1 us
    pallas_call x1, Pallas kernels, local(): call(make_middle_kernel(nx), [volume, (2,) + slab], 11 + nx, [pltpu.VMEM(...  13.5 us
    unnamed x14, local copies, waits for them, and re-layouts  6.38 us
    ppermute x3, waiting for transfers between devices, local(): lax.ppermute(payload, 'gx', [(i, i ^ k) for i in range(nx)])  6.05 us
    ppermute x3, starting transfers between devices, local(): lax.ppermute(payload, 'gx', [(i, i ^ k) for i in range(nx)])  5.25 us
    ppermute x3, starting transfers between devices, local(): lax.ppermute(chip_ends, 'gz', [(i, i ^ 2 * k) for i in range(nz)])  4.83 us
    pallas_call x1, Pallas kernels, local(): call(x_factor_kernel, [volume] * 4 + [(5,) + plane, volume], 4, [pltpu.VM...  3.9 us
  transfers between devices with their start and end apart: 10, of which 4 were waited for; matrix products, arithmetic and copies ran while one was open for 2% of the time, Pallas kernels for 26%

commit v1 on v0

v1 whole, which is shorter than its diff:
```python
import jax
import jax.numpy as jnp
from jax import lax
from jax.experimental import pallas as pl
from jax.experimental.pallas import tpu as pltpu
from jax.sharding import PartitionSpec as P

HALF_X = 0.5 * 1600.0 * 0.5
HALF_Y = 0.5 * 0.5 * 0.5
HALF_Z = 0.5 * 400.0 * 0.5
Y_CHUNKS = 8

F32 = jnp.float32
VMEM = pl.BlockSpec(memory_space=pltpu.VMEM)
SMEM = pl.BlockSpec(memory_space=pltpu.SMEM)
HBM = pl.BlockSpec(memory_space=pltpu.HBM)


def call(kernel, outs, ins, scratch=(), flops=0, touched=0, out_specs=None):
    return pl.pallas_call(
        kernel,
        out_shape=tuple(jax.ShapeDtypeStruct(s, F32) for s in outs),
        in_specs=[SMEM] + ins,
        out_specs=tuple(out_specs or [VMEM] * len(outs)),
        scratch_shapes=list(scratch),
        compiler_params=pltpu.CompilerParams(vmem_limit_bytes=8 << 20),
        cost_estimate=pl.CostEstimate(
            flops=flops, bytes_accessed=4 * touched, transcendentals=0
        ),
    )


def iota(shape, dim):
    return lax.broadcasted_iota(jnp.int32, shape, dim)


def shift(x, s, axis):
    return pltpu.roll(x, s % x.shape[axis], axis)


def factor(
    nu, rows, half, lo_term, hi_term, c_out, n_out, gf_out, gl_out, cf, cb,
    beside_pivots=lambda i: None, beside_responses=lambda i: None,
):
    mid = rows // 2
    s, t = 1.0 + lo_term, 1.0 + hi_term
    for i in range(rows - 1):
        e = half * (nu(i) + nu(i + 1))
        r = 1.0 / (s + e)
        c = e * r
        cf[i] = c
        if i < mid:
            c_out[i] = c
            n_out[i] = r
        s = 1.0 + c * s
        if i + 1 == mid:
            s_mid = s
        j = rows - 1 - i
        e = half * (nu(j) + nu(j - 1))
        r = 1.0 / (t + e)
        c = e * r
        cb[j] = c
        if j > mid:
            c_out[j] = c
            n_out[j] = r
        t = 1.0 + c * t
        if j - 1 == mid:
            t_mid = t
        beside_pivots(i)
    n_out[mid] = 1.0 / (s_mid + t_mid - 1.0)
    gl = 1.0 / (s + hi_term)
    gf = 1.0 / (t + lo_term)
    beside_pivots(rows - 1)
    ends = [gf, None, gl]
    gl_out[rows - 1] = gl
    gf_out[0] = gf
    for i in range(rows - 1):
        gl = cf[rows - 2 - i] * gl
        gl_out[rows - 2 - i] = gl
        gf = cb[i + 1] * gf
        gf_out[i + 1] = gf
        beside_responses(i)
    beside_responses(rows - 1)
    ends[1] = gl
    return ends


def block_solve(rhs, rows, c, n, out):
    mid = rows // 2
    d = rhs(0)
    out[0] = d
    u = rhs(rows - 1)
    out[rows - 1] = u
    for i in range(1, mid):
        d = rhs(i) + c[i - 1] * d
        out[i] = d
        j = rows - 1 - i
        if j > mid:
            u = rhs(j) + c[j + 1] * u
            out[j] = u
    d = (rhs(mid) + c[mid - 1] * d + c[mid + 1] * u) * n[mid]
    out[mid] = d
    u = d
    for i in range(1, mid + 1):
        j = mid - i
        d = out[j] * n[j] + c[j] * d
        out[j] = d
        j = mid + i
        if j < rows:
            u = out[j] * n[j] + c[j] * u
            out[j] = u
    return d, u


def load_kernel(pos, visc_hbm, vel_hbm, visc, vel, visc_z, near, far, vel_z, sems):
    rows, depth, width = visc.shape
    copies = []
    half = rows // 2
    for k, (src, dst) in enumerate(((visc_hbm, visc), (vel_hbm, vel))):
        for p in range(2):
            at = pl.ds(p * half, half)
            copies.append(pltpu.make_async_copy(src.at[at], dst.at[at], sems.at[k, p]))
    for c in copies:
        c.start()
    upper = lax.rem(pos[2], 2)
    near_at = (1 - upper) * (depth - 1)
    far_at = upper * (depth - 1)
    for k, (dst, turned) in enumerate(((visc, visc_z), (vel, vel_z))):
        for p in range(2):
            copies[2 * k + p].wait()
        turned[...] = jnp.transpose(dst[...], (1, 0, 2))
        near[1 - k] = turned[near_at]
        far[1 - k] = turned[far_at]


def x_factor_kernel(pos, visc, vel, force_hbm, c, n, gf, gl, coef, rhs, cf, cb, force, sem):
    rows, depth, width = visc.shape
    copy = pltpu.make_async_copy(force_hbm, force, sem)
    copy.start()
    lo_wall = jnp.where(pos[0] == 0, HALF_X, 0.0)
    hi_wall = jnp.where(pos[0] == pos[1] - 1, HALF_X, 0.0)
    lane = iota((depth, width), 1)
    sub = iota((depth, width), 0)

    def explicit(i):
        v = vel[i]
        nu = visc[i]
        vn = jnp.where(lane == width - 1, 0.0, shift(v, -1, 1))
        nn = jnp.where(lane == width - 1, 0.0, shift(nu, -1, 1))
        fy = (2.0 * HALF_Y) * (nu + nn) * (vn - v)
        fl = jnp.where(lane == 0, (2.0 * HALF_Y) * nu * v, shift(fy, 1, 1))
        fz = (2.0 * HALF_Z) * (nu + shift(nu, -1, 0)) * (shift(v, -1, 0) - v)
        fz = jnp.where(sub == depth - 1, 0.0, fz)
        rhs[i] = 2.0 * v + (fy - fl) + (fz - shift(fz, 1, 0))

    def add_force(i):
        if i == 0:
            copy.wait()
        rhs[i] = rhs[i] + force[i]

    ends = factor(
        lambda i: visc[i], rows, HALF_X, lo_wall * visc[0], hi_wall * visc[rows - 1],
        c, n, gf, gl, cf, cb, explicit, add_force,
    )
    for k in range(3):
        coef[k] = ends[k]
    coef[3] = visc[0]
    coef[4] = visc[rows - 1]


def z_factor_kernel(pos, visc_z, c, n, gf, gl, planes, cf, cb):
    depth = visc_z.shape[0]
    lo_wall = jnp.where(pos[2] == 0, HALF_Z, 0.0)
    hi_wall = jnp.where(pos[2] == pos[3] - 1, HALF_Z, 0.0)
    ends = factor(
        lambda i: visc_z[i], depth, HALF_Z, lo_wall * visc_z[0], hi_wall * visc_z[depth - 1],
        c, n, gf, gl, cf, cb,
    )
    for k in range(3):
        planes[k] = ends[k]


def to_lines(block):
    lines, width = block.shape
    turned = block.T.reshape(Y_CHUNKS, width // Y_CHUNKS, lines)
    return jnp.transpose(turned, (1, 0, 2))


def from_lines(block):
    length, chunks, lines = block.shape
    return jnp.transpose(block, (1, 0, 2)).reshape(length * chunks, lines).T


def y_factor_kernel(pos, visc, c, n, gf, gl, al, ga, inv, nu, cf, cb):
    rows, depth, width = visc.shape
    length, chunks, lines = c.shape
    group = 128 // depth
    for g in range(rows // group):
        block = visc[g * group:(g + 1) * group].reshape(128, width)
        nu[:, :, g * 128:(g + 1) * 128] = to_lines(block)
    sub = iota((chunks, lines), 0)
    lo = jnp.where(sub == 0, HALF_Y * nu[0], 0.0)
    hi = jnp.where(sub == chunks - 1, HALF_Y * nu[length - 1], 0.0)
    first, across, last = factor(
        lambda i: nu[i], length, HALF_Y, lo, hi, c, n, gf, gl, cf, cb
    )
    inner = sub < chunks - 1
    e = HALF_Y * (nu[length - 1] + shift(nu[0], -1, 0))
    b = jnp.where(inner, 1.0 / e + last + shift(first, -1, 0), 1.0)
    o = jnp.where(sub < chunks - 2, shift(across, -1, 0), 0.0)
    s, k = 1, 0
    while s < chunks:
        r = 1.0 / b
        a = shift(o * r, s, 0)
        g = o * shift(r, -s, 0)
        al[k] = a
        ga[k] = g
        b = b - g * o - a * shift(o, s, 0)
        o = g * shift(o, -s, 0)
        s *= 2
        k += 1
    inv[...] = 1.0 / b


def x_solve_kernel(pos, visc, vel, rhs0, c, n, coef, near, far, pair, cross, w, payload, edge_lo, edge_hi):
    rows, depth, width = visc.shape
    sub = iota((depth, width), 0)
    upper = lax.rem(pos[2], 2)
    two = 2.0 * HALF_Z
    by_pair = two * (near[1] + pair[1]) * (pair[0] - near[0])
    by_cross = two * (far[1] + cross[1]) * (cross[0] - far[0])
    edge_lo[...] = jnp.where(upper == 0, by_cross, by_pair)
    edge_hi[...] = jnp.where(upper == 0, by_pair, by_cross)

    def rhs(i):
        at = pl.ds(i, 1)
        lo = jnp.where(sub == 0, edge_lo[at], 0.0)
        return rhs0[i] + jnp.where(sub == depth - 1, edge_hi[at], lo)

    d, u = block_solve(rhs, rows, c, n, w)
    payload[0] = d
    payload[1] = u
    for k in range(5):
        payload[2 + k] = coef[k]


def make_middle_kernel(parts_n):
    def kernel(pos, *refs):
        parts = refs[:parts_n]
        (w, gf, gl, vel, cy, ny, gfy, gly, aly, gay, invy, cz, nz,
         dz, ends, slots, flux, src, sol, turned) = refs[parts_n:]
        rows, depth, width = w.shape
        me = pos[0]
        for k in range(parts_n):
            slots[jnp.bitwise_xor(me, k)] = parts[k][...]
        zero = jnp.zeros((depth, width), F32)
        flux[0] = zero
        flux[parts_n] = zero
        lower, source = [], []
        for f in range(parts_n - 1):
            e = HALF_X * (slots[f, 6] + slots[f + 1, 5])
            pivot = 1.0 / e + slots[f, 4] + slots[f + 1, 2]
            right = slots[f + 1, 0] - slots[f, 1]
            if f:
                pivot = pivot - slots[f, 3] * lower[-1]
                right = right + lower[-1] * source[-1]
            r = 1.0 / pivot
            lower.append(slots[f + 1, 3] * r)
            source.append(right)
            flux[f + 1] = right * r
        q = flux[parts_n - 1]
        for f in reversed(range(parts_n - 2)):
            q = flux[f + 1] + lower[f] * q
            flux[f + 1] = q
        q_left = flux[me]
        q_right = flux[me + 1]

        group = 128 // depth
        for g in range(rows // group):
            at = pl.ds(g * group, group)
            d = w[at] + q_right * gl[at] - q_left * gf[at] - 2.0 * vel[at]
            src[:, :, g * 128:(g + 1) * 128] = to_lines(d.reshape(128, width))

        length, chunks, lines = src.shape
        sub = iota((chunks, lines), 0)
        d, u = block_solve(lambda i: src[i], length, cy, ny, sol)
        q = jnp.where(sub < chunks - 1, shift(d, -1, 0) - u, 0.0)
        for k in range(aly.shape[0]):
            q = q + aly[k] * shift(q, 1 << k, 0) + gay[k] * shift(q, -(1 << k), 0)
        q = q * invy[...]
        ql = shift(q, 1, 0)
        for i in range(length):
            sol[i] = sol[i] + q * gly[i] - ql * gfy[i]
        for g in range(rows // group):
            block = from_lines(sol[:, :, g * 128:(g + 1) * 128])
            block = block.reshape(group, depth, width)
            turned[:, g * group:(g + 1) * group, :] = jnp.transpose(block, (1, 0, 2))
        d, u = block_solve(lambda i: turned[i], depth, cz, nz, dz)
        ends[0] = d
        ends[1] = u

    return kernel


def final_kernel(pos, dz, gf, gl, q_left, q_right, out, buf, sems):
    depth, rows, width = dz.shape
    parts = buf.shape[0]
    group = rows // parts
    copies = []
    for p in range(parts):
        at = slice(p * group, (p + 1) * group)
        d = dz[:, at] + q_right[at] * gl[:, at] - q_left[at] * gf[:, at]
        buf[p] = jnp.transpose(d, (1, 0, 2))
        copy = pltpu.make_async_copy(buf.at[p], out.at[pl.ds(p * group, group)], sems.at[p])
        copy.start()
        copies.append(copy)
    for copy in copies:
        copy.wait()


def ordered(parts, me):
    bit = 1
    parts = list(parts)
    while bit < len(parts):
        odd = (me & bit) != 0
        parts = [jnp.where(odd, parts[i ^ bit], parts[i]) for i in range(len(parts))]
        bit *= 2
    return parts


def local(velocity, viscosity, force):
    rows, depth, width = velocity.shape
    nx, nz = lax.axis_size("gx"), lax.axis_size("gz")
    chips = nz // 2
    ix, iz = lax.axis_index("gx"), lax.axis_index("gz")
    upper = iz % 2
    chip = iz // 2
    pos = jnp.stack([ix, jnp.int32(nx), iz, jnp.int32(nz)]).astype(jnp.int32)
    volume = (rows, depth, width)
    zmajor = (depth, rows, width)
    lines = (width // Y_CHUNKS, Y_CHUNKS, rows * depth)
    size = rows * depth * width
    plane = (depth, width)
    slab = (rows, width)
    y_steps = (Y_CHUNKS - 1).bit_length()

    pair_route = [(i, i ^ 1) for i in range(nz)]
    cross_route = [(i, i + 1 if i % 2 else i - 1) for i in range(1, nz - 1)]

    def to_chip(k):
        return [(i, i ^ (2 * k)) for i in range(nz)]

    visc, vel, visc_z, near, far = call(
        load_kernel, [volume, volume, zmajor, (2,) + slab, (2,) + slab], [HBM, HBM],
        [pltpu.VMEM(zmajor, F32), pltpu.SemaphoreType.DMA((2, 2))], size, 6 * size,
    )(pos, viscosity, velocity)
    pair = lax.ppermute(near, "gz", pair_route)
    cross = lax.ppermute(far, "gz", cross_route)

    c_z, n_z, gf_z, gl_z, planes = call(
        z_factor_kernel, [zmajor] * 4 + [(3,) + slab], [VMEM],
        [pltpu.VMEM(zmajor, F32)] * 2, 20 * size, 5 * size,
    )(pos, visc_z)
    c_x, n_x, gf_x, gl_x, coef, rhs0 = call(
        x_factor_kernel, [volume] * 4 + [(5,) + plane, volume], [VMEM, VMEM, HBM],
        [pltpu.VMEM(volume, F32)] * 3 + [pltpu.SemaphoreType.DMA(())], 60 * size, 9 * size,
    )(pos, visc, vel, force)
    c_y, n_y, gf_y, gl_y, al_y, ga_y, inv_y = call(
        y_factor_kernel, [lines] * 4 + [(y_steps,) + lines[1:]] * 2 + [lines[1:]], [VMEM],
        [pltpu.VMEM(lines, F32)] * 3, 30 * size, 6 * size,
    )(pos, visc)

    mate_c = lax.ppermute(planes, "gz", pair_route)

    w, payload = call(
        x_solve_kernel, [volume, (7,) + plane], [VMEM] * 10,
        [pltpu.VMEM(slab, F32)] * 2, 20 * size, 6 * size,
    )(pos, visc, vel, rhs0, c_x, n_x, coef, near, far, pair, cross)
    mid_reach = 1.0 / (HALF_Z * (near[1] + pair[1]))
    end_reach = 1.0 / (HALF_Z * (far[1] + cross[1]))
    low_c = jnp.where(upper == 0, planes, mate_c)
    high_c = jnp.where(upper == 0, mate_c, planes)
    weight = 1.0 / (mid_reach + low_c[2] + high_c[0])
    low_fl, high_fl = low_c[1], high_c[1]
    chip_c = jnp.stack([
        low_c[0] - weight * low_fl * low_fl + jnp.where(upper == 0, end_reach, 0.0),
        weight * low_fl * high_fl,
        high_c[2] - weight * high_fl * high_fl + jnp.where(upper == 0, 0.0, end_reach),
    ])
    payload, chip_c = lax.optimization_barrier((payload, chip_c))
    parts = [payload] + [
        lax.ppermute(payload, "gx", [(i, i ^ k) for i in range(nx)]) for k in range(1, nx)
    ]
    all_c = ordered(
        [chip_c] + [lax.ppermute(chip_c, "gz", to_chip(k)) for k in range(1, chips)], chip
    )
    lower, inverse = [], []
    for f in range(chips - 1):
        pivot = all_c[f][2] + all_c[f + 1][0]
        if f:
            pivot = pivot - all_c[f][1] * lower[-1]
        inverse.append(1.0 / pivot)
        lower.append(all_c[f + 1][1] * inverse[-1])

    dz, ends = call(
        make_middle_kernel(nx), [zmajor, (2,) + slab], [VMEM] * (nx + 13),
        [pltpu.VMEM((nx, 7) + plane, F32), pltpu.VMEM((nx + 1,) + plane, F32),
         pltpu.VMEM(lines, F32), pltpu.VMEM(lines, F32), pltpu.VMEM(zmajor, F32)],
        60 * size, 14 * size,
    )(pos, *parts, w, gf_x, gl_x, vel, c_y, n_y, gf_y, gl_y, al_y, ga_y, inv_y, c_z, n_z)

    mate = lax.ppermute(ends, "gz", pair_route)
    low = jnp.where(upper == 0, ends, mate)
    high = jnp.where(upper == 0, mate, ends)
    jump = high[0] - low[1]
    q_mid = weight * jump
    chip_ends = jnp.stack([low[0] + low_fl * q_mid, high[1] - high_fl * q_mid])
    by_chip = ordered(
        [chip_ends] + [lax.ppermute(chip_ends, "gz", to_chip(k)) for k in range(1, chips)], chip
    )
    source, fluxes = [], []
    for f in range(chips - 1):
        right = by_chip[f + 1][0] - by_chip[f][1]
        if f:
            right = right + lower[f - 1] * source[-1]
        source.append(right)
        fluxes.append(right * inverse[f])
    for f in reversed(range(chips - 2)):
        fluxes[f] = fluxes[f] + lower[f] * fluxes[f + 1]
    chip_left = chip_right = jnp.zeros(slab, F32)
    for f in range(chips - 1):
        chip_right = jnp.where(chip == f, fluxes[f], chip_right)
        chip_left = jnp.where(chip == f + 1, fluxes[f], chip_left)
    q_mid = weight * (jump + chip_right * high_fl + chip_left * low_fl)
    q_left = jnp.where(upper == 0, chip_left, q_mid)
    q_right = jnp.where(upper == 0, q_mid, chip_right)
    return call(
        final_kernel, [volume], [VMEM] * 5,
        [pltpu.VMEM((4, rows // 4, depth, width), F32), pltpu.SemaphoreType.DMA((4,))],
        4 * size, 4 * size, [HBM],
    )(pos, dz, gf_z, gl_z, q_left, q_right)[0]


def solution(mesh):
    return jax.shard_map(
        local,
        mesh=mesh,
        in_specs=(P("gx", "gz", None), P("gx", "gz", None), P("gx", "gz", None)),
        out_specs=P("gx", "gz", None),
        check_vma=False,
    )
```

time: 81.5 us -> 52.2 us (0.64)
  Pallas kernels: 37.1 us -> 11.8 us
  blocking collectives: 14.1 us -> 0 us
  waiting for transfers between devices: 7.53 us -> 16.5 us
  starting transfers between devices: 12.4 us -> 16.9 us
  local copies, waits for them, and re-layouts: 7.48 us -> 3.71 us
    pallas_call x6 -> x7, Pallas kernels: 37.1 us -> 11.8 us  [the longest x1 4.1 us: local(): call(x_factor_kernel, [volume] * 4 + [(5,) + plane, volume], [VMEM, VMEM,...]
    all_gather x1 -> x0, blocking collectives: 14.1 us -> none  [local(): all_c = lax.all_gather(chip_c, 'gz', axis_index_groups=groups)]
    ppermute x6 -> x9, waiting for transfers between devices: 0.62 us -> 12 us  [the longest x3 8 us: local(): lax.ppermute(chip_c, 'gz', to_chip(k))]
    ppermute x6 -> x9, starting transfers between devices: 6.1 us -> 12.4 us  [the longest x1 3.91 us: local(): pair = lax.ppermute(near, 'gz', pair_route)]
    unnamed x14 -> x18, local copies, waits for them, and re-layouts: 6.38 us -> 3.71 us
    another operation x2 -> x1, other arithmetic: 1.79 us -> 0.01 us  [local(): jnp.stack([low_c[0] - weight * low_fl * low_fl + jnp.where(upper == 0, en...]
    ppermute x3, waiting for transfers between devices: 6.05 us -> 4.56 us  [local(): lax.ppermute(payload, 'gx', [(i, i ^ k) for i in range(nx)])]
    slice x1 -> x0, local copies, waits for them, and re-layouts: 1.1 us -> none  [local(): reach = 1.0 / (HALF_Z * (viscosity[:, depth - 1] + right_face))]
  transfers between devices with their start and end apart: 10 -> 13, of which waited for: 4 -> 6; matrix products, arithmetic and copies ran while one was open for 2% -> 0% of each run, Pallas kernels for 26% -> 12%
where the time goes in v1:
time: 52.2 us; the launch traced here: 51.8 us
  starting transfers between devices  16.9 us (32%)
  waiting for transfers between devices  16.5 us (32%)
  Pallas kernels  11.8 us (23%)
  local copies, waits for them, and re-layouts  3.71 us (7%)
  other arithmetic  2.62 us (5%)
    ppermute x3, waiting for transfers between devices, local(): lax.ppermute(chip_c, 'gz', to_chip(k))  8 us
    ppermute x3, waiting for transfers between devices, local(): lax.ppermute(payload, 'gx', [(i, i ^ k) for i in range(nx)])  4.56 us
    ppermute x3, starting transfers between devices, local(): lax.ppermute(payload, 'gx', [(i, i ^ k) for i in range(nx)])  4.45 us
    pallas_call x1, Pallas kernels, local(): call(x_factor_kernel, [volume] * 4 + [(5,) + plane, volume], [VMEM, VMEM,...  4.1 us
    ppermute x3, waiting for transfers between devices, local(): lax.ppermute(chip_ends, 'gz', to_chip(k))  3.96 us
    ppermute x1, starting transfers between devices, local(): pair = lax.ppermute(near, 'gz', pair_route)  3.91 us
    ppermute x3, starting transfers between devices, local(): lax.ppermute(chip_ends, 'gz', to_chip(k))  3.78 us
    unnamed x18, local copies, waits for them, and re-layouts  3.71 us
  transfers between devices with their start and end apart: 13, of which 6 were waited for; matrix products, arithmetic and copies ran while one was open for 0% of the time, Pallas kernels for 12%

profile of v1, /device:TPU:0, one launch (start us, length us, event | category | flops | bytes accessed | tf_op | source)
XLA Modules:
  0.0 51.8 jit_solution(16524152212333290753)
XLA Ops:
  0.0 0.1 pad_add_fusion.pos
  0.1 0.0 copy-start.1
  0.1 1.0 %copy-done.1 = f32[64,8,256]{2,1,0:T(8,128)S(1)} copy-done((f32[64,8,256]{2,1,0:T(8,128)S(1)}, f32[64,8,256]{2,1,0:T(8,128)}, u32[]{:S(2)}) %copy-start.1) | copy-done | bytes 524312
  1.1 0.0 copy-start.2
  1.1 1.0 %copy-done.2 = f32[64,8,256]{2,1,0:T(8,128)S(1)} copy-done((f32[64,8,256]{2,1,0:T(8,128)S(1)}, f32[64,8,256]{2,1,0:T(8,128)}, u32[]{:S(2)}) %copy-start.2) | copy-done | bytes 524312
  2.2 1.0 %shard_map.37 = (f32[64,8,256]{2,1,0:T(8,128)S(1)}, f32[64,8,256]{2,1,0:T(8,128)S(1)}, f32[8,64,256]{2,1,0:T(8,128)S(1)}, f32[2,64,256]{2,1,0:T(8,128)S(1)}, f32[2,64,256]{2,1,0:T(8,128)S(1)}) custom-call(s32[4]{0:T(128)S(1)} %pad_add_fusion.pos, f32[64,8,256]{2,1,0:T(8,128)S(1)} %copy-done.1, f32[64,8,256]{2,1,0:T(8,128)S(1)} %copy-done.2), custom_call_target="tpu_custom_call" | custom-call | flops 131072 | bytes 3145728 | tf_op jit(solution)/shard_map/pallas_call | solution.py:353
  3.2 1.6 %shard_map.40 = (f32[8,64,256]{2,1,0:T(8,128)S(1)}, f32[8,64,256]{2,1,0:T(8,128)S(1)}, f32[8,64,256]{2,1,0:T(8,128)S(1)}, f32[8,64,256]{2,1,0:T(8,128)S(1)}, f32[3,64,256]{2,1,0:T(8,128)}) custom-call(s32[4]{0:T(128)S(1)} %pad_add_fusion.pos, f32[8,64,256]{2,1,0:T(8,128)S(1)} %get-tuple-element.43.visc_z), custom_call_target="tpu_custom_call" | custom-call | flops 2621440 | bytes 2621440 | tf_op jit(solution)/shard_map/pallas_call | solution.py:360
  4.7 0.5 collective-permute-start.2
  5.2 0.7 %collective-permute-start.1 = (f32[2,64,256]{2,1,0:T(8,128)S(1)}, f32[2,64,256]{2,1,0:T(8,128)S(1)}, u32[]{:S(2)}, u32[]{:S(2)}) collective-permute-start(f32[2,64,256]{2,1,0:T(8,128)S(1)} %get-tuple-element.41.far), channel_id=1, source_target_pairs={{1,2},{2,1},{3,4},{4,3},{5,6},{6,5},{9,10},{10,9},{11,12},{12,11},... | collective-permute-start | bytes 393224 | tf_op jit(solution)/shard_map/ppermute | solution.py:358
  5.9 3.9 %collective-permute-start = (f32[2,64,256]{2,1,0:T(8,128)S(1)}, f32[2,64,256]{2,1,0:T(8,128)}, u32[]{:S(2)}, u32[]{:S(2)}) collective-permute-start(f32[2,64,256]{2,1,0:T(8,128)S(1)} %get-tuple-element.40.near), channel_id=1, source_target_pairs={{0,1},{1,0},{2,3},{3,2},{4,5},{5,4},{6,7},{7,6},{8,9},{9,8},{10,11... | collective-permute-start | bytes 393224 | tf_op jit(solution)/shard_map/ppermute | solution.py:357
  9.8 0.0 copy-start
  9.8 1.0 %copy-done = f32[64,8,256]{2,1,0:T(8,128)S(1)} copy-done((f32[64,8,256]{2,1,0:T(8,128)S(1)}, f32[64,8,256]{2,1,0:T(8,128)}, u32[]{:S(2)}) %copy-start) | copy-done | bytes 524312
  10.8 4.1 %shard_map.38 = (f32[64,8,256]{2,1,0:T(8,128)S(1)}, f32[64,8,256]{2,1,0:T(8,128)S(1)}, f32[64,8,256]{2,1,0:T(8,128)S(1)}, f32[64,8,256]{2,1,0:T(8,128)S(1)}, f32...) custom-call(s32[4]{0:T(128)S(1)} %pad_add_fusion.pos, f32[64,8,256]{2,1,0:T(8,128)S(1)} %get-tuple-element.34.visc, ...), custom_call_target="tpu_custom_call" | custom-call | flops 7864320 | bytes 4718592 | tf_op jit(solution)/shard_map/pallas_call | solution.py:364
  14.9 0.0 collective-permute-done.1.cross
  14.9 0.0 collective-permute-done.pair
  14.9 1.2 %shard_map.39 = (f32[64,8,256]{2,1,0:T(8,128)S(1)}, f32[7,8,256]{2,1,0:T(8,128)S(1)}) custom-call(s32[4]{0:T(128)S(1)} %pad_add_fusion.pos, f32[64,8,256]{2,1,0:T(8,128)S(1)} %get-tuple-element.34.visc, f32[64,8,256]{2,1,0:T(8,128)S(1)} %get-tuple-element.35.vel.refs_7_, f32[64,8,256]{2,1,0:T(8,128)S(1)} %get-tuple-element.36.rhs0, ...), custom_call_target="tpu_custom_call" | custom-call | flops 2621440 | bytes 3145728 | tf_op jit(solution)/shard_map/pallas_call | solution.py:375
  16.1 0.0 collective-permute-done.2
  16.2 1.1 %broadcast_select_fusion.6 = (f32[3,64,256]{2,1,0:T(8,128)S(1)}, f32[3,64,256]{2,1,0:T(8,128)S(1)}) fusion(f32[3,64,256]{2,1,0:T(8,128)} %collective-permute-done.2, f32[3,64,256]{2,1,0:T(8,128)} %get-tuple-element.44, pred[]{:T(512)S(6)} %eq.12), kind=kLoop, calls=%fused_computation.9 | loop fusion | flops 98304 | bytes 786433 | tf_op jit(solution)/shard_map/jit(_where)/select_n | solution.py:382
  17.2 0.0 copy-start.3
  17.2 0.0 copy-start.5
  17.2 1.0 %fusion.23 = (f32[1,64,256]{2,1,0:T(8,128)S(1)}, f32[1,64,256]{2,1,0:T(8,128)S(1)}) fusion(f32[3,64,256]{2,1,0:T(8,128)S(1)} %get-tuple-element.92, pred[]{:T(512)S(6)} %eq.12, f32[2,64,256]{2,1,0:T(8,128)S(1)} %collective-permute-done.1.cross, f32[2,64,256]{2,1,0:T(8,128)S(1)} %get-tuple-element.41.far, f32[3,64,256]{2,1,0:T(8,128)S(1)} %get-tuple-element.91, ...), kind=kLoop, calls=%fused_computation.52 | loop fusion | flops 229376 | bytes 655361 | tf_op jit(solution)/shard_map/add | solution.py:386
  18.2 0.0 copy-start.7
  18.2 0.0 copy-done.3
  18.2 0.0 copy-done.5
  18.3 0.6 %copy-done.7 = f32[1,64,256]{2,1,0:T(8,128)} copy-done((f32[1,64,256]{2,1,0:T(8,128)}, f32[1,64,256]{2,1,0:T(8,128)S(1)}, u32[]{:S(2)}) %copy-start.7) | copy-done | bytes 65560
  18.9 1.6 %collective-permute-start.3 = (f32[7,8,256]{2,1,0:T(8,128)S(1)}, f32[7,8,256]{2,1,0:T(8,128)S(1)}, u32[]{:S(2)}, u32[]{:S(2)}) collective-permute-start(f32[7,8,256]{2,1,0:T(8,128)S(1)} %get-tuple-element.45.refs_0_), channel_id=1, source_target_pairs={{0,8},{8,0},{16,24},{24,16},{1,9},{9,1},{17,25},{25,17},{2,10},{10... | collective-permute-start | bytes 172040 | tf_op jit(solution)/shard_map/ppermute | solution.py:392
  20.5 2.6 %collective-permute-start.4 = (f32[7,8,256]{2,1,0:T(8,128)S(1)}, f32[7,8,256]{2,1,0:T(8,128)S(1)}, u32[]{:S(2)}, u32[]{:S(2)}) collective-permute-start(f32[7,8,256]{2,1,0:T(8,128)S(1)} %get-tuple-element.45.refs_0_), channel_id=1, source_target_pairs={{0,16},{8,24},{16,0},{24,8},{1,17},{9,25},{17,1},{25,9},{2,18},{10... | collective-permute-start | bytes 172040 | tf_op jit(solution)/shard_map/ppermute | solution.py:392
  23.1 0.2 collective-permute-start.5
  23.3 1.2 %shard_map.41 = (f32[32,8,512]{2,1,0:T(8,128)S(1)}, f32[32,8,512]{2,1,0:T(8,128)S(1)}, f32[32,8,512]{2,1,0:T(8,128)S(1)}, f32[32,8,512]{2,1,0:T(8,128)S(1)}, f32...) custom-call(s32[4]{0:T(128)S(1)} %pad_add_fusion.pos, f32[64,8,256]{2,1,0:T(8,128)S(1)} %get-tuple-element.34.visc), custom_call_target="tpu_custom_call" | custom-call | flops 3932160 | bytes 3145728 | tf_op jit(solution)/shard_map/pallas_call | solution.py:368
  24.5 0.0 collective-permute-done.3.refs_1_
  24.5 2.3 %collective-permute-done.4.refs_2_ = f32[7,8,256]{2,1,0:T(8,128)S(1)} collective-permute-done((f32[7,8,256]{2,1,0:T(8,128)S(1)}, f32[7,8,256]{2,1,0:T(8,128)S(1)}, u32[]{:S(2)}, u32[]{:S(2)}) %collective-permute-start.4) | collective-permute-done | bytes 57376 | tf_op jit(solution)/shard_map/ppermute | solution.py:392
  26.9 2.2 %collective-permute-done.5.refs_3_ = f32[7,8,256]{2,1,0:T(8,128)S(1)} collective-permute-done((f32[7,8,256]{2,1,0:T(8,128)S(1)}, f32[7,8,256]{2,1,0:T(8,128)S(1)}, u32[]{:S(2)}, u32[]{:S(2)}) %collective-permute-start.5) | collective-permute-done | bytes 57376 | tf_op jit(solution)/shard_map/ppermute | solution.py:392
  29.1 1.3 %shard_map.42 = (f32[8,64,256]{2,1,0:T(8,128)S(1)}, f32[2,64,256]{2,1,0:T(8,128)S(1)}) custom-call(s32[4]{0:T(128)S(1)} %pad_add_fusion.pos, f32[7,8,256]{2,1,0:T(8,128)S(1)} %get-tuple-element.45.refs_0_, f32[7,8,256]{2,1,0:T(8,128)S(1)} %collective-permute-done.3.refs_1_, f32[7,8,256]{2,1,0:T(8,128)S(1)} %collective-permute-done.4.refs_2_, ...), custom_call_target="tpu_custom_call" | custom-call | flops 7864320 | bytes 7340032 | tf_op jit(solution)/shard_map/pallas_call | solution.py:405
  30.4 0.1 collective-permute-start.6
  30.5 0.0 copy-start.4
  30.5 0.0 copy-start.6
  30.5 0.0 copy-start.8
  30.6 1.6 %collective-permute-start.10 = (f32[3,64,256]{2,1,0:T(8,128)S(1)}, f32[3,64,256]{2,1,0:T(8,128)S(1)}, u32[]{:S(2)}, u32[]{:S(2)}) collective-permute-start(f32[3,64,256]{2,1,0:T(8,128)S(1)} %pad_maximum_fusion), channel_id=1, source_target_pairs={{0,2},{1,3},{2,0},{3,1},{4,6},{5,7},{6,4},{7,5},{8,10},{9,11},{10,... | collective-permute-start | bytes 589832 | tf_op jit(solution)/shard_map/ppermute | solution.py:395
  32.1 1.5 %collective-permute-start.11 = (f32[3,64,256]{2,1,0:T(8,128)S(1)}, f32[3,64,256]{2,1,0:T(8,128)S(1)}, u32[]{:S(2)}, u32[]{:S(2)}) collective-permute-start(f32[3,64,256]{2,1,0:T(8,128)S(1)} %pad_maximum_fusion), channel_id=1, source_target_pairs={{0,6},{1,7},{2,4},{3,5},{4,2},{5,3},{6,0},{7,1},{8,14},{9,15},{10,... | collective-permute-start | bytes 589832 | tf_op jit(solution)/shard_map/ppermute | solution.py:395
  33.7 0.5 collective-permute-start.12
  34.1 0.0 collective-permute-done.6
  34.2 0.0 copy-done.4
  34.2 0.0 copy-done.6
  34.2 0.0 copy-done.8
  34.2 1.6 %collective-permute-start.7 = (f32[2,64,256]{2,1,0:T(8,128)S(1)}, f32[2,64,256]{2,1,0:T(8,128)S(1)}, u32[]{:S(2)}, u32[]{:S(2)}) collective-permute-start(f32[2,64,256]{2,1,0:T(8,128)S(1)} %pad_maximum_fusion.1), channel_id=1, source_target_pairs={{0,2},{1,3},{2,0},{3,1},{4,6},{5,7},{6,4},{7,5},{8,10},{9,11},{10,... | collective-permute-start | bytes 393224 | tf_op jit(solution)/shard_map/ppermute | solution.py:419
  35.8 0.6 %collective-permute-start.8 = (f32[2,64,256]{2,1,0:T(8,128)S(1)}, f32[2,64,256]{2,1,0:T(8,128)S(1)}, u32[]{:S(2)}, u32[]{:S(2)}) collective-permute-start(f32[2,64,256]{2,1,0:T(8,128)S(1)} %pad_maximum_fusion.1), channel_id=1, source_target_pairs={{0,4},{1,5},{2,6},{3,7},{4,0},{5,1},{6,2},{7,3},{8,12},{9,13},{10,... | collective-permute-start | bytes 393224 | tf_op jit(solution)/shard_map/ppermute | solution.py:419
  36.4 1.9 %collective-permute-done.10 = f32[3,64,256]{2,1,0:T(8,128)S(1)} collective-permute-done((f32[3,64,256]{2,1,0:T(8,128)S(1)}, f32[3,64,256]{2,1,0:T(8,128)S(1)}, u32[]{:S(2)}, u32[]{:S(2)}) %collective-permute-start.10) | collective-permute-done | bytes 196640 | tf_op jit(solution)/shard_map/ppermute | solution.py:395
  38.4 1.6 %collective-permute-start.9 = (f32[2,64,256]{2,1,0:T(8,128)S(1)}, f32[2,64,256]{2,1,0:T(8,128)S(1)}, u32[]{:S(2)}, u32[]{:S(2)}) collective-permute-start(f32[2,64,256]{2,1,0:T(8,128)S(1)} %pad_maximum_fusion.1), channel_id=1, source_target_pairs={{0,6},{1,7},{2,4},{3,5},{4,2},{5,3},{6,0},{7,1},{8,14},{9,15},{10,... | collective-permute-start | bytes 393224 | tf_op jit(solution)/shard_map/ppermute | solution.py:419
  39.9 3.7 %collective-permute-done.11 = f32[3,64,256]{2,1,0:T(8,128)S(1)} collective-permute-done((f32[3,64,256]{2,1,0:T(8,128)S(1)}, f32[3,64,256]{2,1,0:T(8,128)S(1)}, u32[]{:S(2)}, u32[]{:S(2)}) %collective-permute-start.11) | collective-permute-done | bytes 196640 | tf_op jit(solution)/shard_map/ppermute | solution.py:395
  43.6 2.4 %collective-permute-done.12 = f32[3,64,256]{2,1,0:T(8,128)S(1)} collective-permute-done((f32[3,64,256]{2,1,0:T(8,128)S(1)}, f32[3,64,256]{2,1,0:T(8,128)S(1)}, u32[]{:S(2)}, u32[]{:S(2)}) %collective-permute-start.12) | collective-permute-done | bytes 196640 | tf_op jit(solution)/shard_map/ppermute | solution.py:395
  46.0 0.1 broadcast_select_fusion.4
  46.1 0.0 collective-permute-done.7
  46.2 4.0 %collective-permute-done.8 = f32[2,64,256]{2,1,0:T(8,128)S(1)} collective-permute-done((f32[2,64,256]{2,1,0:T(8,128)S(1)}, f32[2,64,256]{2,1,0:T(8,128)S(1)}, u32[]{:S(2)}, u32[]{:S(2)}) %collective-permute-start.8) | collective-permute-done | bytes 131104 | tf_op jit(solution)/shard_map/ppermute | solution.py:419
  50.1 0.0 collective-permute-done.9
  50.1 0.1 broadcast_select_fusion.14
  50.2 0.1 select_select_fusion
  50.3 0.1 broadcast_select_fusion.16
  50.4 1.4 %shard_map.43 = f32[64,8,256]{2,1,0:T(8,128)} custom-call(s32[4]{0:T(128)S(1)} %pad_add_fusion.pos, f32[8,64,256]{2,1,0:T(8,128)S(1)} %get-tuple-element.58.dz, f32[8,64,256]{2,1,0:T(8,128)S(1)} %get-tuple-element.59.gf, f32[8,64,256]{2,1,0:T(8,128)S(1)} %get-tuple-element.60.gl, f32[64,256]{1,0:T(8,128)S(1)} %broadcast_select_fusion.17.q_left, ...), custom_call_target="tpu_custom_call" | custom-call | flops 524288 | bytes 2097152 | tf_op jit(solution)/shard_map/pallas_call | solution.py:437
  (6 shorter events, 0.1 us)
Async XLA Ops:
  0.1 1.0 %copy-start.1 = (f32[64,8,256]{2,1,0:T(8,128)S(1)}, f32[64,8,256]{2,1,0:T(8,128)}, u32[]{:S(2)}) copy-start(f32[64,8,256]{2,1,0:T(8,128)} %visc_hbm.1) | copy-start | bytes 1572868
  1.1 1.0 %copy-start.2 = (f32[64,8,256]{2,1,0:T(8,128)S(1)}, f32[64,8,256]{2,1,0:T(8,128)}, u32[]{:S(2)}) copy-start(f32[64,8,256]{2,1,0:T(8,128)} %vel_hbm.1) | copy-start | bytes 1572868
  4.7 11.4 %collective-permute-start.2 = (f32[3,64,256]{2,1,0:T(8,128)}, f32[3,64,256]{2,1,0:T(8,128)}, u32[]{:S(2)}, u32[]{:S(2)}) collective-permute-start(f32[3,64,256]{2,1,0:T(8,128)} %get-tuple-element.44), channel_id=1, source_target_pairs={{0,1},{1,0},{2,3},{3,2},{4,5},{5,4},{6,7},{7,6},{8,9},{9,8},{10,11... | collective-permute-start | bytes 589832 | tf_op jit(solution)/shard_map/ppermute | solution.py:373
  5.2 9.7 %collective-permute-start.1 = (f32[2,64,256]{2,1,0:T(8,128)S(1)}, f32[2,64,256]{2,1,0:T(8,128)S(1)}, u32[]{:S(2)}, u32[]{:S(2)}) collective-permute-start(f32[2,64,256]{2,1,0:T(8,128)S(1)} %get-tuple-element.41.far), channel_id=1, source_target_pairs={{1,2},{2,1},{3,4},{4,3},{5,6},{6,5},{9,10},{10,9},{11,12},{12,11},... | collective-permute-start | bytes 393224 | tf_op jit(solution)/shard_map/ppermute | solution.py:358
  5.9 9.1 %collective-permute-start = (f32[2,64,256]{2,1,0:T(8,128)S(1)}, f32[2,64,256]{2,1,0:T(8,128)}, u32[]{:S(2)}, u32[]{:S(2)}) collective-permute-start(f32[2,64,256]{2,1,0:T(8,128)S(1)} %get-tuple-element.40.near), channel_id=1, source_target_pairs={{0,1},{1,0},{2,3},{3,2},{4,5},{5,4},{6,7},{7,6},{8,9},{9,8},{10,11... | collective-permute-start | bytes 393224 | tf_op jit(solution)/shard_map/ppermute | solution.py:357
  9.8 1.0 %copy-start = (f32[64,8,256]{2,1,0:T(8,128)S(1)}, f32[64,8,256]{2,1,0:T(8,128)}, u32[]{:S(2)}) copy-start(f32[64,8,256]{2,1,0:T(8,128)} %force_hbm.1) | copy-start | bytes 1572868
  17.2 1.0 %copy-start.3 = (f32[3,64,256]{2,1,0:T(8,128)}, f32[3,64,256]{2,1,0:T(8,128)S(1)}, u32[]{:S(2)}) copy-start(f32[3,64,256]{2,1,0:T(8,128)S(1)} %get-tuple-element.92) | copy-start | bytes 589828
  17.2 1.0 %copy-start.5 = (f32[3,64,256]{2,1,0:T(8,128)}, f32[3,64,256]{2,1,0:T(8,128)S(1)}, u32[]{:S(2)}) copy-start(f32[3,64,256]{2,1,0:T(8,128)S(1)} %get-tuple-element.91) | copy-start | bytes 589828
  18.2 0.6 %copy-start.7 = (f32[1,64,256]{2,1,0:T(8,128)}, f32[1,64,256]{2,1,0:T(8,128)S(1)}, u32[]{:S(2)}) copy-start(f32[1,64,256]{2,1,0:T(8,128)S(1)} %get-tuple-element.84) | copy-start | bytes 196612
  18.9 5.6 %collective-permute-start.3 = (f32[7,8,256]{2,1,0:T(8,128)S(1)}, f32[7,8,256]{2,1,0:T(8,128)S(1)}, u32[]{:S(2)}, u32[]{:S(2)}) collective-permute-start(f32[7,8,256]{2,1,0:T(8,128)S(1)} %get-tuple-element.45.refs_0_), channel_id=1, source_target_pairs={{0,8},{8,0},{16,24},{24,16},{1,9},{9,1},{17,25},{25,17},{2,10},{10... | collective-permute-start | bytes 172040 | tf_op jit(solution)/shard_map/ppermute | solution.py:392
  20.5 6.3 %collective-permute-start.4 = (f32[7,8,256]{2,1,0:T(8,128)S(1)}, f32[7,8,256]{2,1,0:T(8,128)S(1)}, u32[]{:S(2)}, u32[]{:S(2)}) collective-permute-start(f32[7,8,256]{2,1,0:T(8,128)S(1)} %get-tuple-element.45.refs_0_), channel_id=1, source_target_pairs={{0,16},{8,24},{16,0},{24,8},{1,17},{9,25},{17,1},{25,9},{2,18},{10... | collective-permute-start | bytes 172040 | tf_op jit(solution)/shard_map/ppermute | solution.py:392
  23.1 6.0 %collective-permute-start.5 = (f32[7,8,256]{2,1,0:T(8,128)S(1)}, f32[7,8,256]{2,1,0:T(8,128)S(1)}, u32[]{:S(2)}, u32[]{:S(2)}) collective-permute-start(f32[7,8,256]{2,1,0:T(8,128)S(1)} %get-tuple-element.45.refs_0_), channel_id=1, source_target_pairs={{0,24},{8,16},{16,8},{24,0},{1,25},{9,17},{17,9},{25,1},{2,26},{10... | collective-permute-start | bytes 172040 | tf_op jit(solution)/shard_map/ppermute | solution.py:392
  30.4 3.7 %collective-permute-start.6 = (f32[2,64,256]{2,1,0:T(8,128)S(1)}, f32[2,64,256]{2,1,0:T(8,128)S(1)}, u32[]{:S(2)}, u32[]{:S(2)}) collective-permute-start(f32[2,64,256]{2,1,0:T(8,128)S(1)} %get-tuple-element.61), channel_id=1, source_target_pairs={{0,1},{1,0},{2,3},{3,2},{4,5},{5,4},{6,7},{7,6},{8,9},{9,8},{10,11... | collective-permute-start | bytes 393224 | tf_op jit(solution)/shard_map/ppermute | solution.py:412
  30.5 3.6 %copy-start.4 = (f32[3,64,256]{2,1,0:T(8,128)S(1)}, f32[3,64,256]{2,1,0:T(8,128)}, u32[]{:S(2)}) copy-start(f32[3,64,256]{2,1,0:T(8,128)} %copy-done.3) | copy-start | bytes 589828
  30.5 3.6 %copy-start.6 = (f32[3,64,256]{2,1,0:T(8,128)S(1)}, f32[3,64,256]{2,1,0:T(8,128)}, u32[]{:S(2)}) copy-start(f32[3,64,256]{2,1,0:T(8,128)} %copy-done.5) | copy-start | bytes 589828
  30.5 3.6 %copy-start.8 = (f32[1,64,256]{2,1,0:T(8,128)S(1)}, f32[1,64,256]{2,1,0:T(8,128)}, u32[]{:S(2)}) copy-start(f32[1,64,256]{2,1,0:T(8,128)} %copy-done.7) | copy-start | bytes 196612
  30.6 7.8 %collective-permute-start.10 = (f32[3,64,256]{2,1,0:T(8,128)S(1)}, f32[3,64,256]{2,1,0:T(8,128)S(1)}, u32[]{:S(2)}, u32[]{:S(2)}) collective-permute-start(f32[3,64,256]{2,1,0:T(8,128)S(1)} %pad_maximum_fusion), channel_id=1, source_target_pairs={{0,2},{1,3},{2,0},{3,1},{4,6},{5,7},{6,4},{7,5},{8,10},{9,11},{10,... | collective-permute-start | bytes 589832 | tf_op jit(solution)/shard_map/ppermute | solution.py:395
  32.1 11.5 %collective-permute-start.11 = (f32[3,64,256]{2,1,0:T(8,128)S(1)}, f32[3,64,256]{2,1,0:T(8,128)S(1)}, u32[]{:S(2)}, u32[]{:S(2)}) collective-permute-start(f32[3,64,256]{2,1,0:T(8,128)S(1)} %pad_maximum_fusion), channel_id=1, source_target_pairs={{0,6},{1,7},{2,4},{3,5},{4,2},{5,3},{6,0},{7,1},{8,14},{9,15},{10,... | collective-permute-start | bytes 589832 | tf_op jit(solution)/shard_map/ppermute | solution.py:395
  33.7 12.4 %collective-permute-start.12 = (f32[3,64,256]{2,1,0:T(8,128)S(1)}, f32[3,64,256]{2,1,0:T(8,128)S(1)}, u32[]{:S(2)}, u32[]{:S(2)}) collective-permute-start(f32[3,64,256]{2,1,0:T(8,128)S(1)} %pad_maximum_fusion), channel_id=1, source_target_pairs={{0,4},{1,5},{2,6},{3,7},{4,0},{5,1},{6,2},{7,3},{8,12},{9,13},{10,... | collective-permute-start | bytes 589832 | tf_op jit(solution)/shard_map/ppermute | solution.py:395
  34.2 11.9 %collective-permute-start.7 = (f32[2,64,256]{2,1,0:T(8,128)S(1)}, f32[2,64,256]{2,1,0:T(8,128)S(1)}, u32[]{:S(2)}, u32[]{:S(2)}) collective-permute-start(f32[2,64,256]{2,1,0:T(8,128)S(1)} %pad_maximum_fusion.1), channel_id=1, source_target_pairs={{0,2},{1,3},{2,0},{3,1},{4,6},{5,7},{6,4},{7,5},{8,10},{9,11},{10,... | collective-permute-start | bytes 393224 | tf_op jit(solution)/shard_map/ppermute | solution.py:419
  35.8 14.3 %collective-permute-start.8 = (f32[2,64,256]{2,1,0:T(8,128)S(1)}, f32[2,64,256]{2,1,0:T(8,128)S(1)}, u32[]{:S(2)}, u32[]{:S(2)}) collective-permute-start(f32[2,64,256]{2,1,0:T(8,128)S(1)} %pad_maximum_fusion.1), channel_id=1, source_target_pairs={{0,4},{1,5},{2,6},{3,7},{4,0},{5,1},{6,2},{7,3},{8,12},{9,13},{10,... | collective-permute-start | bytes 393224 | tf_op jit(solution)/shard_map/ppermute | solution.py:419
  38.4 11.8 %collective-permute-start.9 = (f32[2,64,256]{2,1,0:T(8,128)S(1)}, f32[2,64,256]{2,1,0:T(8,128)S(1)}, u32[]{:S(2)}, u32[]{:S(2)}) collective-permute-start(f32[2,64,256]{2,1,0:T(8,128)S(1)} %pad_maximum_fusion.1), channel_id=1, source_target_pairs={{0,6},{1,7},{2,4},{3,5},{4,2},{5,3},{6,0},{7,1},{8,14},{9,15},{10,... | collective-permute-start | bytes 393224 | tf_op jit(solution)/shard_map/ppermute | solution.py:419

commit v2 on v1

--- a/solution.py
+++ b/solution.py
@@ -12,7 +12,6 @@
 
 F32 = jnp.float32
 VMEM = pl.BlockSpec(memory_space=pltpu.VMEM)
-SMEM = pl.BlockSpec(memory_space=pltpu.SMEM)
 HBM = pl.BlockSpec(memory_space=pltpu.HBM)
 
 
@@ -20,7 +19,7 @@
     return pl.pallas_call(
         kernel,
         out_shape=tuple(jax.ShapeDtypeStruct(s, F32) for s in outs),
-        in_specs=[SMEM] + ins,
+        in_specs=ins,
         out_specs=tuple(out_specs or [VMEM] * len(outs)),
         scratch_shapes=list(scratch),
         compiler_params=pltpu.CompilerParams(vmem_limit_bytes=8 << 20),
@@ -112,33 +111,23 @@
     return d, u
 
 
-def load_kernel(pos, visc_hbm, vel_hbm, visc, vel, visc_z, near, far, vel_z, sems):
-    rows, depth, width = visc.shape
-    copies = []
-    half = rows // 2
-    for k, (src, dst) in enumerate(((visc_hbm, visc), (vel_hbm, vel))):
-        for p in range(2):
-            at = pl.ds(p * half, half)
-            copies.append(pltpu.make_async_copy(src.at[at], dst.at[at], sems.at[k, p]))
-    for c in copies:
-        c.start()
-    upper = lax.rem(pos[2], 2)
+def turn_kernel(visc, vel, visc_z, near, far, vel_z):
+    depth = visc.shape[1]
+    upper = lax.rem(lax.axis_index("gz"), 2)
     near_at = (1 - upper) * (depth - 1)
     far_at = upper * (depth - 1)
-    for k, (dst, turned) in enumerate(((visc, visc_z), (vel, vel_z))):
-        for p in range(2):
-            copies[2 * k + p].wait()
-        turned[...] = jnp.transpose(dst[...], (1, 0, 2))
-        near[1 - k] = turned[near_at]
-        far[1 - k] = turned[far_at]
-
-
-def x_factor_kernel(pos, visc, vel, force_hbm, c, n, gf, gl, coef, rhs, cf, cb, force, sem):
+    for k, (src, turned) in enumerate(((vel, vel_z), (visc, visc_z))):
+        turned[...] = jnp.transpose(src[...], (1, 0, 2))
+        near[k] = turned[near_at]
+        far[k] = turned[far_at]
+
+
+def x_factor_kernel(visc, vel, force_hbm, c, n, gf, gl, coef, rhs, cf, cb, force, sem):
     rows, depth, width = visc.shape
     copy = pltpu.make_async_copy(force_hbm, force, sem)
     copy.start()
-    lo_wall = jnp.where(pos[0] == 0, HALF_X, 0.0)
-    hi_wall = jnp.where(pos[0] == pos[1] - 1, HALF_X, 0.0)
+    lo_wall = jnp.where(lax.axis_index("gx") == 0, HALF_X, 0.0)
+    hi_wall = jnp.where(lax.axis_index("gx") == lax.axis_size("gx") - 1, HALF_X, 0.0)
     lane = iota((depth, width), 1)
     sub = iota((depth, width), 0)
 
@@ -168,10 +157,10 @@
     coef[4] = visc[rows - 1]
 
 
-def z_factor_kernel(pos, visc_z, c, n, gf, gl, planes, cf, cb):
+def z_factor_kernel(visc_z, c, n, gf, gl, planes, cf, cb):
     depth = visc_z.shape[0]
-    lo_wall = jnp.where(pos[2] == 0, HALF_Z, 0.0)
-    hi_wall = jnp.where(pos[2] == pos[3] - 1, HALF_Z, 0.0)
+    lo_wall = jnp.where(lax.axis_index("gz") == 0, HALF_Z, 0.0)
+    hi_wall = jnp.where(lax.axis_index("gz") == lax.axis_size("gz") - 1, HALF_Z, 0.0)
     ends = factor(
         lambda i: visc_z[i], depth, HALF_Z, lo_wall * visc_z[0], hi_wall * visc_z[depth - 1],
         c, n, gf, gl, cf, cb,
@@ -191,7 +180,7 @@
     return jnp.transpose(block, (1, 0, 2)).reshape(length * chunks, lines).T
 
 
-def y_factor_kernel(pos, visc, c, n, gf, gl, al, ga, inv, nu, cf, cb):
+def y_factor_kernel(visc, c, n, gf, gl, al, ga, inv, nu, cf, cb):
     rows, depth, width = visc.shape
     length, chunks, lines = c.shape
     group = 128 // depth
@@ -222,10 +211,10 @@
     inv[...] = 1.0 / b
 
 
-def x_solve_kernel(pos, visc, vel, rhs0, c, n, coef, near, far, pair, cross, w, payload, edge_lo, edge_hi):
+def x_solve_kernel(visc, vel, rhs0, c, n, coef, near, far, pair, cross, w, payload, edge_lo, edge_hi):
     rows, depth, width = visc.shape
     sub = iota((depth, width), 0)
-    upper = lax.rem(pos[2], 2)
+    upper = lax.rem(lax.axis_index("gz"), 2)
     two = 2.0 * HALF_Z
     by_pair = two * (near[1] + pair[1]) * (pair[0] - near[0])
     by_cross = two * (far[1] + cross[1]) * (cross[0] - far[0])
@@ -245,12 +234,12 @@
 
 
 def make_middle_kernel(parts_n):
-    def kernel(pos, *refs):
+    def kernel(*refs):
         parts = refs[:parts_n]
         (w, gf, gl, vel, cy, ny, gfy, gly, aly, gay, invy, cz, nz,
          dz, ends, slots, flux, src, sol, turned) = refs[parts_n:]
         rows, depth, width = w.shape
-        me = pos[0]
+        me = lax.axis_index("gx")
         for k in range(parts_n):
             slots[jnp.bitwise_xor(me, k)] = parts[k][...]
         zero = jnp.zeros((depth, width), F32)
@@ -302,40 +291,84 @@
     return kernel
 
 
-def final_kernel(pos, dz, gf, gl, q_left, q_right, out, buf, sems):
-    depth, rows, width = dz.shape
-    parts = buf.shape[0]
-    group = rows // parts
-    copies = []
-    for p in range(parts):
-        at = slice(p * group, (p + 1) * group)
-        d = dz[:, at] + q_right[at] * gl[:, at] - q_left[at] * gf[:, at]
-        buf[p] = jnp.transpose(d, (1, 0, 2))
-        copy = pltpu.make_async_copy(buf.at[p], out.at[pl.ds(p * group, group)], sems.at[p])
-        copy.start()
-        copies.append(copy)
-    for copy in copies:
-        copy.wait()
-
-
-def ordered(parts, me):
-    bit = 1
-    parts = list(parts)
-    while bit < len(parts):
-        odd = (me & bit) != 0
-        parts = [jnp.where(odd, parts[i ^ bit], parts[i]) for i in range(len(parts))]
-        bit *= 2
-    return parts
+def chip_factor_kernel(own, mate, near, far, pair, cross, pair_c, chip_c):
+    is_low = lax.rem(lax.axis_index("gz"), 2) == 0
+    low = [jnp.where(is_low, own[k], mate[k]) for k in range(3)]
+    high = [jnp.where(is_low, mate[k], own[k]) for k in range(3)]
+    mid_reach = 1.0 / (HALF_Z * (near[1] + pair[1]))
+    end_reach = 1.0 / (HALF_Z * (far[1] + cross[1]))
+    weight = 1.0 / (mid_reach + low[2] + high[0])
+    pair_c[0] = weight
+    pair_c[1] = low[1]
+    pair_c[2] = high[1]
+    chip_c[0] = low[0] - weight * low[1] * low[1] + jnp.where(is_low, end_reach, 0.0)
+    chip_c[1] = weight * low[1] * high[1]
+    chip_c[2] = high[2] - weight * high[1] * high[1] + jnp.where(is_low, 0.0, end_reach)
+
+
+def pair_kernel(own, mate, pair_c, chip_ends, jump_out):
+    is_low = lax.rem(lax.axis_index("gz"), 2) == 0
+    low_last = jnp.where(is_low, own[1], mate[1])
+    high_first = jnp.where(is_low, mate[0], own[0])
+    jump = high_first - low_last
+    q_mid = pair_c[0] * jump
+    jump_out[...] = jump
+    chip_ends[0] = jnp.where(is_low, own[0], mate[0]) + pair_c[1] * q_mid
+    chip_ends[1] = jnp.where(is_low, mate[1], own[1]) - pair_c[2] * q_mid
+
+
+def make_final_kernel(chips):
+    def kernel(*refs):
+        coefs, ends = refs[:chips], refs[chips:2 * chips]
+        pair_c, jump, dz, gf, gl, out, c_at, d_at, flux, buf, sems = refs[2 * chips:]
+        depth, rows, width = dz.shape
+        parts = buf.shape[0]
+        group = rows // parts
+        chip = lax.div(lax.axis_index("gz"), 2)
+        is_low = lax.rem(lax.axis_index("gz"), 2) == 0
+        for k in range(chips):
+            c_at[jnp.bitwise_xor(chip, k)] = coefs[k][...]
+            d_at[jnp.bitwise_xor(chip, k)] = ends[k][...]
+        zero = jnp.zeros((group, width), F32)
+        copies = []
+        for p in range(parts):
+            at = slice(p * group, (p + 1) * group)
+            flux[0] = zero
+            flux[chips] = zero
+            lower, right = [], None
+            for f in range(chips - 1):
+                pivot = c_at[f, 2, at] + c_at[f + 1, 0, at]
+                source = d_at[f + 1, 0, at] - d_at[f, 1, at]
+                if f:
+                    pivot = pivot - c_at[f, 1, at] * lower[-1]
+                    source = source + lower[-1] * right
+                r = 1.0 / pivot
+                lower.append(c_at[f + 1, 1, at] * r)
+                right = source
+                flux[f + 1] = source * r
+            q = flux[chips - 1]
+            for f in reversed(range(chips - 2)):
+                q = flux[f + 1] + lower[f] * q
+                flux[f + 1] = q
+            left, right = flux[chip], flux[chip + 1]
+            mid = pair_c[0, at] * (jump[at] + right * pair_c[2, at] + left * pair_c[1, at])
+            q_left = jnp.where(is_low, left, mid)
+            q_right = jnp.where(is_low, mid, right)
+            d = dz[:, at] + q_right * gl[:, at] - q_left * gf[:, at]
+            buf[p] = jnp.transpose(d, (1, 0, 2))
+            copy = pltpu.make_async_copy(buf.at[p], out.at[pl.ds(p * group, group)], sems.at[p])
+            copy.start()
+            copies.append(copy)
+        for copy in copies:
+            copy.wait()
+
+    return kernel
 
 
 def local(velocity, viscosity, force):
     rows, depth, width = velocity.shape
     nx, nz = lax.axis_size("gx"), lax.axis_size("gz")
     chips = nz // 2
-    ix, iz = lax.axis_index("gx"), lax.axis_index("gz")
-    upper = iz % 2
-    chip = iz // 2
-    pos = jnp.stack([ix, jnp.int32(nx), iz, jnp.int32(nz)]).astype(jnp.int32)
     volume = (rows, depth, width)
     zmajor = (depth, rows, width)
     lines = (width // Y_CHUNKS, Y_CHUNKS, rows * depth)
@@ -350,95 +383,65 @@
     def to_chip(k):
         return [(i, i ^ (2 * k)) for i in range(nz)]
 
-    visc, vel, visc_z, near, far = call(
-        load_kernel, [volume, volume, zmajor, (2,) + slab, (2,) + slab], [HBM, HBM],
-        [pltpu.VMEM(zmajor, F32), pltpu.SemaphoreType.DMA((2, 2))], size, 6 * size,
-    )(pos, viscosity, velocity)
+    visc, vel = viscosity, velocity
+    visc_z, near, far = call(
+        turn_kernel, [zmajor, (2,) + slab, (2,) + slab], [VMEM, VMEM],
+        [pltpu.VMEM(zmajor, F32)], size, 6 * size,
+    )(visc, vel)
     pair = lax.ppermute(near, "gz", pair_route)
     cross = lax.ppermute(far, "gz", cross_route)
 
     c_z, n_z, gf_z, gl_z, planes = call(
         z_factor_kernel, [zmajor] * 4 + [(3,) + slab], [VMEM],
         [pltpu.VMEM(zmajor, F32)] * 2, 20 * size, 5 * size,
-    )(pos, visc_z)
+    )(visc_z)
     c_x, n_x, gf_x, gl_x, coef, rhs0 = call(
         x_factor_kernel, [volume] * 4 + [(5,) + plane, volume], [VMEM, VMEM, HBM],
         [pltpu.VMEM(volume, F32)] * 3 + [pltpu.SemaphoreType.DMA(())], 60 * size, 9 * size,
-    )(pos, visc, vel, force)
+    )(visc, vel, force)
     c_y, n_y, gf_y, gl_y, al_y, ga_y, inv_y = call(
         y_factor_kernel, [lines] * 4 + [(y_steps,) + lines[1:]] * 2 + [lines[1:]], [VMEM],
         [pltpu.VMEM(lines, F32)] * 3, 30 * size, 6 * size,
-    )(pos, visc)
+    )(visc)
 
     mate_c = lax.ppermute(planes, "gz", pair_route)
 
     w, payload = call(
         x_solve_kernel, [volume, (7,) + plane], [VMEM] * 10,
         [pltpu.VMEM(slab, F32)] * 2, 20 * size, 6 * size,
-    )(pos, visc, vel, rhs0, c_x, n_x, coef, near, far, pair, cross)
-    mid_reach = 1.0 / (HALF_Z * (near[1] + pair[1]))
-    end_reach = 1.0 / (HALF_Z * (far[1] + cross[1]))
-    low_c = jnp.where(upper == 0, planes, mate_c)
-    high_c = jnp.where(upper == 0, mate_c, planes)
-    weight = 1.0 / (mid_reach + low_c[2] + high_c[0])
-    low_fl, high_fl = low_c[1], high_c[1]
-    chip_c = jnp.stack([
-        low_c[0] - weight * low_fl * low_fl + jnp.where(upper == 0, end_reach, 0.0),
-        weight * low_fl * high_fl,
-        high_c[2] - weight * high_fl * high_fl + jnp.where(upper == 0, 0.0, end_reach),
-    ])
+    )(visc, vel, rhs0, c_x, n_x, coef, near, far, pair, cross)
+    pair_c, chip_c = call(
+        chip_factor_kernel, [(3,) + slab] * 2, [VMEM] * 6, (), size, size
+    )(planes, mate_c, near, far, pair, cross)
     payload, chip_c = lax.optimization_barrier((payload, chip_c))
     parts = [payload] + [
         lax.ppermute(payload, "gx", [(i, i ^ k) for i in range(nx)]) for k in range(1, nx)
     ]
-    all_c = ordered(
-        [chip_c] + [lax.ppermute(chip_c, "gz", to_chip(k)) for k in range(1, chips)], chip
-    )
-    lower, inverse = [], []
-    for f in range(chips - 1):
-        pivot = all_c[f][2] + all_c[f + 1][0]
-        if f:
-            pivot = pivot - all_c[f][1] * lower[-1]
-        inverse.append(1.0 / pivot)
-        lower.append(all_c[f + 1][1] * inverse[-1])
-
+    coefs = [chip_c] + [lax.ppermute(chip_c, "gz", to_chip(k)) for k in range(1, chips)]
+
+    w, *coefs = lax.optimization_barrier((w, *coefs))
     dz, ends = call(
         make_middle_kernel(nx), [zmajor, (2,) + slab], [VMEM] * (nx + 13),
         [pltpu.VMEM((nx, 7) + plane, F32), pltpu.VMEM((nx + 1,) + plane, F32),
          pltpu.VMEM(lines, F32), pltpu.VMEM(lines, F32), pltpu.VMEM(zmajor, F32)],
         60 * size, 14 * size,
-    )(pos, *parts, w, gf_x, gl_x, vel, c_y, n_y, gf_y, gl_y, al_y, ga_y, inv_y, c_z, n_z)
+    )(*parts, w, gf_x, gl_x, vel, c_y, n_y, gf_y, gl_y, al_y, ga_y, inv_y, c_z, n_z)
 
     mate = lax.ppermute(ends, "gz", pair_route)
-    low = jnp.where(upper == 0, ends, mate)
-    high = jnp.where(upper == 0, mate, ends)
-    jump = high[0] - low[1]
-    q_mid = weight * jump
-    chip_ends = jnp.stack([low[0] + low_fl * q_mid, high[1] - high_fl * q_mid])
-    by_chip = ordered(
-        [chip_ends] + [lax.ppermute(chip_ends, "gz", to_chip(k)) for k in range(1, chips)], chip
-    )
-    source, fluxes = [], []
-    for f in range(chips - 1):
-        right = by_chip[f + 1][0] - by_chip[f][1]
-        if f:
-            right = right + lower[f - 1] * source[-1]
-        source.append(right)
-        fluxes.append(right * inverse[f])
-    for f in reversed(range(chips - 2)):
-        fluxes[f] = fluxes[f] + lower[f] * fluxes[f + 1]
-    chip_left = chip_right = jnp.zeros(slab, F32)
-    for f in range(chips - 1):
-        chip_right = jnp.where(chip == f, fluxes[f], chip_right)
-        chip_left = jnp.where(chip == f + 1, fluxes[f], chip_left)
-    q_mid = weight * (jump + chip_right * high_fl + chip_left * low_fl)
-    q_left = jnp.where(upper == 0, chip_left, q_mid)
-    q_right = jnp.where(upper == 0, q_mid, chip_right)
+    chip_ends, jump = call(pair_kernel, [(2,) + slab, slab], [VMEM] * 3, (), size, size)(
+        ends, mate, pair_c
+    )
+    others = [chip_ends] + [lax.ppermute(chip_ends, "gz", to_chip(k)) for k in range(1, chips)]
+    parts_out = 4
+    group = (rows // parts_out, width)
     return call(
-        final_kernel, [volume], [VMEM] * 5,
-        [pltpu.VMEM((4, rows // 4, depth, width), F32), pltpu.SemaphoreType.DMA((4,))],
-        4 * size, 4 * size, [HBM],
-    )(pos, dz, gf_z, gl_z, q_left, q_right)[0]
+        make_final_kernel(chips), [volume], [VMEM] * (2 * chips + 5),
+        [pltpu.VMEM((chips, 3) + slab, F32), pltpu.VMEM((chips, 2) + slab, F32),
+         pltpu.VMEM((chips + 1,) + group, F32),
+         pltpu.VMEM((parts_out, rows // parts_out, depth, width), F32),
+         pltpu.SemaphoreType.DMA((parts_out,))],
+        8 * size, 5 * size, [HBM],
+    )(*coefs, *others, pair_c, jump, dz, gf_z, gl_z)[0]
 
 
 def solution(mesh):

time: 52.2 us -> 39.6 us (0.76)
  Pallas kernels: 11.8 us -> 7.08 us
  waiting for transfers between devices: 16.5 us -> 12.5 us
  other arithmetic: 2.62 us -> 0 us
  local copies, waits for them, and re-layouts: 3.71 us -> 2.1 us
  starting transfers between devices: 16.9 us -> 17.6 us
    ppermute x3, starting transfers between devices: 3.57 us -> 7.87 us  [local(): lax.ppermute(chip_c, 'gz', to_chip(k))]
    ppermute x3, waiting for transfers between devices: 8 us -> 4.02 us  [local(): lax.ppermute(chip_c, 'gz', to_chip(k))]
    ppermute x1, starting transfers between devices: 3.91 us -> 0.08 us  [local(): pair = lax.ppermute(near, 'gz', pair_route)]
    ppermute x3, waiting for transfers between devices: 4.56 us -> 0.78 us  [local(): lax.ppermute(payload, 'gx', [(i, i ^ k) for i in range(nx)])]
    ppermute x3, waiting for transfers between devices: 3.96 us -> 6.33 us  [local(): lax.ppermute(chip_ends, 'gz', to_chip(k))]
    unnamed x18 -> x10, local copies, waits for them, and re-layouts: 3.71 us -> 2.1 us
    select_n x7 -> x0, other arithmetic: 1.46 us -> none  [the longest x1 1.05 us: local(): high_c = jnp.where(upper == 0, mate_c, planes)]
    ppermute x1, waiting for transfers between devices: 0.01 us -> 1.33 us  [local(): mate = lax.ppermute(ends, 'gz', pair_route)]
  transfers between devices with their start and end apart: 13 -> 13, of which waited for: 6 -> 6; matrix products, arithmetic and copies ran while one was open for 0% -> 0% of each run, Pallas kernels for 12% -> 11%
where the time goes in v2:
time: 39.6 us; the launch traced here: 39.4 us
  starting transfers between devices  17.6 us (44%)
  waiting for transfers between devices  12.5 us (32%)
  Pallas kernels  7.08 us (18%)
  local copies, waits for them, and re-layouts  2.1 us (5%)
    ppermute x3, starting transfers between devices, local(): lax.ppermute(chip_c, 'gz', to_chip(k))  7.87 us
    ppermute x3, waiting for transfers between devices, local(): lax.ppermute(chip_ends, 'gz', to_chip(k))  6.33 us
    ppermute x3, starting transfers between devices, local(): lax.ppermute(payload, 'gx', [(i, i ^ k) for i in range(nx)])  4.9 us
    ppermute x3, waiting for transfers between devices, local(): lax.ppermute(chip_c, 'gz', to_chip(k))  4.02 us
    pallas_call x1, Pallas kernels, local(): call(x_factor_kernel, [volume] * 4 + [(5,) + plane, volume], [VMEM, VMEM,...  3.56 us
    ppermute x3, starting transfers between devices, local(): lax.ppermute(chip_ends, 'gz', to_chip(k))  3.55 us
    unnamed x10, local copies, waits for them, and re-layouts  2.1 us
    ppermute x1, waiting for transfers between devices, local(): mate = lax.ppermute(ends, 'gz', pair_route)  1.33 us
  transfers between devices with their start and end apart: 13, of which 6 were waited for; matrix products, arithmetic and copies ran while one was open for 0% of the time, Pallas kernels for 11%

profile of v2, /device:TPU:0, one launch (start us, length us, event | category | flops | bytes accessed | tf_op | source)
XLA Modules:
  0.0 39.4 jit_solution(13396853851920092077)
XLA Ops:
  0.0 0.0 copy-start
  0.0 1.0 %copy-done = f32[64,8,256]{2,1,0:T(8,128)S(1)} copy-done((f32[64,8,256]{2,1,0:T(8,128)S(1)}, f32[64,8,256]{2,1,0:T(8,128)}, u32[]{:S(2)}) %copy-start) | copy-done | bytes 524312
  1.0 0.0 copy-start.2
  1.0 1.0 %copy-done.2 = f32[64,8,256]{2,1,0:T(8,128)S(1)} copy-done((f32[64,8,256]{2,1,0:T(8,128)S(1)}, f32[64,8,256]{2,1,0:T(8,128)}, u32[]{:S(2)}) %copy-start.2) | copy-done | bytes 524312
  2.1 0.0 copy-start.3
  2.1 0.0 copy-start.4
  2.1 0.3 shard_map.38
  2.4 0.0 copy-start.1
  2.4 0.4 shard_map.40
  2.8 0.5 %collective-permute-start.2 = (f32[3,64,256]{2,1,0:T(8,128)S(1)}, f32[3,64,256]{2,1,0:T(8,128)S(1)}, u32[]{:S(2)}, u32[]{:S(2)}) collective-permute-start(f32[3,64,256]{2,1,0:T(8,128)S(1)} %get-tuple-element.50.own), channel_id=1, source_target_pairs={{0,1},{1,0},{2,3},{3,2},{4,5},{5,4},{6,7},{7,6},{8,9},{9,8},{10,11... | collective-permute-start | bytes 589832 | tf_op jit(solution)/shard_map/ppermute | solution.py:407
  3.3 0.1 collective-permute-start
  3.4 0.7 %collective-permute-start.1 = (f32[2,64,256]{2,1,0:T(8,128)S(1)}, f32[2,64,256]{2,1,0:T(8,128)S(1)}, u32[]{:S(2)}, u32[]{:S(2)}) collective-permute-start(f32[2,64,256]{2,1,0:T(8,128)S(1)} %get-tuple-element.46.far), channel_id=1, source_target_pairs={{1,2},{2,1},{3,4},{4,3},{5,6},{6,5},{9,10},{10,9},{11,12},{12,11},... | collective-permute-start | bytes 393224 | tf_op jit(solution)/shard_map/ppermute | solution.py:392
  4.0 0.0 copy-done.3
  4.0 0.0 copy-done.4
  4.1 0.0 copy-done.1
  4.1 3.6 %shard_map.37 = (f32[64,8,256]{2,1,0:T(8,128)S(1)}, f32[64,8,256]{2,1,0:T(8,128)S(1)}, f32[64,8,256]{2,1,0:T(8,128)S(1)}, f32[64,8,256]{2,1,0:T(8,128)S(1)}, f32...) custom-call(f32[64,8,256]{2,1,0:T(8,128)S(1)} %copy-done.1, f32[64,8,256]{2,1,0:T(8,128)S(1)} %copy-done.3, ...), custom_call_target="tpu_custom_call" | custom-call | flops 7864320 | bytes 4718592 | tf_op jit(solution)/shard_map/pallas_call | solution.py:398
  7.6 0.0 collective-permute-done.pair
  7.6 0.0 collective-permute-done.1.cross
  7.7 0.3 shard_map.39
  7.9 0.0 collective-permute-done.2.mate
  7.9 0.1 shard_map.41
  8.0 5.0 %collective-permute-start.3 = (f32[3,64,256]{2,1,0:T(8,128)S(1)}, f32[3,64,256]{2,1,0:T(8,128)S(1)}, u32[]{:S(2)}, u32[]{:S(2)}) collective-permute-start(f32[3,64,256]{2,1,0:T(8,128)S(1)} %get-tuple-element.53.refs_0_), channel_id=1, source_target_pairs={{0,2},{1,3},{2,0},{3,1},{4,6},{5,7},{6,4},{7,5},{8,10},{9,11},{10,... | collective-permute-start | bytes 589832 | tf_op jit(solution)/shard_map/ppermute | solution.py:420
  13.0 2.7 %collective-permute-start.4 = (f32[3,64,256]{2,1,0:T(8,128)S(1)}, f32[3,64,256]{2,1,0:T(8,128)S(1)}, u32[]{:S(2)}, u32[]{:S(2)}) collective-permute-start(f32[3,64,256]{2,1,0:T(8,128)S(1)} %get-tuple-element.53.refs_0_), channel_id=1, source_target_pairs={{0,4},{1,5},{2,6},{3,7},{4,0},{5,1},{6,2},{7,3},{8,12},{9,13},{10,... | collective-permute-start | bytes 589832 | tf_op jit(solution)/shard_map/ppermute | solution.py:420
  15.7 0.2 collective-permute-start.5
  15.9 1.8 %collective-permute-start.6 = (f32[7,8,256]{2,1,0:T(8,128)S(1)}, f32[7,8,256]{2,1,0:T(8,128)S(1)}, u32[]{:S(2)}, u32[]{:S(2)}) collective-permute-start(f32[7,8,256]{2,1,0:T(8,128)S(1)} %get-tuple-element.57.refs_0_), channel_id=1, source_target_pairs={{0,8},{8,0},{16,24},{24,16},{1,9},{9,1},{17,25},{25,17},{2,10},{10... | collective-permute-start | bytes 172040 | tf_op jit(solution)/shard_map/ppermute | solution.py:418
  17.7 2.6 %collective-permute-start.7 = (f32[7,8,256]{2,1,0:T(8,128)S(1)}, f32[7,8,256]{2,1,0:T(8,128)S(1)}, u32[]{:S(2)}, u32[]{:S(2)}) collective-permute-start(f32[7,8,256]{2,1,0:T(8,128)S(1)} %get-tuple-element.57.refs_0_), channel_id=1, source_target_pairs={{0,16},{8,24},{16,0},{24,8},{1,17},{9,25},{17,1},{25,9},{2,18},{10... | collective-permute-start | bytes 172040 | tf_op jit(solution)/shard_map/ppermute | solution.py:418
  20.3 0.0 collective-permute-done.3.refs_1_
  20.3 0.5 %collective-permute-start.8 = (f32[7,8,256]{2,1,0:T(8,128)S(1)}, f32[7,8,256]{2,1,0:T(8,128)S(1)}, u32[]{:S(2)}, u32[]{:S(2)}) collective-permute-start(f32[7,8,256]{2,1,0:T(8,128)S(1)} %get-tuple-element.57.refs_0_), channel_id=1, source_target_pairs={{0,24},{8,16},{16,8},{24,0},{1,25},{9,17},{17,9},{25,1},{2,26},{10... | collective-permute-start | bytes 172040 | tf_op jit(solution)/shard_map/ppermute | solution.py:418
  20.8 0.6 %shard_map.42 = (f32[32,8,512]{2,1,0:T(8,128)S(1)}, f32[32,8,512]{2,1,0:T(8,128)S(1)}, f32[32,8,512]{2,1,0:T(8,128)S(1)}, f32[32,8,512]{2,1,0:T(8,128)S(1)}, f32...) custom-call(f32[64,8,256]{2,1,0:T(8,128)S(1)} %copy-done.1), custom_call_target="tpu_custom_call" | custom-call | flops 3932160 | bytes 3145728 | tf_op jit(solution)/shard_map/pallas_call | solution.py:402
  21.4 4.0 %collective-permute-done.4.refs_2_ = f32[3,64,256]{2,1,0:T(8,128)S(1)} collective-permute-done((f32[3,64,256]{2,1,0:T(8,128)S(1)}, f32[3,64,256]{2,1,0:T(8,128)S(1)}, u32[]{:S(2)}, u32[]{:S(2)}) %collective-permute-start.4) | collective-permute-done | bytes 196640 | tf_op jit(solution)/shard_map/ppermute | solution.py:420
  25.4 0.0 collective-permute-done.5.refs_3_
  25.4 0.0 collective-permute-done.6.refs_1_
  25.5 0.0 collective-permute-done.7.refs_2_
  25.5 0.8 %collective-permute-done.8.refs_3_ = f32[7,8,256]{2,1,0:T(8,128)S(1)} collective-permute-done((f32[7,8,256]{2,1,0:T(8,128)S(1)}, f32[7,8,256]{2,1,0:T(8,128)S(1)}, u32[]{:S(2)}, u32[]{:S(2)}) %collective-permute-start.8) | collective-permute-done | bytes 57376 | tf_op jit(solution)/shard_map/ppermute | solution.py:418
  26.2 0.8 %shard_map.43 = (f32[8,64,256]{2,1,0:T(8,128)S(1)}, f32[2,64,256]{2,1,0:T(8,128)S(1)}) custom-call(f32[7,8,256]{2,1,0:T(8,128)S(1)} %get-tuple-element.57.refs_0_, f32[7,8,256]{2,1,0:T(8,128)S(1)} %collective-permute-done.6.refs_1_, f32[7,8,256]{2,1,0:T(8,128)S(1)} %collective-permute-done.7.refs_2_, f32[7,8,256]{2,1,0:T(8,128)S(1)} %collective-permute-done.8.refs_3_, ...), custom_call_target="tpu_custom_call" | custom-call | flops 7864320 | bytes 7340032 | tf_op jit(solution)/shard_map/pallas_call | solution.py:423
  27.0 0.1 collective-permute-start.9
  27.1 1.3 %collective-permute-done.9.mate = f32[2,64,256]{2,1,0:T(8,128)S(1)} collective-permute-done((f32[2,64,256]{2,1,0:T(8,128)S(1)}, f32[2,64,256]{2,1,0:T(8,128)S(1)}, u32[]{:S(2)}, u32[]{:S(2)}) %collective-permute-start.9) | collective-permute-done | bytes 131104 | tf_op jit(solution)/shard_map/ppermute | solution.py:430
  28.5 1.6 %collective-permute-start.10 = (f32[2,64,256]{2,1,0:T(8,128)S(1)}, f32[2,64,256]{2,1,0:T(8,128)S(1)}, u32[]{:S(2)}, u32[]{:S(2)}) collective-permute-start(f32[2,64,256]{2,1,0:T(8,128)S(1)} %get-tuple-element.72.refs_4_), channel_id=1, source_target_pairs={{0,2},{1,3},{2,0},{3,1},{4,6},{5,7},{6,4},{7,5},{8,10},{9,11},{10,... | collective-permute-start | bytes 393224 | tf_op jit(solution)/shard_map/ppermute | solution.py:434
  30.0 1.6 %collective-permute-start.11 = (f32[2,64,256]{2,1,0:T(8,128)S(1)}, f32[2,64,256]{2,1,0:T(8,128)S(1)}, u32[]{:S(2)}, u32[]{:S(2)}) collective-permute-start(f32[2,64,256]{2,1,0:T(8,128)S(1)} %get-tuple-element.72.refs_4_), channel_id=1, source_target_pairs={{0,4},{1,5},{2,6},{3,7},{4,0},{5,1},{6,2},{7,3},{8,12},{9,13},{10,... | collective-permute-start | bytes 393224 | tf_op jit(solution)/shard_map/ppermute | solution.py:434
  31.6 0.4 collective-permute-start.12
  32.0 2.4 %collective-permute-done.10.refs_5_ = f32[2,64,256]{2,1,0:T(8,128)S(1)} collective-permute-done((f32[2,64,256]{2,1,0:T(8,128)S(1)}, f32[2,64,256]{2,1,0:T(8,128)S(1)}, u32[]{:S(2)}, u32[]{:S(2)}) %collective-permute-start.10) | collective-permute-done | bytes 131104 | tf_op jit(solution)/shard_map/ppermute | solution.py:434
  34.4 2.8 %collective-permute-done.11.refs_6_ = f32[2,64,256]{2,1,0:T(8,128)S(1)} collective-permute-done((f32[2,64,256]{2,1,0:T(8,128)S(1)}, f32[2,64,256]{2,1,0:T(8,128)S(1)}, u32[]{:S(2)}, u32[]{:S(2)}) %collective-permute-start.11) | collective-permute-done | bytes 131104 | tf_op jit(solution)/shard_map/ppermute | solution.py:434
  37.2 1.1 %collective-permute-done.12.refs_7_ = f32[2,64,256]{2,1,0:T(8,128)S(1)} collective-permute-done((f32[2,64,256]{2,1,0:T(8,128)S(1)}, f32[2,64,256]{2,1,0:T(8,128)S(1)}, u32[]{:S(2)}, u32[]{:S(2)}) %collective-permute-start.12) | collective-permute-done | bytes 131104 | tf_op jit(solution)/shard_map/ppermute | solution.py:434
  38.3 1.1 %shard_map.45 = f32[64,8,256]{2,1,0:T(8,128)} custom-call(f32[3,64,256]{2,1,0:T(8,128)S(1)} %get-tuple-element.53.refs_0_, f32[3,64,256]{2,1,0:T(8,128)S(1)} %collective-permute-done.3.refs_1_, f32[3,64,256]{2,1,0:T(8,128)S(1)} %collective-permute-done.4.refs_2_, f32[3,64,256]{2,1,0:T(8,128)S(1)} %collective-permute-done.5.refs_3_, ...), custom_call_target="tpu_custom_call" | custom-call | flops 1048576 | bytes 2621440 | tf_op jit(solution)/shard_map/pallas_call | solution.py:437
  (1 shorter events, 0.0 us)
Async XLA Ops:
  0.0 1.0 %copy-start = (f32[64,8,256]{2,1,0:T(8,128)S(1)}, f32[64,8,256]{2,1,0:T(8,128)}, u32[]{:S(2)}) copy-start(f32[64,8,256]{2,1,0:T(8,128)} %visc.7) | copy-start | bytes 1572868
  1.0 1.0 %copy-start.2 = (f32[64,8,256]{2,1,0:T(8,128)S(1)}, f32[64,8,256]{2,1,0:T(8,128)}, u32[]{:S(2)}) copy-start(f32[64,8,256]{2,1,0:T(8,128)} %refs_7_.1) | copy-start | bytes 1572868
  2.1 2.0 %copy-start.3 = (f32[64,8,256]{2,1,0:T(8,128)S(1)}, f32[64,8,256]{2,1,0:T(8,128)}, u32[]{:S(2)}) copy-start(f32[64,8,256]{2,1,0:T(8,128)} %refs_7_.1) | copy-start | bytes 1572868
  2.1 2.0 %copy-start.4 = (f32[64,8,256]{2,1,0:T(8,128)S(1)}, f32[64,8,256]{2,1,0:T(8,128)}, u32[]{:S(2)}) copy-start(f32[64,8,256]{2,1,0:T(8,128)} %force_hbm.1) | copy-start | bytes 1572868
  2.4 1.7 %copy-start.1 = (f32[64,8,256]{2,1,0:T(8,128)S(1)}, f32[64,8,256]{2,1,0:T(8,128)}, u32[]{:S(2)}) copy-start(f32[64,8,256]{2,1,0:T(8,128)} %visc.7) | copy-start | bytes 1572868
  2.8 5.1 %collective-permute-start.2 = (f32[3,64,256]{2,1,0:T(8,128)S(1)}, f32[3,64,256]{2,1,0:T(8,128)S(1)}, u32[]{:S(2)}, u32[]{:S(2)}) collective-permute-start(f32[3,64,256]{2,1,0:T(8,128)S(1)} %get-tuple-element.50.own), channel_id=1, source_target_pairs={{0,1},{1,0},{2,3},{3,2},{4,5},{5,4},{6,7},{7,6},{8,9},{9,8},{10,11... | collective-permute-start | bytes 589832 | tf_op jit(solution)/shard_map/ppermute | solution.py:407
  3.3 4.3 %collective-permute-start = (f32[2,64,256]{2,1,0:T(8,128)S(1)}, f32[2,64,256]{2,1,0:T(8,128)S(1)}, u32[]{:S(2)}, u32[]{:S(2)}) collective-permute-start(f32[2,64,256]{2,1,0:T(8,128)S(1)} %get-tuple-element.45.near), channel_id=1, source_target_pairs={{0,1},{1,0},{2,3},{3,2},{4,5},{5,4},{6,7},{7,6},{8,9},{9,8},{10,11... | collective-permute-start | bytes 393224 | tf_op jit(solution)/shard_map/ppermute | solution.py:391
  3.4 4.3 %collective-permute-start.1 = (f32[2,64,256]{2,1,0:T(8,128)S(1)}, f32[2,64,256]{2,1,0:T(8,128)S(1)}, u32[]{:S(2)}, u32[]{:S(2)}) collective-permute-start(f32[2,64,256]{2,1,0:T(8,128)S(1)} %get-tuple-element.46.far), channel_id=1, source_target_pairs={{1,2},{2,1},{3,4},{4,3},{5,6},{6,5},{9,10},{10,9},{11,12},{12,11},... | collective-permute-start | bytes 393224 | tf_op jit(solution)/shard_map/ppermute | solution.py:392
  8.0 12.2 %collective-permute-start.3 = (f32[3,64,256]{2,1,0:T(8,128)S(1)}, f32[3,64,256]{2,1,0:T(8,128)S(1)}, u32[]{:S(2)}, u32[]{:S(2)}) collective-permute-start(f32[3,64,256]{2,1,0:T(8,128)S(1)} %get-tuple-element.53.refs_0_), channel_id=1, source_target_pairs={{0,2},{1,3},{2,0},{3,1},{4,6},{5,7},{6,4},{7,5},{8,10},{9,11},{10,... | collective-permute-start | bytes 589832 | tf_op jit(solution)/shard_map/ppermute | solution.py:420
  13.0 12.5 %collective-permute-start.4 = (f32[3,64,256]{2,1,0:T(8,128)S(1)}, f32[3,64,256]{2,1,0:T(8,128)S(1)}, u32[]{:S(2)}, u32[]{:S(2)}) collective-permute-start(f32[3,64,256]{2,1,0:T(8,128)S(1)} %get-tuple-element.53.refs_0_), channel_id=1, source_target_pairs={{0,4},{1,5},{2,6},{3,7},{4,0},{5,1},{6,2},{7,3},{8,12},{9,13},{10,... | collective-permute-start | bytes 589832 | tf_op jit(solution)/shard_map/ppermute | solution.py:420
  15.7 9.7 %collective-permute-start.5 = (f32[3,64,256]{2,1,0:T(8,128)S(1)}, f32[3,64,256]{2,1,0:T(8,128)S(1)}, u32[]{:S(2)}, u32[]{:S(2)}) collective-permute-start(f32[3,64,256]{2,1,0:T(8,128)S(1)} %get-tuple-element.53.refs_0_), channel_id=1, source_target_pairs={{0,6},{1,7},{2,4},{3,5},{4,2},{5,3},{6,0},{7,1},{8,14},{9,15},{10,... | collective-permute-start | bytes 589832 | tf_op jit(solution)/shard_map/ppermute | solution.py:420
  15.9 9.6 %collective-permute-start.6 = (f32[7,8,256]{2,1,0:T(8,128)S(1)}, f32[7,8,256]{2,1,0:T(8,128)S(1)}, u32[]{:S(2)}, u32[]{:S(2)}) collective-permute-start(f32[7,8,256]{2,1,0:T(8,128)S(1)} %get-tuple-element.57.refs_0_), channel_id=1, source_target_pairs={{0,8},{8,0},{16,24},{24,16},{1,9},{9,1},{17,25},{25,17},{2,10},{10... | collective-permute-start | bytes 172040 | tf_op jit(solution)/shard_map/ppermute | solution.py:418
  17.7 7.8 %collective-permute-start.7 = (f32[7,8,256]{2,1,0:T(8,128)S(1)}, f32[7,8,256]{2,1,0:T(8,128)S(1)}, u32[]{:S(2)}, u32[]{:S(2)}) collective-permute-start(f32[7,8,256]{2,1,0:T(8,128)S(1)} %get-tuple-element.57.refs_0_), channel_id=1, source_target_pairs={{0,16},{8,24},{16,0},{24,8},{1,17},{9,25},{17,1},{25,9},{2,18},{10... | collective-permute-start | bytes 172040 | tf_op jit(solution)/shard_map/ppermute | solution.py:418
  20.3 6.0 %collective-permute-start.8 = (f32[7,8,256]{2,1,0:T(8,128)S(1)}, f32[7,8,256]{2,1,0:T(8,128)S(1)}, u32[]{:S(2)}, u32[]{:S(2)}) collective-permute-start(f32[7,8,256]{2,1,0:T(8,128)S(1)} %get-tuple-element.57.refs_0_), channel_id=1, source_target_pairs={{0,24},{8,16},{16,8},{24,0},{1,25},{9,17},{17,9},{25,1},{2,26},{10... | collective-permute-start | bytes 172040 | tf_op jit(solution)/shard_map/ppermute | solution.py:418
  27.0 1.4 %collective-permute-start.9 = (f32[2,64,256]{2,1,0:T(8,128)S(1)}, f32[2,64,256]{2,1,0:T(8,128)S(1)}, u32[]{:S(2)}, u32[]{:S(2)}) collective-permute-start(f32[2,64,256]{2,1,0:T(8,128)S(1)} %get-tuple-element.70.own), channel_id=1, source_target_pairs={{0,1},{1,0},{2,3},{3,2},{4,5},{5,4},{6,7},{7,6},{8,9},{9,8},{10,11... | collective-permute-start | bytes 393224 | tf_op jit(solution)/shard_map/ppermute | solution.py:430
  28.5 6.0 %collective-permute-start.10 = (f32[2,64,256]{2,1,0:T(8,128)S(1)}, f32[2,64,256]{2,1,0:T(8,128)S(1)}, u32[]{:S(2)}, u32[]{:S(2)}) collective-permute-start(f32[2,64,256]{2,1,0:T(8,128)S(1)} %get-tuple-element.72.refs_4_), channel_id=1, source_target_pairs={{0,2},{1,3},{2,0},{3,1},{4,6},{5,7},{6,4},{7,5},{8,10},{9,11},{10,... | collective-permute-start | bytes 393224 | tf_op jit(solution)/shard_map/ppermute | solution.py:434
  30.0 7.2 %collective-permute-start.11 = (f32[2,64,256]{2,1,0:T(8,128)S(1)}, f32[2,64,256]{2,1,0:T(8,128)S(1)}, u32[]{:S(2)}, u32[]{:S(2)}) collective-permute-start(f32[2,64,256]{2,1,0:T(8,128)S(1)} %get-tuple-element.72.refs_4_), channel_id=1, source_target_pairs={{0,4},{1,5},{2,6},{3,7},{4,0},{5,1},{6,2},{7,3},{8,12},{9,13},{10,... | collective-permute-start | bytes 393224 | tf_op jit(solution)/shard_map/ppermute | solution.py:434
  31.6 6.7 %collective-permute-start.12 = (f32[2,64,256]{2,1,0:T(8,128)S(1)}, f32[2,64,256]{2,1,0:T(8,128)S(1)}, u32[]{:S(2)}, u32[]{:S(2)}) collective-permute-start(f32[2,64,256]{2,1,0:T(8,128)S(1)} %get-tuple-element.72.refs_4_), channel_id=1, source_target_pairs={{0,6},{1,7},{2,4},{3,5},{4,2},{5,3},{6,0},{7,1},{8,14},{9,15},{10,... | collective-permute-start | bytes 393224 | tf_op jit(solution)/shard_map/ppermute | solution.py:434

commit v3 on v2

--- a/solution.py
+++ b/solution.py
@@ -37,10 +37,7 @@
     return pltpu.roll(x, s % x.shape[axis], axis)
 
 
-def factor(
-    nu, rows, half, lo_term, hi_term, c_out, n_out, gf_out, gl_out, cf, cb,
-    beside_pivots=lambda i: None, beside_responses=lambda i: None,
-):
+def factor(nu, rows, half, lo_term, hi_term, c_out, n_out, gf_out, gl_out, cf, cb):
     mid = rows // 2
     s, t = 1.0 + lo_term, 1.0 + hi_term
     for i in range(rows - 1):
@@ -65,11 +62,9 @@
         t = 1.0 + c * t
         if j - 1 == mid:
             t_mid = t
-        beside_pivots(i)
     n_out[mid] = 1.0 / (s_mid + t_mid - 1.0)
     gl = 1.0 / (s + hi_term)
     gf = 1.0 / (t + lo_term)
-    beside_pivots(rows - 1)
     ends = [gf, None, gl]
     gl_out[rows - 1] = gl
     gf_out[0] = gf
@@ -78,8 +73,6 @@
         gl_out[rows - 2 - i] = gl
         gf = cb[i + 1] * gf
         gf_out[i + 1] = gf
-        beside_responses(i)
-    beside_responses(rows - 1)
     ends[1] = gl
     return ends
 
@@ -111,15 +104,32 @@
     return d, u
 
 
-def turn_kernel(visc, vel, visc_z, near, far, vel_z):
-    depth = visc.shape[1]
+def turn_kernel(visc_hbm, vel_hbm, visc, vel, visc_z, near, far, vel_z, sems):
+    rows, depth, width = visc.shape
     upper = lax.rem(lax.axis_index("gz"), 2)
     near_at = (1 - upper) * (depth - 1)
     far_at = upper * (depth - 1)
-    for k, (src, turned) in enumerate(((vel, vel_z), (visc, visc_z))):
-        turned[...] = jnp.transpose(src[...], (1, 0, 2))
-        near[k] = turned[near_at]
-        far[k] = turned[far_at]
+    pieces = sems.shape[1]
+    piece = rows // pieces
+    copies = [
+        [
+            pltpu.make_async_copy(
+                src.at[pl.ds(p * piece, piece)], dst.at[pl.ds(p * piece, piece)], sems.at[k, p]
+            )
+            for p in range(pieces)
+        ]
+        for k, (src, dst) in enumerate(((vel_hbm, vel), (visc_hbm, visc)))
+    ]
+    for p in range(pieces):
+        for k in range(2):
+            copies[k][p].start()
+    for p in range(pieces):
+        at = slice(p * piece, (p + 1) * piece)
+        for k, (src, turned) in enumerate(((vel, vel_z), (visc, visc_z))):
+            copies[k][p].wait()
+            turned[:, at] = jnp.transpose(src[at], (1, 0, 2))
+            near[k, at] = turned[near_at, at]
+            far[k, at] = turned[far_at, at]
 
 
 def x_factor_kernel(visc, vel, force_hbm, c, n, gf, gl, coef, rhs, cf, cb, force, sem):
@@ -128,36 +138,39 @@
     copy.start()
     lo_wall = jnp.where(lax.axis_index("gx") == 0, HALF_X, 0.0)
     hi_wall = jnp.where(lax.axis_index("gx") == lax.axis_size("gx") - 1, HALF_X, 0.0)
-    lane = iota((depth, width), 1)
-    sub = iota((depth, width), 0)
-
-    def explicit(i):
-        v = vel[i]
-        nu = visc[i]
-        vn = jnp.where(lane == width - 1, 0.0, shift(v, -1, 1))
-        nn = jnp.where(lane == width - 1, 0.0, shift(nu, -1, 1))
-        fy = (2.0 * HALF_Y) * (nu + nn) * (vn - v)
-        fl = jnp.where(lane == 0, (2.0 * HALF_Y) * nu * v, shift(fy, 1, 1))
-        fz = (2.0 * HALF_Z) * (nu + shift(nu, -1, 0)) * (shift(v, -1, 0) - v)
-        fz = jnp.where(sub == depth - 1, 0.0, fz)
-        rhs[i] = 2.0 * v + (fy - fl) + (fz - shift(fz, 1, 0))
-
-    def add_force(i):
-        if i == 0:
-            copy.wait()
-        rhs[i] = rhs[i] + force[i]
-
     ends = factor(
         lambda i: visc[i], rows, HALF_X, lo_wall * visc[0], hi_wall * visc[rows - 1],
-        c, n, gf, gl, cf, cb, explicit, add_force,
+        c, n, gf, gl, cf, cb,
     )
     for k in range(3):
         coef[k] = ends[k]
     coef[3] = visc[0]
     coef[4] = visc[rows - 1]
-
-
-def z_factor_kernel(visc_z, c, n, gf, gl, planes, cf, cb):
+    block = min(rows, 16)
+    lane = iota((block, depth, width), 2)
+    sub = iota((block, depth, width), 1)
+    copy.wait()
+    for i in range(0, rows, block):
+        at = slice(i, i + block)
+        v = vel[at]
+        nu = visc[at]
+        vn = jnp.where(lane == width - 1, 0.0, shift(v, -1, 2))
+        nn = jnp.where(lane == width - 1, 0.0, shift(nu, -1, 2))
+        fy = (2.0 * HALF_Y) * (nu + nn) * (vn - v)
+        fl = jnp.where(lane == 0, (2.0 * HALF_Y) * nu * v, shift(fy, 1, 2))
+        fz = (2.0 * HALF_Z) * (nu + shift(nu, -1, 1)) * (shift(v, -1, 1) - v)
+        fz = jnp.where(sub == depth - 1, 0.0, fz)
+        rhs[at] = force[at] + 2.0 * v + (fy - fl) + (fz - shift(fz, 1, 1))
+
+
+def split_rows(source, keep, give):
+    half = keep.shape[1]
+    upper = lax.rem(lax.axis_index("gz"), 2)
+    keep[...] = source[:, pl.ds(pl.multiple_of(upper * half, half), half)]
+    give[...] = source[:, pl.ds(pl.multiple_of((1 - upper) * half, half), half)]
+
+
+def z_factor_kernel(visc_z, c, n, gf, gl, keep, give, cf, cb, planes):
     depth = visc_z.shape[0]
     lo_wall = jnp.where(lax.axis_index("gz") == 0, HALF_Z, 0.0)
     hi_wall = jnp.where(lax.axis_index("gz") == lax.axis_size("gz") - 1, HALF_Z, 0.0)
@@ -167,6 +180,7 @@
     )
     for k in range(3):
         planes[k] = ends[k]
+    split_rows(planes, keep, give)
 
 
 def to_lines(block):
@@ -237,7 +251,7 @@
     def kernel(*refs):
         parts = refs[:parts_n]
         (w, gf, gl, vel, cy, ny, gfy, gly, aly, gay, invy, cz, nz,
-         dz, ends, slots, flux, src, sol, turned) = refs[parts_n:]
+         dz, keep, give, slots, flux, src, sol, turned, ends) = refs[parts_n:]
         rows, depth, width = w.shape
         me = lax.axis_index("gx")
         for k in range(parts_n):
@@ -287,16 +301,20 @@
         d, u = block_solve(lambda i: turned[i], depth, cz, nz, dz)
         ends[0] = d
         ends[1] = u
+        split_rows(ends, keep, give)
 
     return kernel
 
 
 def chip_factor_kernel(own, mate, near, far, pair, cross, pair_c, chip_c):
-    is_low = lax.rem(lax.axis_index("gz"), 2) == 0
+    half = own.shape[1]
+    upper = lax.rem(lax.axis_index("gz"), 2)
+    at = pl.ds(pl.multiple_of(upper * half, half), half)
+    is_low = upper == 0
     low = [jnp.where(is_low, own[k], mate[k]) for k in range(3)]
     high = [jnp.where(is_low, mate[k], own[k]) for k in range(3)]
-    mid_reach = 1.0 / (HALF_Z * (near[1] + pair[1]))
-    end_reach = 1.0 / (HALF_Z * (far[1] + cross[1]))
+    mid_reach = 1.0 / (HALF_Z * (near[1, at] + pair[1, at]))
+    end_reach = 1.0 / (HALF_Z * (far[1, at] + cross[1, at]))
     weight = 1.0 / (mid_reach + low[2] + high[0])
     pair_c[0] = weight
     pair_c[1] = low[1]
@@ -306,63 +324,75 @@
     chip_c[2] = high[2] - weight * high[1] * high[1] + jnp.where(is_low, 0.0, end_reach)
 
 
-def pair_kernel(own, mate, pair_c, chip_ends, jump_out):
+def pair_kernel(own, mate, pair_c, chip_c, payload, jump_out):
     is_low = lax.rem(lax.axis_index("gz"), 2) == 0
     low_last = jnp.where(is_low, own[1], mate[1])
     high_first = jnp.where(is_low, mate[0], own[0])
     jump = high_first - low_last
     q_mid = pair_c[0] * jump
     jump_out[...] = jump
-    chip_ends[0] = jnp.where(is_low, own[0], mate[0]) + pair_c[1] * q_mid
-    chip_ends[1] = jnp.where(is_low, mate[1], own[1]) - pair_c[2] * q_mid
-
-
-def make_final_kernel(chips):
+    payload[0] = jnp.where(is_low, own[0], mate[0]) + pair_c[1] * q_mid
+    payload[1] = jnp.where(is_low, mate[1], own[1]) - pair_c[2] * q_mid
+    for k in range(3):
+        payload[2 + k] = chip_c[k]
+
+
+def make_flux_kernel(chips):
     def kernel(*refs):
-        coefs, ends = refs[:chips], refs[chips:2 * chips]
-        pair_c, jump, dz, gf, gl, out, c_at, d_at, flux, buf, sems = refs[2 * chips:]
-        depth, rows, width = dz.shape
-        parts = buf.shape[0]
-        group = rows // parts
+        parts = refs[:chips]
+        pair_c, jump, mine, theirs, slots, flux = refs[chips:]
         chip = lax.div(lax.axis_index("gz"), 2)
         is_low = lax.rem(lax.axis_index("gz"), 2) == 0
         for k in range(chips):
-            c_at[jnp.bitwise_xor(chip, k)] = coefs[k][...]
-            d_at[jnp.bitwise_xor(chip, k)] = ends[k][...]
-        zero = jnp.zeros((group, width), F32)
-        copies = []
-        for p in range(parts):
-            at = slice(p * group, (p + 1) * group)
-            flux[0] = zero
-            flux[chips] = zero
-            lower, right = [], None
-            for f in range(chips - 1):
-                pivot = c_at[f, 2, at] + c_at[f + 1, 0, at]
-                source = d_at[f + 1, 0, at] - d_at[f, 1, at]
-                if f:
-                    pivot = pivot - c_at[f, 1, at] * lower[-1]
-                    source = source + lower[-1] * right
-                r = 1.0 / pivot
-                lower.append(c_at[f + 1, 1, at] * r)
-                right = source
-                flux[f + 1] = source * r
-            q = flux[chips - 1]
-            for f in reversed(range(chips - 2)):
-                q = flux[f + 1] + lower[f] * q
-                flux[f + 1] = q
-            left, right = flux[chip], flux[chip + 1]
-            mid = pair_c[0, at] * (jump[at] + right * pair_c[2, at] + left * pair_c[1, at])
-            q_left = jnp.where(is_low, left, mid)
-            q_right = jnp.where(is_low, mid, right)
-            d = dz[:, at] + q_right * gl[:, at] - q_left * gf[:, at]
-            buf[p] = jnp.transpose(d, (1, 0, 2))
-            copy = pltpu.make_async_copy(buf.at[p], out.at[pl.ds(p * group, group)], sems.at[p])
-            copy.start()
-            copies.append(copy)
-        for copy in copies:
-            copy.wait()
+            slots[jnp.bitwise_xor(chip, k)] = parts[k][...]
+        flux[0] = jnp.zeros_like(jump)
+        flux[chips] = jnp.zeros_like(jump)
+        lower, right = [], None
+        for f in range(chips - 1):
+            pivot = slots[f, 4] + slots[f + 1, 2]
+            source = slots[f + 1, 0] - slots[f, 1]
+            if f:
+                pivot = pivot - slots[f, 3] * lower[-1]
+                source = source + lower[-1] * right
+            r = 1.0 / pivot
+            lower.append(slots[f + 1, 3] * r)
+            right = source
+            flux[f + 1] = source * r
+        q = flux[chips - 1]
+        for f in reversed(range(chips - 2)):
+            q = flux[f + 1] + lower[f] * q
+            flux[f + 1] = q
+        left, right = flux[chip], flux[chip + 1]
+        mid = pair_c[0] * (jump[...] + right * pair_c[2] + left * pair_c[1])
+        mine[0] = jnp.where(is_low, left, mid)
+        mine[1] = jnp.where(is_low, mid, right)
+        theirs[0] = jnp.where(is_low, mid, left)
+        theirs[1] = jnp.where(is_low, right, mid)
 
     return kernel
+
+
+def final_kernel(mine, got, dz, gf, gl, out, buf, sems):
+    depth, rows, width = dz.shape
+    parts = buf.shape[0]
+    group = rows // parts
+    half = rows // 2
+    is_low = lax.rem(lax.axis_index("gz"), 2) == 0
+    copies = []
+    for p in range(parts):
+        at = slice(p * group, (p + 1) * group)
+        top = p * group < half
+        inside = slice(p * group % half, p * group % half + group)
+        own_rows = is_low if top else jnp.logical_not(is_low)
+        q_left = jnp.where(own_rows, mine[0, inside], got[0, inside])
+        q_right = jnp.where(own_rows, mine[1, inside], got[1, inside])
+        d = dz[:, at] + q_right * gl[:, at] - q_left * gf[:, at]
+        buf[p] = jnp.transpose(d, (1, 0, 2))
+        copy = pltpu.make_async_copy(buf.at[p], out.at[pl.ds(p * group, group)], sems.at[p])
+        copy.start()
+        copies.append(copy)
+    for copy in copies:
+        copy.wait()
 
 
 def local(velocity, viscosity, force):
@@ -383,17 +413,21 @@
     def to_chip(k):
         return [(i, i ^ (2 * k)) for i in range(nz)]
 
-    visc, vel = viscosity, velocity
-    visc_z, near, far = call(
-        turn_kernel, [zmajor, (2,) + slab, (2,) + slab], [VMEM, VMEM],
-        [pltpu.VMEM(zmajor, F32)], size, 6 * size,
-    )(visc, vel)
+    pieces = 4
+    visc, vel, visc_z, near, far = call(
+        turn_kernel, [volume, volume, zmajor, (2,) + slab, (2,) + slab], [HBM, HBM],
+        [pltpu.VMEM(zmajor, F32), pltpu.SemaphoreType.DMA((2, pieces))], size, 6 * size,
+    )(
+        pltpu.with_memory_space_constraint(viscosity, pltpu.HBM),
+        pltpu.with_memory_space_constraint(velocity, pltpu.HBM),
+    )
     pair = lax.ppermute(near, "gz", pair_route)
     cross = lax.ppermute(far, "gz", cross_route)
 
-    c_z, n_z, gf_z, gl_z, planes = call(
-        z_factor_kernel, [zmajor] * 4 + [(3,) + slab], [VMEM],
-        [pltpu.VMEM(zmajor, F32)] * 2, 20 * size, 5 * size,
+    half = (rows // 2, width)
+    c_z, n_z, gf_z, gl_z, planes, give_c = call(
+        z_factor_kernel, [zmajor] * 4 + [(3,) + half] * 2, [VMEM],
+        [pltpu.VMEM(zmajor, F32)] * 2 + [pltpu.VMEM((3,) + slab, F32)], 20 * size, 5 * size,
     )(visc_z)
     c_x, n_x, gf_x, gl_x, coef, rhs0 = call(
         x_factor_kernel, [volume] * 4 + [(5,) + plane, volume], [VMEM, VMEM, HBM],
@@ -404,44 +438,41 @@
         [pltpu.VMEM(lines, F32)] * 3, 30 * size, 6 * size,
     )(visc)
 
-    mate_c = lax.ppermute(planes, "gz", pair_route)
+    mate_c = lax.ppermute(give_c, "gz", pair_route)
 
     w, payload = call(
         x_solve_kernel, [volume, (7,) + plane], [VMEM] * 10,
         [pltpu.VMEM(slab, F32)] * 2, 20 * size, 6 * size,
     )(visc, vel, rhs0, c_x, n_x, coef, near, far, pair, cross)
     pair_c, chip_c = call(
-        chip_factor_kernel, [(3,) + slab] * 2, [VMEM] * 6, (), size, size
+        chip_factor_kernel, [(3,) + half] * 2, [VMEM] * 6, (), size, size
     )(planes, mate_c, near, far, pair, cross)
-    payload, chip_c = lax.optimization_barrier((payload, chip_c))
     parts = [payload] + [
         lax.ppermute(payload, "gx", [(i, i ^ k) for i in range(nx)]) for k in range(1, nx)
     ]
-    coefs = [chip_c] + [lax.ppermute(chip_c, "gz", to_chip(k)) for k in range(1, chips)]
-
-    w, *coefs = lax.optimization_barrier((w, *coefs))
-    dz, ends = call(
-        make_middle_kernel(nx), [zmajor, (2,) + slab], [VMEM] * (nx + 13),
+    dz, keep, give = call(
+        make_middle_kernel(nx), [zmajor, (2,) + half, (2,) + half], [VMEM] * (nx + 13),
         [pltpu.VMEM((nx, 7) + plane, F32), pltpu.VMEM((nx + 1,) + plane, F32),
-         pltpu.VMEM(lines, F32), pltpu.VMEM(lines, F32), pltpu.VMEM(zmajor, F32)],
+         pltpu.VMEM(lines, F32), pltpu.VMEM(lines, F32), pltpu.VMEM(zmajor, F32),
+         pltpu.VMEM((2,) + slab, F32)],
         60 * size, 14 * size,
     )(*parts, w, gf_x, gl_x, vel, c_y, n_y, gf_y, gl_y, al_y, ga_y, inv_y, c_z, n_z)
 
-    mate = lax.ppermute(ends, "gz", pair_route)
-    chip_ends, jump = call(pair_kernel, [(2,) + slab, slab], [VMEM] * 3, (), size, size)(
-        ends, mate, pair_c
+    mate = lax.ppermute(give, "gz", pair_route)
+    chip_ends, jump = call(pair_kernel, [(5,) + half, half], [VMEM] * 4, (), size, size)(
+        keep, mate, pair_c, chip_c
     )
     others = [chip_ends] + [lax.ppermute(chip_ends, "gz", to_chip(k)) for k in range(1, chips)]
-    parts_out = 4
-    group = (rows // parts_out, width)
+    mine, theirs = call(
+        make_flux_kernel(chips), [(2,) + half] * 2, [VMEM] * (chips + 2),
+        [pltpu.VMEM((chips, 5) + half, F32), pltpu.VMEM((chips + 1,) + half, F32)], size, size,
+    )(*others, pair_c, jump)
+    got = lax.ppermute(theirs, "gz", pair_route)
     return call(
-        make_final_kernel(chips), [volume], [VMEM] * (2 * chips + 5),
-        [pltpu.VMEM((chips, 3) + slab, F32), pltpu.VMEM((chips, 2) + slab, F32),
-         pltpu.VMEM((chips + 1,) + group, F32),
-         pltpu.VMEM((parts_out, rows // parts_out, depth, width), F32),
-         pltpu.SemaphoreType.DMA((parts_out,))],
-        8 * size, 5 * size, [HBM],
-    )(*coefs, *others, pair_c, jump, dz, gf_z, gl_z)[0]
+        final_kernel, [volume], [VMEM] * 5,
+        [pltpu.VMEM((4, rows // 4, depth, width), F32), pltpu.SemaphoreType.DMA((4,))],
+        4 * size, 4 * size, [HBM],
+    )(mine, got, dz, gf_z, gl_z)[0]
 
 
 def solution(mesh):

time: 39.6 us -> 37.1 us (0.937)
  starting transfers between devices: 17.6 us -> 20.9 us
  waiting for transfers between devices: 12.5 us -> 9.85 us
  local copies, waits for them, and re-layouts: 2.1 us -> 0.01 us
  Pallas kernels: 7.08 us -> 6.1 us
    ppermute x5 -> x3, waiting for transfers between devices: 5.35 us -> 2.09 us  [the longest x1 1.24 us: local(): got = lax.ppermute(theirs, 'gz', pair_route)]
    unnamed x10 -> x2, local copies, waits for them, and re-layouts: 2.1 us -> 0.01 us
    pallas_call x1, Pallas kernels: 3.56 us -> 1.52 us  [local(): call(x_factor_kernel, [volume] * 4 + [(5,) + plane, volume], [VMEM, VMEM,...]
    ppermute x3, starting transfers between devices: 3.55 us -> 5.25 us  [local(): lax.ppermute(chip_ends, 'gz', to_chip(k))]
    ppermute x3, waiting for transfers between devices: 6.33 us -> 7.74 us  [local(): lax.ppermute(chip_ends, 'gz', to_chip(k))]
    pallas_call x6 -> x7, Pallas kernels: 2.63 us -> 3.73 us  [the longest x1 1.46 us: local(): call(turn_kernel, [volume, volume, zmajor, (2,) + slab, (2,) + slab], [HB...]
    ppermute x3, waiting for transfers between devices: 0.78 us -> 0.01 us  [local(): lax.ppermute(payload, 'gx', [(i, i ^ k) for i in range(nx)])]
    ppermute x5 -> x3, starting transfers between devices: 8.45 us -> 9.21 us  [the longest x1 5.43 us: local(): mate_c = lax.ppermute(give_c, 'gz', pair_route)]
  transfers between devices with their start and end apart: 13 -> 11, of which waited for: 6 -> 5; matrix products, arithmetic and copies ran while one was open for 0% -> 0% of each run, Pallas kernels for 11% -> 9%
where the time goes in v3:
time: 37.1 us; the launch traced here: 37 us
  starting transfers between devices  20.9 us (56%)
  waiting for transfers between devices  9.85 us (27%)
  Pallas kernels  6.1 us (16%)
    ppermute x3, waiting for transfers between devices, local(): lax.ppermute(chip_ends, 'gz', to_chip(k))  7.74 us
    ppermute x1, starting transfers between devices, local(): mate_c = lax.ppermute(give_c, 'gz', pair_route)  5.43 us
    ppermute x3, starting transfers between devices, local(): lax.ppermute(payload, 'gx', [(i, i ^ k) for i in range(nx)])  5.25 us
    ppermute x3, starting transfers between devices, local(): lax.ppermute(chip_ends, 'gz', to_chip(k))  5.25 us
    ppermute x1, starting transfers between devices, local(): mate = lax.ppermute(give, 'gz', pair_route)  3.71 us
    pallas_call x1, Pallas kernels, local(): call(x_factor_kernel, [volume] * 4 + [(5,) + plane, volume], [VMEM, VMEM,...  1.52 us
    pallas_call x1, Pallas kernels, local(): call(turn_kernel, [volume, volume, zmajor, (2,) + slab, (2,) + slab], [HB...  1.46 us
    ppermute x1, waiting for transfers between devices, local(): got = lax.ppermute(theirs, 'gz', pair_route)  1.24 us
  transfers between devices with their start and end apart: 11, of which 5 were waited for; matrix products, arithmetic and copies ran while one was open for 0% of the time, Pallas kernels for 9%

profile of v3, /device:TPU:0, one launch (start us, length us, event | category | flops | bytes accessed | tf_op | source)
XLA Modules:
  0.0 37.0 jit_solution(9414363088808849553)
XLA Ops:
  0.0 0.0 copy-start
  0.0 1.5 %shard_map.37 = (f32[64,8,256]{2,1,0:T(8,128)S(1)}, f32[64,8,256]{2,1,0:T(8,128)S(1)}, f32[8,64,256]{2,1,0:T(8,128)S(1)}, f32[2,64,256]{2,1,0:T(8,128)S(1)}, f32[2,64,256]{2,1,0:T(8,128)S(1)}) custom-call(f32[64,8,256]{2,1,0:T(8,128)} %visc_hbm.1, f32[64,8,256]{2,1,0:T(8,128)} %vel_hbm.1), custom_call_target="tpu_custom_call" | custom-call | flops 131072 | bytes 3145728 | tf_op jit(solution)/shard_map/pallas_call | solution.py:417
  1.5 0.5 %collective-permute-start = (f32[2,64,256]{2,1,0:T(8,128)S(1)}, f32[2,64,256]{2,1,0:T(8,128)S(1)}, u32[]{:S(2)}, u32[]{:S(2)}) collective-permute-start(f32[2,64,256]{2,1,0:T(8,128)S(1)} %get-tuple-element.46.near), channel_id=1, source_target_pairs={{0,1},{1,0},{2,3},{3,2},{4,5},{5,4},{6,7},{7,6},{8,9},{9,8},{10,11... | collective-permute-start | bytes 393224 | tf_op jit(solution)/shard_map/ppermute | solution.py:424
  2.0 0.7 %collective-permute-start.1 = (f32[2,64,256]{2,1,0:T(8,128)S(1)}, f32[2,64,256]{2,1,0:T(8,128)S(1)}, u32[]{:S(2)}, u32[]{:S(2)}) collective-permute-start(f32[2,64,256]{2,1,0:T(8,128)S(1)} %get-tuple-element.47.far), channel_id=1, source_target_pairs={{1,2},{2,1},{3,4},{4,3},{5,6},{6,5},{9,10},{10,9},{11,12},{12,11},... | collective-permute-start | bytes 393224 | tf_op jit(solution)/shard_map/ppermute | solution.py:425
  2.7 0.0 copy-done
  2.7 1.5 %shard_map.38 = (f32[64,8,256]{2,1,0:T(8,128)S(1)}, f32[64,8,256]{2,1,0:T(8,128)S(1)}, f32[64,8,256]{2,1,0:T(8,128)S(1)}, f32[64,8,256]{2,1,0:T(8,128)S(1)}, f32...) custom-call(f32[64,8,256]{2,1,0:T(8,128)S(1)} %get-tuple-element.40.visc, ...), custom_call_target="tpu_custom_call" | custom-call | flops 7864320 | bytes 4718592 | tf_op jit(solution)/shard_map/pallas_call | solution.py:432
  4.2 0.0 collective-permute-done.pair
  4.2 0.0 collective-permute-done.1.cross
  4.2 0.2 shard_map.39
  4.4 2.7 %collective-permute-start.2 = (f32[7,8,256]{2,1,0:T(8,128)S(1)}, f32[7,8,256]{2,1,0:T(8,128)S(1)}, u32[]{:S(2)}, u32[]{:S(2)}) collective-permute-start(f32[7,8,256]{2,1,0:T(8,128)S(1)} %get-tuple-element.48.refs_0_), channel_id=1, source_target_pairs={{0,8},{8,0},{16,24},{24,16},{1,9},{9,1},{17,25},{25,17},{2,10},{10... | collective-permute-start | bytes 172040 | tf_op jit(solution)/shard_map/ppermute | solution.py:451
  7.1 2.6 %collective-permute-start.3 = (f32[7,8,256]{2,1,0:T(8,128)S(1)}, f32[7,8,256]{2,1,0:T(8,128)S(1)}, u32[]{:S(2)}, u32[]{:S(2)}) collective-permute-start(f32[7,8,256]{2,1,0:T(8,128)S(1)} %get-tuple-element.48.refs_0_), channel_id=1, source_target_pairs={{0,16},{8,24},{16,0},{24,8},{1,17},{9,25},{17,1},{25,9},{2,18},{10... | collective-permute-start | bytes 172040 | tf_op jit(solution)/shard_map/ppermute | solution.py:451
  9.7 0.0 collective-permute-start.4
  9.7 0.4 %shard_map.41 = (f32[8,64,256]{2,1,0:T(8,128)S(1)}, f32[8,64,256]{2,1,0:T(8,128)S(1)}, f32[8,64,256]{2,1,0:T(8,128)S(1)}, f32[8,64,256]{2,1,0:T(8,128)S(1)}, f32...) custom-call(f32[8,64,256]{2,1,0:T(8,128)S(1)} %get-tuple-element.59.visc_z), custom_call_target="tpu_custom_call" | custom-call | flops 2621440 | bytes 2621440 | tf_op jit(solution)/shard_map/pallas_call | solution.py:428
  10.1 5.4 %collective-permute-start.6 = (f32[3,32,256]{2,1,0:T(8,128)S(1)}, f32[3,32,256]{2,1,0:T(8,128)S(1)}, u32[]{:S(2)}, u32[]{:S(2)}) collective-permute-start(f32[3,32,256]{2,1,0:T(8,128)S(1)} %get-tuple-element.65), channel_id=1, source_target_pairs={{0,1},{1,0},{2,3},{3,2},{4,5},{5,4},{6,7},{7,6},{8,9},{9,8},{10,11... | collective-permute-start | bytes 294920 | tf_op jit(solution)/shard_map/ppermute | solution.py:441
  15.6 0.6 %shard_map.40 = (f32[32,8,512]{2,1,0:T(8,128)S(1)}, f32[32,8,512]{2,1,0:T(8,128)S(1)}, f32[32,8,512]{2,1,0:T(8,128)S(1)}, f32[32,8,512]{2,1,0:T(8,128)S(1)}, f32...) custom-call(f32[64,8,256]{2,1,0:T(8,128)S(1)} %get-tuple-element.40.visc), custom_call_target="tpu_custom_call" | custom-call | flops 3932160 | bytes 3145728 | tf_op jit(solution)/shard_map/pallas_call | solution.py:436
  16.2 0.0 collective-permute-done.2.refs_1_
  16.2 0.0 collective-permute-done.3.refs_2_
  16.2 0.0 collective-permute-done.4.refs_3_
  16.2 0.8 %shard_map.42 = (f32[8,64,256]{2,1,0:T(8,128)S(1)}, f32[2,32,256]{2,1,0:T(8,128)S(1)}, f32[2,32,256]{2,1,0:T(8,128)S(1)}) custom-call(f32[7,8,256]{2,1,0:T(8,128)S(1)} %get-tuple-element.48.refs_0_, f32[7,8,256]{2,1,0:T(8,128)S(1)} %collective-permute-done.2.refs_1_, f32[7,8,256]{2,1,0:T(8,128)S(1)} %collective-permute-done.3.refs_2_, ...), custom_call_target="tpu_custom_call" | custom-call | flops 7864320 | bytes 7340032 | tf_op jit(solution)/shard_map/pallas_call | solution.py:453
  17.0 3.7 %collective-permute-start.5 = (f32[2,32,256]{2,1,0:T(8,128)S(1)}, f32[2,32,256]{2,1,0:T(8,128)S(1)}, u32[]{:S(2)}, u32[]{:S(2)}) collective-permute-start(f32[2,32,256]{2,1,0:T(8,128)S(1)} %get-tuple-element.63), channel_id=1, source_target_pairs={{0,1},{1,0},{2,3},{3,2},{4,5},{5,4},{6,7},{7,6},{8,9},{9,8},{10,11... | collective-permute-start | bytes 196616 | tf_op jit(solution)/shard_map/ppermute | solution.py:461
  20.7 0.0 collective-permute-done.6.mate
  20.8 0.8 %collective-permute-done.5.mate = f32[2,32,256]{2,1,0:T(8,128)S(1)} collective-permute-done((f32[2,32,256]{2,1,0:T(8,128)S(1)}, f32[2,32,256]{2,1,0:T(8,128)S(1)}, u32[]{:S(2)}, u32[]{:S(2)}) %collective-permute-start.5) | collective-permute-done | bytes 65568 | tf_op jit(solution)/shard_map/ppermute | solution.py:461
  21.7 1.9 %collective-permute-start.7 = (f32[5,32,256]{2,1,0:T(8,128)S(1)}, f32[5,32,256]{2,1,0:T(8,128)S(1)}, u32[]{:S(2)}, u32[]{:S(2)}) collective-permute-start(f32[5,32,256]{2,1,0:T(8,128)S(1)} %get-tuple-element.68.refs_0_), channel_id=1, source_target_pairs={{0,2},{1,3},{2,0},{3,1},{4,6},{5,7},{6,4},{7,5},{8,10},{9,11},{10,... | collective-permute-start | bytes 491528 | tf_op jit(solution)/shard_map/ppermute | solution.py:465
  23.6 2.2 %collective-permute-start.8 = (f32[5,32,256]{2,1,0:T(8,128)S(1)}, f32[5,32,256]{2,1,0:T(8,128)S(1)}, u32[]{:S(2)}, u32[]{:S(2)}) collective-permute-start(f32[5,32,256]{2,1,0:T(8,128)S(1)} %get-tuple-element.68.refs_0_), channel_id=1, source_target_pairs={{0,4},{1,5},{2,6},{3,7},{4,0},{5,1},{6,2},{7,3},{8,12},{9,13},{10,... | collective-permute-start | bytes 491528 | tf_op jit(solution)/shard_map/ppermute | solution.py:465
  25.8 1.1 %collective-permute-start.9 = (f32[5,32,256]{2,1,0:T(8,128)S(1)}, f32[5,32,256]{2,1,0:T(8,128)S(1)}, u32[]{:S(2)}, u32[]{:S(2)}) collective-permute-start(f32[5,32,256]{2,1,0:T(8,128)S(1)} %get-tuple-element.68.refs_0_), channel_id=1, source_target_pairs={{0,6},{1,7},{2,4},{3,5},{4,2},{5,3},{6,0},{7,1},{8,14},{9,15},{10,... | collective-permute-start | bytes 491528 | tf_op jit(solution)/shard_map/ppermute | solution.py:465
  26.9 1.7 %collective-permute-done.7.refs_1_ = f32[5,32,256]{2,1,0:T(8,128)S(1)} collective-permute-done((f32[5,32,256]{2,1,0:T(8,128)S(1)}, f32[5,32,256]{2,1,0:T(8,128)S(1)}, u32[]{:S(2)}, u32[]{:S(2)}) %collective-permute-start.7) | collective-permute-done | bytes 163872 | tf_op jit(solution)/shard_map/ppermute | solution.py:465
  28.6 4.2 %collective-permute-done.8.refs_2_ = f32[5,32,256]{2,1,0:T(8,128)S(1)} collective-permute-done((f32[5,32,256]{2,1,0:T(8,128)S(1)}, f32[5,32,256]{2,1,0:T(8,128)S(1)}, u32[]{:S(2)}, u32[]{:S(2)}) %collective-permute-start.8) | collective-permute-done | bytes 163872 | tf_op jit(solution)/shard_map/ppermute | solution.py:465
  32.8 1.8 %collective-permute-done.9.refs_3_ = f32[5,32,256]{2,1,0:T(8,128)S(1)} collective-permute-done((f32[5,32,256]{2,1,0:T(8,128)S(1)}, f32[5,32,256]{2,1,0:T(8,128)S(1)}, u32[]{:S(2)}, u32[]{:S(2)}) %collective-permute-start.9) | collective-permute-done | bytes 163872 | tf_op jit(solution)/shard_map/ppermute | solution.py:465
  34.6 0.1 shard_map.45
  34.8 0.1 collective-permute-start.10
  34.8 1.2 %collective-permute-done.10.got = f32[2,32,256]{2,1,0:T(8,128)S(1)} collective-permute-done((f32[2,32,256]{2,1,0:T(8,128)S(1)}, f32[2,32,256]{2,1,0:T(8,128)S(1)}, u32[]{:S(2)}, u32[]{:S(2)}) %collective-permute-start.10) | collective-permute-done | bytes 65568 | tf_op jit(solution)/shard_map/ppermute | solution.py:470
  36.1 0.9 %shard_map.46 = f32[64,8,256]{2,1,0:T(8,128)} custom-call(f32[2,32,256]{2,1,0:T(8,128)S(1)} %get-tuple-element.70.mine, f32[2,32,256]{2,1,0:T(8,128)S(1)} %collective-permute-done.10.got, f32[8,64,256]{2,1,0:T(8,128)S(1)} %get-tuple-element.72.dz, f32[8,64,256]{2,1,0:T(8,128)S(1)} %get-tuple-element.73.gf, f32[8,64,256]{2,1,0:T(8,128)S(1)} %get-tuple-element.74.gl), custom_call_target="tpu_custom_call" | custom-call | flops 524288 | bytes 2097152 | tf_op jit(solution)/shard_map/pallas_call | solution.py:471
  (2 shorter events, 0.1 us)
Async XLA Ops:
  0.0 2.7 %copy-start = (f32[64,8,256]{2,1,0:T(8,128)S(1)}, f32[64,8,256]{2,1,0:T(8,128)}, u32[]{:S(2)}) copy-start(f32[64,8,256]{2,1,0:T(8,128)} %force_hbm.1) | copy-start | bytes 1572868
  1.5 2.7 %collective-permute-start = (f32[2,64,256]{2,1,0:T(8,128)S(1)}, f32[2,64,256]{2,1,0:T(8,128)S(1)}, u32[]{:S(2)}, u32[]{:S(2)}) collective-permute-start(f32[2,64,256]{2,1,0:T(8,128)S(1)} %get-tuple-element.46.near), channel_id=1, source_target_pairs={{0,1},{1,0},{2,3},{3,2},{4,5},{5,4},{6,7},{7,6},{8,9},{9,8},{10,11... | collective-permute-start | bytes 393224 | tf_op jit(solution)/shard_map/ppermute | solution.py:424
  2.0 2.2 %collective-permute-start.1 = (f32[2,64,256]{2,1,0:T(8,128)S(1)}, f32[2,64,256]{2,1,0:T(8,128)S(1)}, u32[]{:S(2)}, u32[]{:S(2)}) collective-permute-start(f32[2,64,256]{2,1,0:T(8,128)S(1)} %get-tuple-element.47.far), channel_id=1, source_target_pairs={{1,2},{2,1},{3,4},{4,3},{5,6},{6,5},{9,10},{10,9},{11,12},{12,11},... | collective-permute-start | bytes 393224 | tf_op jit(solution)/shard_map/ppermute | solution.py:425
  4.4 11.8 %collective-permute-start.2 = (f32[7,8,256]{2,1,0:T(8,128)S(1)}, f32[7,8,256]{2,1,0:T(8,128)S(1)}, u32[]{:S(2)}, u32[]{:S(2)}) collective-permute-start(f32[7,8,256]{2,1,0:T(8,128)S(1)} %get-tuple-element.48.refs_0_), channel_id=1, source_target_pairs={{0,8},{8,0},{16,24},{24,16},{1,9},{9,1},{17,25},{25,17},{2,10},{10... | collective-permute-start | bytes 172040 | tf_op jit(solution)/shard_map/ppermute | solution.py:451
  7.1 9.1 %collective-permute-start.3 = (f32[7,8,256]{2,1,0:T(8,128)S(1)}, f32[7,8,256]{2,1,0:T(8,128)S(1)}, u32[]{:S(2)}, u32[]{:S(2)}) collective-permute-start(f32[7,8,256]{2,1,0:T(8,128)S(1)} %get-tuple-element.48.refs_0_), channel_id=1, source_target_pairs={{0,16},{8,24},{16,0},{24,8},{1,17},{9,25},{17,1},{25,9},{2,18},{10... | collective-permute-start | bytes 172040 | tf_op jit(solution)/shard_map/ppermute | solution.py:451
  9.7 6.5 %collective-permute-start.4 = (f32[7,8,256]{2,1,0:T(8,128)S(1)}, f32[7,8,256]{2,1,0:T(8,128)S(1)}, u32[]{:S(2)}, u32[]{:S(2)}) collective-permute-start(f32[7,8,256]{2,1,0:T(8,128)S(1)} %get-tuple-element.48.refs_0_), channel_id=1, source_target_pairs={{0,24},{8,16},{16,8},{24,0},{1,25},{9,17},{17,9},{25,1},{2,26},{10... | collective-permute-start | bytes 172040 | tf_op jit(solution)/shard_map/ppermute | solution.py:451
  10.1 10.6 %collective-permute-start.6 = (f32[3,32,256]{2,1,0:T(8,128)S(1)}, f32[3,32,256]{2,1,0:T(8,128)S(1)}, u32[]{:S(2)}, u32[]{:S(2)}) collective-permute-start(f32[3,32,256]{2,1,0:T(8,128)S(1)} %get-tuple-element.65), channel_id=1, source_target_pairs={{0,1},{1,0},{2,3},{3,2},{4,5},{5,4},{6,7},{7,6},{8,9},{9,8},{10,11... | collective-permute-start | bytes 294920 | tf_op jit(solution)/shard_map/ppermute | solution.py:441
  17.0 4.6 %collective-permute-start.5 = (f32[2,32,256]{2,1,0:T(8,128)S(1)}, f32[2,32,256]{2,1,0:T(8,128)S(1)}, u32[]{:S(2)}, u32[]{:S(2)}) collective-permute-start(f32[2,32,256]{2,1,0:T(8,128)S(1)} %get-tuple-element.63), channel_id=1, source_target_pairs={{0,1},{1,0},{2,3},{3,2},{4,5},{5,4},{6,7},{7,6},{8,9},{9,8},{10,11... | collective-permute-start | bytes 196616 | tf_op jit(solution)/shard_map/ppermute | solution.py:461
  21.7 7.0 %collective-permute-start.7 = (f32[5,32,256]{2,1,0:T(8,128)S(1)}, f32[5,32,256]{2,1,0:T(8,128)S(1)}, u32[]{:S(2)}, u32[]{:S(2)}) collective-permute-start(f32[5,32,256]{2,1,0:T(8,128)S(1)} %get-tuple-element.68.refs_0_), channel_id=1, source_target_pairs={{0,2},{1,3},{2,0},{3,1},{4,6},{5,7},{6,4},{7,5},{8,10},{9,11},{10,... | collective-permute-start | bytes 491528 | tf_op jit(solution)/shard_map/ppermute | solution.py:465
  23.6 9.2 %collective-permute-start.8 = (f32[5,32,256]{2,1,0:T(8,128)S(1)}, f32[5,32,256]{2,1,0:T(8,128)S(1)}, u32[]{:S(2)}, u32[]{:S(2)}) collective-permute-start(f32[5,32,256]{2,1,0:T(8,128)S(1)} %get-tuple-element.68.refs_0_), channel_id=1, source_target_pairs={{0,4},{1,5},{2,6},{3,7},{4,0},{5,1},{6,2},{7,3},{8,12},{9,13},{10,... | collective-permute-start | bytes 491528 | tf_op jit(solution)/shard_map/ppermute | solution.py:465
  25.8 8.9 %collective-permute-start.9 = (f32[5,32,256]{2,1,0:T(8,128)S(1)}, f32[5,32,256]{2,1,0:T(8,128)S(1)}, u32[]{:S(2)}, u32[]{:S(2)}) collective-permute-start(f32[5,32,256]{2,1,0:T(8,128)S(1)} %get-tuple-element.68.refs_0_), channel_id=1, source_target_pairs={{0,6},{1,7},{2,4},{3,5},{4,2},{5,3},{6,0},{7,1},{8,14},{9,15},{10,... | collective-permute-start | bytes 491528 | tf_op jit(solution)/shard_map/ppermute | solution.py:465
  34.8 1.3 %collective-permute-start.10 = (f32[2,32,256]{2,1,0:T(8,128)S(1)}, f32[2,32,256]{2,1,0:T(8,128)S(1)}, u32[]{:S(2)}, u32[]{:S(2)}) collective-permute-start(f32[2,32,256]{2,1,0:T(8,128)S(1)} %get-tuple-element.71), channel_id=1, source_target_pairs={{0,1},{1,0},{2,3},{3,2},{4,5},{5,4},{6,7},{7,6},{8,9},{9,8},{10,11... | collective-permute-start | bytes 196616 | tf_op jit(solution)/shard_map/ppermute | solution.py:470

commit v4 on v3

--- a/solution.py
+++ b/solution.py
@@ -104,32 +104,32 @@
     return d, u
 
 
-def turn_kernel(visc_hbm, vel_hbm, visc, vel, visc_z, near, far, vel_z, sems):
+def far_kernel(visc_hbm, vel_hbm, far, sems):
+    rows, depth, width = visc_hbm.shape
+    at = lax.rem(lax.axis_index("gz"), 2) * (depth - 1)
+    copies = [
+        pltpu.make_async_copy(src.at[:, at], far.at[k], sems.at[k])
+        for k, src in enumerate((vel_hbm, visc_hbm))
+    ]
+    for copy in copies:
+        copy.start()
+    for copy in copies:
+        copy.wait()
+
+
+def load_kernel(visc_hbm, vel_hbm, visc, vel, visc_z, near, vel_z, sems):
     rows, depth, width = visc.shape
-    upper = lax.rem(lax.axis_index("gz"), 2)
-    near_at = (1 - upper) * (depth - 1)
-    far_at = upper * (depth - 1)
-    pieces = sems.shape[1]
-    piece = rows // pieces
+    near_at = (1 - lax.rem(lax.axis_index("gz"), 2)) * (depth - 1)
     copies = [
-        [
-            pltpu.make_async_copy(
-                src.at[pl.ds(p * piece, piece)], dst.at[pl.ds(p * piece, piece)], sems.at[k, p]
-            )
-            for p in range(pieces)
-        ]
+        pltpu.make_async_copy(src, dst, sems.at[k])
         for k, (src, dst) in enumerate(((vel_hbm, vel), (visc_hbm, visc)))
     ]
-    for p in range(pieces):
-        for k in range(2):
-            copies[k][p].start()
-    for p in range(pieces):
-        at = slice(p * piece, (p + 1) * piece)
-        for k, (src, turned) in enumerate(((vel, vel_z), (visc, visc_z))):
-            copies[k][p].wait()
-            turned[:, at] = jnp.transpose(src[at], (1, 0, 2))
-            near[k, at] = turned[near_at, at]
-            far[k, at] = turned[far_at, at]
+    for copy in copies:
+        copy.start()
+    for k, (src, turned) in enumerate(((vel, vel_z), (visc, visc_z))):
+        copies[k].wait()
+        turned[...] = jnp.transpose(src[...], (1, 0, 2))
+        near[k] = turned[near_at]
 
 
 def x_factor_kernel(visc, vel, force_hbm, c, n, gf, gl, coef, rhs, cf, cb, force, sem):
@@ -225,13 +225,17 @@
     inv[...] = 1.0 / b
 
 
-def x_solve_kernel(visc, vel, rhs0, c, n, coef, near, far, pair, cross, w, payload, edge_lo, edge_hi):
+def outer_edge_kernel(far, cross, edge):
+    edge[...] = (2.0 * HALF_Z) * (far[1] + cross[1]) * (cross[0] - far[0])
+
+
+def x_solve_kernel(visc, vel, rhs0, c, n, coef, near, pair, by_cross_ref, w, payload, edge_lo, edge_hi):
     rows, depth, width = visc.shape
     sub = iota((depth, width), 0)
     upper = lax.rem(lax.axis_index("gz"), 2)
     two = 2.0 * HALF_Z
     by_pair = two * (near[1] + pair[1]) * (pair[0] - near[0])
-    by_cross = two * (far[1] + cross[1]) * (cross[0] - far[0])
+    by_cross = by_cross_ref[...]
     edge_lo[...] = jnp.where(upper == 0, by_cross, by_pair)
     edge_hi[...] = jnp.where(upper == 0, by_pair, by_cross)
 
@@ -413,14 +417,15 @@
     def to_chip(k):
         return [(i, i ^ (2 * k)) for i in range(nz)]
 
-    pieces = 4
-    visc, vel, visc_z, near, far = call(
-        turn_kernel, [volume, volume, zmajor, (2,) + slab, (2,) + slab], [HBM, HBM],
-        [pltpu.VMEM(zmajor, F32), pltpu.SemaphoreType.DMA((2, pieces))], size, 6 * size,
-    )(
-        pltpu.with_memory_space_constraint(viscosity, pltpu.HBM),
-        pltpu.with_memory_space_constraint(velocity, pltpu.HBM),
-    )
+    viscosity = pltpu.with_memory_space_constraint(viscosity, pltpu.HBM)
+    velocity = pltpu.with_memory_space_constraint(velocity, pltpu.HBM)
+    (far,) = call(
+        far_kernel, [(2,) + slab], [HBM, HBM], [pltpu.SemaphoreType.DMA((2,))], 0, size
+    )(viscosity, velocity)
+    visc, vel, visc_z, near = call(
+        load_kernel, [volume, volume, zmajor, (2,) + slab], [HBM, HBM],
+        [pltpu.VMEM(zmajor, F32), pltpu.SemaphoreType.DMA((2,))], size, 6 * size,
+    )(viscosity, velocity)
     pair = lax.ppermute(near, "gz", pair_route)
     cross = lax.ppermute(far, "gz", cross_route)
 
@@ -440,10 +445,11 @@
 
     mate_c = lax.ppermute(give_c, "gz", pair_route)
 
+    (outer_edge,) = call(outer_edge_kernel, [slab], [VMEM] * 2)(far, cross)
     w, payload = call(
-        x_solve_kernel, [volume, (7,) + plane], [VMEM] * 10,
+        x_solve_kernel, [volume, (7,) + plane], [VMEM] * 9,
         [pltpu.VMEM(slab, F32)] * 2, 20 * size, 6 * size,
-    )(visc, vel, rhs0, c_x, n_x, coef, near, far, pair, cross)
+    )(visc, vel, rhs0, c_x, n_x, coef, near, pair, outer_edge)
     pair_c, chip_c = call(
         chip_factor_kernel, [(3,) + half] * 2, [VMEM] * 6, (), size, size
     )(planes, mate_c, near, far, pair, cross)

time: 37.1 us -> 36.1 us (0.973)
  starting transfers between devices: 20.9 us -> 14.1 us
  waiting for transfers between devices: 9.85 us -> 14.8 us
  Pallas kernels: 6.1 us -> 6.99 us
    ppermute x1, starting transfers between devices: 5.43 us -> 0.07 us  [local(): mate_c = lax.ppermute(give_c, 'gz', pair_route)]
    ppermute x3, waiting for transfers between devices: 0.01 us -> 4.59 us  [local(): lax.ppermute(payload, 'gx', [(i, i ^ k) for i in range(nx)])]
    ppermute x1, starting transfers between devices: 0.52 us -> 4.32 us  [local(): pair = lax.ppermute(near, 'gz', pair_route)]
    ppermute x1, starting transfers between devices: 3.71 us -> 0.07 us  [local(): mate = lax.ppermute(give, 'gz', pair_route)]
    ppermute x3, starting transfers between devices: 5.25 us -> 4.27 us  [local(): lax.ppermute(chip_ends, 'gz', to_chip(k))]
    pallas_call x2 -> x4, Pallas kernels: 1.68 us -> 2.57 us  [the longest x1 1.38 us: local(): call(load_kernel, [volume, volume, zmajor, (2,) + slab], [HBM, HBM], [plt...]
    ppermute x3, starting transfers between devices: 5.25 us -> 4.45 us  [local(): lax.ppermute(payload, 'gx', [(i, i ^ k) for i in range(nx)])]
  transfers between devices with their start and end apart: 11 -> 11, of which waited for: 5 -> 7; matrix products, arithmetic and copies ran while one was open for 0% -> 0% of each run, Pallas kernels for 9% -> 13%
where the time goes in v4:
time: 36.1 us; the launch traced here: 35.9 us
  waiting for transfers between devices  14.8 us (41%)
  starting transfers between devices  14.1 us (39%)
  Pallas kernels  6.99 us (19%)
    ppermute x3, waiting for transfers between devices, local(): lax.ppermute(chip_ends, 'gz', to_chip(k))  7.74 us
    ppermute x3, waiting for transfers between devices, local(): lax.ppermute(payload, 'gx', [(i, i ^ k) for i in range(nx)])  4.59 us
    ppermute x3, starting transfers between devices, local(): lax.ppermute(payload, 'gx', [(i, i ^ k) for i in range(nx)])  4.45 us
    ppermute x1, starting transfers between devices, local(): pair = lax.ppermute(near, 'gz', pair_route)  4.32 us
    ppermute x3, starting transfers between devices, local(): lax.ppermute(chip_ends, 'gz', to_chip(k))  4.27 us
    pallas_call x1, Pallas kernels, local(): call(x_factor_kernel, [volume] * 4 + [(5,) + plane, volume], [VMEM, VMEM,...  1.51 us
    pallas_call x1, Pallas kernels, local(): call(load_kernel, [volume, volume, zmajor, (2,) + slab], [HBM, HBM], [plt...  1.38 us
    ppermute x1, waiting for transfers between devices, local(): got = lax.ppermute(theirs, 'gz', pair_route)  1.24 us
  transfers between devices with their start and end apart: 11, of which 7 were waited for; matrix products, arithmetic and copies ran while one was open for 0% of the time, Pallas kernels for 13%

profile of v4, /device:TPU:0, one launch (start us, length us, event | category | flops | bytes accessed | tf_op | source)
XLA Modules:
  0.0 35.9 jit_solution(121064208789018798)
XLA Ops:
  0.0 0.9 %shard_map.39.far = f32[2,64,256]{2,1,0:T(8,128)S(1)} custom-call(f32[64,8,256]{2,1,0:T(8,128)} %visc_hbm.3, f32[64,8,256]{2,1,0:T(8,128)} %vel_hbm.3), custom_call_target="tpu_custom_call" | custom-call | bytes 524288 | tf_op jit(solution)/shard_map/pallas_call | solution.py:422
  0.9 0.0 copy-start
  0.9 0.8 %collective-permute-start.1 = (f32[2,64,256]{2,1,0:T(8,128)S(1)}, f32[2,64,256]{2,1,0:T(8,128)S(1)}, u32[]{:S(2)}, u32[]{:S(2)}) collective-permute-start(f32[2,64,256]{2,1,0:T(8,128)S(1)} %shard_map.39.far), channel_id=1, source_target_pairs={{1,2},{2,1},{3,4},{4,3},{5,6},{6,5},{9,10},{10,9},{11,12},{12,11},... | collective-permute-start | bytes 393224 | tf_op jit(solution)/shard_map/ppermute | solution.py:430
  1.7 1.4 %shard_map.37 = (f32[64,8,256]{2,1,0:T(8,128)S(1)}, f32[64,8,256]{2,1,0:T(8,128)S(1)}, f32[8,64,256]{2,1,0:T(8,128)S(1)}, f32[2,64,256]{2,1,0:T(8,128)S(1)}) custom-call(f32[64,8,256]{2,1,0:T(8,128)} %visc_hbm.3, f32[64,8,256]{2,1,0:T(8,128)} %vel_hbm.3), custom_call_target="tpu_custom_call" | custom-call | flops 131072 | bytes 3145728 | tf_op jit(solution)/shard_map/pallas_call | solution.py:425
  3.1 4.3 %collective-permute-start = (f32[2,64,256]{2,1,0:T(8,128)S(1)}, f32[2,64,256]{2,1,0:T(8,128)S(1)}, u32[]{:S(2)}, u32[]{:S(2)}) collective-permute-start(f32[2,64,256]{2,1,0:T(8,128)S(1)} %get-tuple-element.45.near), channel_id=1, source_target_pairs={{0,1},{1,0},{2,3},{3,2},{4,5},{5,4},{6,7},{7,6},{8,9},{9,8},{10,11... | collective-permute-start | bytes 393224 | tf_op jit(solution)/shard_map/ppermute | solution.py:429
  7.4 0.0 copy-done
  7.4 1.5 %shard_map.38 = (f32[64,8,256]{2,1,0:T(8,128)S(1)}, f32[64,8,256]{2,1,0:T(8,128)S(1)}, f32[64,8,256]{2,1,0:T(8,128)S(1)}, f32[64,8,256]{2,1,0:T(8,128)S(1)}, f32...) custom-call(f32[64,8,256]{2,1,0:T(8,128)S(1)} %get-tuple-element.39.visc, ...), custom_call_target="tpu_custom_call" | custom-call | flops 7864320 | bytes 4718592 | tf_op jit(solution)/shard_map/pallas_call | solution.py:437
  9.0 0.0 collective-permute-done.1.cross
  9.0 0.0 collective-permute-done.pair
  9.0 0.3 shard_map.41
  9.3 1.6 %collective-permute-start.2 = (f32[7,8,256]{2,1,0:T(8,128)S(1)}, f32[7,8,256]{2,1,0:T(8,128)S(1)}, u32[]{:S(2)}, u32[]{:S(2)}) collective-permute-start(f32[7,8,256]{2,1,0:T(8,128)S(1)} %get-tuple-element.46.refs_0_), channel_id=1, source_target_pairs={{0,8},{8,0},{16,24},{24,16},{1,9},{9,1},{17,25},{25,17},{2,10},{10... | collective-permute-start | bytes 172040 | tf_op jit(solution)/shard_map/ppermute | solution.py:457
  10.9 2.6 %collective-permute-start.3 = (f32[7,8,256]{2,1,0:T(8,128)S(1)}, f32[7,8,256]{2,1,0:T(8,128)S(1)}, u32[]{:S(2)}, u32[]{:S(2)}) collective-permute-start(f32[7,8,256]{2,1,0:T(8,128)S(1)} %get-tuple-element.46.refs_0_), channel_id=1, source_target_pairs={{0,16},{8,24},{16,0},{24,8},{1,17},{9,25},{17,1},{25,9},{2,18},{10... | collective-permute-start | bytes 172040 | tf_op jit(solution)/shard_map/ppermute | solution.py:457
  13.5 0.2 collective-permute-start.4
  13.7 0.4 %shard_map.43 = (f32[8,64,256]{2,1,0:T(8,128)S(1)}, f32[8,64,256]{2,1,0:T(8,128)S(1)}, f32[8,64,256]{2,1,0:T(8,128)S(1)}, f32[8,64,256]{2,1,0:T(8,128)S(1)}, f32...) custom-call(f32[8,64,256]{2,1,0:T(8,128)S(1)} %get-tuple-element.57.visc_z), custom_call_target="tpu_custom_call" | custom-call | flops 2621440 | bytes 2621440 | tf_op jit(solution)/shard_map/pallas_call | solution.py:433
  14.2 0.1 collective-permute-start.6
  14.2 0.6 %shard_map.42 = (f32[32,8,512]{2,1,0:T(8,128)S(1)}, f32[32,8,512]{2,1,0:T(8,128)S(1)}, f32[32,8,512]{2,1,0:T(8,128)S(1)}, f32[32,8,512]{2,1,0:T(8,128)S(1)}, f32...) custom-call(f32[64,8,256]{2,1,0:T(8,128)S(1)} %get-tuple-element.39.visc), custom_call_target="tpu_custom_call" | custom-call | flops 3932160 | bytes 3145728 | tf_op jit(solution)/shard_map/pallas_call | solution.py:441
  14.9 0.0 collective-permute-done.2.refs_1_
  14.9 2.5 %collective-permute-done.3.refs_2_ = f32[7,8,256]{2,1,0:T(8,128)S(1)} collective-permute-done((f32[7,8,256]{2,1,0:T(8,128)S(1)}, f32[7,8,256]{2,1,0:T(8,128)S(1)}, u32[]{:S(2)}, u32[]{:S(2)}) %collective-permute-start.3) | collective-permute-done | bytes 57376 | tf_op jit(solution)/shard_map/ppermute | solution.py:457
  17.4 2.1 %collective-permute-done.4.refs_3_ = f32[7,8,256]{2,1,0:T(8,128)S(1)} collective-permute-done((f32[7,8,256]{2,1,0:T(8,128)S(1)}, f32[7,8,256]{2,1,0:T(8,128)S(1)}, u32[]{:S(2)}, u32[]{:S(2)}) %collective-permute-start.4) | collective-permute-done | bytes 57376 | tf_op jit(solution)/shard_map/ppermute | solution.py:457
  19.5 0.8 %shard_map.44 = (f32[8,64,256]{2,1,0:T(8,128)S(1)}, f32[2,32,256]{2,1,0:T(8,128)S(1)}, f32[2,32,256]{2,1,0:T(8,128)S(1)}) custom-call(f32[7,8,256]{2,1,0:T(8,128)S(1)} %get-tuple-element.46.refs_0_, f32[7,8,256]{2,1,0:T(8,128)S(1)} %collective-permute-done.2.refs_1_, f32[7,8,256]{2,1,0:T(8,128)S(1)} %collective-permute-done.3.refs_2_, ...), custom_call_target="tpu_custom_call" | custom-call | flops 7864320 | bytes 7340032 | tf_op jit(solution)/shard_map/pallas_call | solution.py:459
  20.3 0.1 collective-permute-start.5
  20.3 0.0 collective-permute-done.6.mate
  20.4 0.1 shard_map.45
  20.4 1.2 %collective-permute-done.5.mate = f32[2,32,256]{2,1,0:T(8,128)S(1)} collective-permute-done((f32[2,32,256]{2,1,0:T(8,128)S(1)}, f32[2,32,256]{2,1,0:T(8,128)S(1)}, u32[]{:S(2)}, u32[]{:S(2)}) %collective-permute-start.5) | collective-permute-done | bytes 65568 | tf_op jit(solution)/shard_map/ppermute | solution.py:467
  21.6 2.0 %collective-permute-start.7 = (f32[5,32,256]{2,1,0:T(8,128)S(1)}, f32[5,32,256]{2,1,0:T(8,128)S(1)}, u32[]{:S(2)}, u32[]{:S(2)}) collective-permute-start(f32[5,32,256]{2,1,0:T(8,128)S(1)} %get-tuple-element.66.refs_0_), channel_id=1, source_target_pairs={{0,2},{1,3},{2,0},{3,1},{4,6},{5,7},{6,4},{7,5},{8,10},{9,11},{10,... | collective-permute-start | bytes 491528 | tf_op jit(solution)/shard_map/ppermute | solution.py:471
  23.6 2.3 %collective-permute-start.8 = (f32[5,32,256]{2,1,0:T(8,128)S(1)}, f32[5,32,256]{2,1,0:T(8,128)S(1)}, u32[]{:S(2)}, u32[]{:S(2)}) collective-permute-start(f32[5,32,256]{2,1,0:T(8,128)S(1)} %get-tuple-element.66.refs_0_), channel_id=1, source_target_pairs={{0,4},{1,5},{2,6},{3,7},{4,0},{5,1},{6,2},{7,3},{8,12},{9,13},{10,... | collective-permute-start | bytes 491528 | tf_op jit(solution)/shard_map/ppermute | solution.py:471
  25.9 0.0 collective-permute-start.9
  25.9 2.5 %collective-permute-done.7.refs_1_ = f32[5,32,256]{2,1,0:T(8,128)S(1)} collective-permute-done((f32[5,32,256]{2,1,0:T(8,128)S(1)}, f32[5,32,256]{2,1,0:T(8,128)S(1)}, u32[]{:S(2)}, u32[]{:S(2)}) %collective-permute-start.7) | collective-permute-done | bytes 163872 | tf_op jit(solution)/shard_map/ppermute | solution.py:471
  28.4 4.5 %collective-permute-done.8.refs_2_ = f32[5,32,256]{2,1,0:T(8,128)S(1)} collective-permute-done((f32[5,32,256]{2,1,0:T(8,128)S(1)}, f32[5,32,256]{2,1,0:T(8,128)S(1)}, u32[]{:S(2)}, u32[]{:S(2)}) %collective-permute-start.8) | collective-permute-done | bytes 163872 | tf_op jit(solution)/shard_map/ppermute | solution.py:471
  32.9 0.7 %collective-permute-done.9.refs_3_ = f32[5,32,256]{2,1,0:T(8,128)S(1)} collective-permute-done((f32[5,32,256]{2,1,0:T(8,128)S(1)}, f32[5,32,256]{2,1,0:T(8,128)S(1)}, u32[]{:S(2)}, u32[]{:S(2)}) %collective-permute-start.9) | collective-permute-done | bytes 163872 | tf_op jit(solution)/shard_map/ppermute | solution.py:471
  33.6 0.1 shard_map.47
  33.7 0.1 collective-permute-start.10
  33.8 1.2 %collective-permute-done.10.got = f32[2,32,256]{2,1,0:T(8,128)S(1)} collective-permute-done((f32[2,32,256]{2,1,0:T(8,128)S(1)}, f32[2,32,256]{2,1,0:T(8,128)S(1)}, u32[]{:S(2)}, u32[]{:S(2)}) %collective-permute-start.10) | collective-permute-done | bytes 65568 | tf_op jit(solution)/shard_map/ppermute | solution.py:476
  35.1 0.9 %shard_map.48 = f32[64,8,256]{2,1,0:T(8,128)} custom-call(f32[2,32,256]{2,1,0:T(8,128)S(1)} %get-tuple-element.68.mine, f32[2,32,256]{2,1,0:T(8,128)S(1)} %collective-permute-done.10.got, f32[8,64,256]{2,1,0:T(8,128)S(1)} %get-tuple-element.70.dz, f32[8,64,256]{2,1,0:T(8,128)S(1)} %get-tuple-element.71.gf, f32[8,64,256]{2,1,0:T(8,128)S(1)} %get-tuple-element.72.gl), custom_call_target="tpu_custom_call" | custom-call | flops 524288 | bytes 2097152 | tf_op jit(solution)/shard_map/pallas_call | solution.py:477
  (2 shorter events, 0.0 us)
Async XLA Ops:
  0.9 6.5 %copy-start = (f32[64,8,256]{2,1,0:T(8,128)S(1)}, f32[64,8,256]{2,1,0:T(8,128)}, u32[]{:S(2)}) copy-start(f32[64,8,256]{2,1,0:T(8,128)} %force_hbm.1) | copy-start | bytes 1572868
  0.9 8.0 %collective-permute-start.1 = (f32[2,64,256]{2,1,0:T(8,128)S(1)}, f32[2,64,256]{2,1,0:T(8,128)S(1)}, u32[]{:S(2)}, u32[]{:S(2)}) collective-permute-start(f32[2,64,256]{2,1,0:T(8,128)S(1)} %shard_map.39.far), channel_id=1, source_target_pairs={{1,2},{2,1},{3,4},{4,3},{5,6},{6,5},{9,10},{10,9},{11,12},{12,11},... | collective-permute-start | bytes 393224 | tf_op jit(solution)/shard_map/ppermute | solution.py:430
  3.1 5.9 %collective-permute-start = (f32[2,64,256]{2,1,0:T(8,128)S(1)}, f32[2,64,256]{2,1,0:T(8,128)S(1)}, u32[]{:S(2)}, u32[]{:S(2)}) collective-permute-start(f32[2,64,256]{2,1,0:T(8,128)S(1)} %get-tuple-element.45.near), channel_id=1, source_target_pairs={{0,1},{1,0},{2,3},{3,2},{4,5},{5,4},{6,7},{7,6},{8,9},{9,8},{10,11... | collective-permute-start | bytes 393224 | tf_op jit(solution)/shard_map/ppermute | solution.py:429
  9.3 5.6 %collective-permute-start.2 = (f32[7,8,256]{2,1,0:T(8,128)S(1)}, f32[7,8,256]{2,1,0:T(8,128)S(1)}, u32[]{:S(2)}, u32[]{:S(2)}) collective-permute-start(f32[7,8,256]{2,1,0:T(8,128)S(1)} %get-tuple-element.46.refs_0_), channel_id=1, source_target_pairs={{0,8},{8,0},{16,24},{24,16},{1,9},{9,1},{17,25},{25,17},{2,10},{10... | collective-permute-start | bytes 172040 | tf_op jit(solution)/shard_map/ppermute | solution.py:457
  10.9 6.4 %collective-permute-start.3 = (f32[7,8,256]{2,1,0:T(8,128)S(1)}, f32[7,8,256]{2,1,0:T(8,128)S(1)}, u32[]{:S(2)}, u32[]{:S(2)}) collective-permute-start(f32[7,8,256]{2,1,0:T(8,128)S(1)} %get-tuple-element.46.refs_0_), channel_id=1, source_target_pairs={{0,16},{8,24},{16,0},{24,8},{1,17},{9,25},{17,1},{25,9},{2,18},{10... | collective-permute-start | bytes 172040 | tf_op jit(solution)/shard_map/ppermute | solution.py:457
  13.5 6.0 %collective-permute-start.4 = (f32[7,8,256]{2,1,0:T(8,128)S(1)}, f32[7,8,256]{2,1,0:T(8,128)S(1)}, u32[]{:S(2)}, u32[]{:S(2)}) collective-permute-start(f32[7,8,256]{2,1,0:T(8,128)S(1)} %get-tuple-element.46.refs_0_), channel_id=1, source_target_pairs={{0,24},{8,16},{16,8},{24,0},{1,25},{9,17},{17,9},{25,1},{2,26},{10... | collective-permute-start | bytes 172040 | tf_op jit(solution)/shard_map/ppermute | solution.py:457
  14.2 6.2 %collective-permute-start.6 = (f32[3,32,256]{2,1,0:T(8,128)S(1)}, f32[3,32,256]{2,1,0:T(8,128)S(1)}, u32[]{:S(2)}, u32[]{:S(2)}) collective-permute-start(f32[3,32,256]{2,1,0:T(8,128)S(1)} %get-tuple-element.63), channel_id=1, source_target_pairs={{0,1},{1,0},{2,3},{3,2},{4,5},{5,4},{6,7},{7,6},{8,9},{9,8},{10,11... | collective-permute-start | bytes 294920 | tf_op jit(solution)/shard_map/ppermute | solution.py:446
  20.3 1.3 %collective-permute-start.5 = (f32[2,32,256]{2,1,0:T(8,128)S(1)}, f32[2,32,256]{2,1,0:T(8,128)S(1)}, u32[]{:S(2)}, u32[]{:S(2)}) collective-permute-start(f32[2,32,256]{2,1,0:T(8,128)S(1)} %get-tuple-element.61), channel_id=1, source_target_pairs={{0,1},{1,0},{2,3},{3,2},{4,5},{5,4},{6,7},{7,6},{8,9},{9,8},{10,11... | collective-permute-start | bytes 196616 | tf_op jit(solution)/shard_map/ppermute | solution.py:467
  21.6 6.7 %collective-permute-start.7 = (f32[5,32,256]{2,1,0:T(8,128)S(1)}, f32[5,32,256]{2,1,0:T(8,128)S(1)}, u32[]{:S(2)}, u32[]{:S(2)}) collective-permute-start(f32[5,32,256]{2,1,0:T(8,128)S(1)} %get-tuple-element.66.refs_0_), channel_id=1, source_target_pairs={{0,2},{1,3},{2,0},{3,1},{4,6},{5,7},{6,4},{7,5},{8,10},{9,11},{10,... | collective-permute-start | bytes 491528 | tf_op jit(solution)/shard_map/ppermute | solution.py:471
  23.6 9.3 %collective-permute-start.8 = (f32[5,32,256]{2,1,0:T(8,128)S(1)}, f32[5,32,256]{2,1,0:T(8,128)S(1)}, u32[]{:S(2)}, u32[]{:S(2)}) collective-permute-start(f32[5,32,256]{2,1,0:T(8,128)S(1)} %get-tuple-element.66.refs_0_), channel_id=1, source_target_pairs={{0,4},{1,5},{2,6},{3,7},{4,0},{5,1},{6,2},{7,3},{8,12},{9,13},{10,... | collective-permute-start | bytes 491528 | tf_op jit(solution)/shard_map/ppermute | solution.py:471
  25.9 7.8 %collective-permute-start.9 = (f32[5,32,256]{2,1,0:T(8,128)S(1)}, f32[5,32,256]{2,1,0:T(8,128)S(1)}, u32[]{:S(2)}, u32[]{:S(2)}) collective-permute-start(f32[5,32,256]{2,1,0:T(8,128)S(1)} %get-tuple-element.66.refs_0_), channel_id=1, source_target_pairs={{0,6},{1,7},{2,4},{3,5},{4,2},{5,3},{6,0},{7,1},{8,14},{9,15},{10,... | collective-permute-start | bytes 491528 | tf_op jit(solution)/shard_map/ppermute | solution.py:471
  33.7 1.3 %collective-permute-start.10 = (f32[2,32,256]{2,1,0:T(8,128)S(1)}, f32[2,32,256]{2,1,0:T(8,128)S(1)}, u32[]{:S(2)}, u32[]{:S(2)}) collective-permute-start(f32[2,32,256]{2,1,0:T(8,128)S(1)} %get-tuple-element.69), channel_id=1, source_target_pairs={{0,1},{1,0},{2,3},{3,2},{4,5},{5,4},{6,7},{7,6},{8,9},{9,8},{10,11... | collective-permute-start | bytes 196616 | tf_op jit(solution)/shard_map/ppermute | solution.py:476

commit v5 on v4

--- a/solution.py
+++ b/solution.py
@@ -328,7 +328,7 @@
     chip_c[2] = high[2] - weight * high[1] * high[1] + jnp.where(is_low, 0.0, end_reach)
 
 
-def pair_kernel(own, mate, pair_c, chip_c, payload, jump_out):
+def pair_kernel(own, mate, pair_c, payload, jump_out):
     is_low = lax.rem(lax.axis_index("gz"), 2) == 0
     low_last = jnp.where(is_low, own[1], mate[1])
     high_first = jnp.where(is_low, mate[0], own[0])
@@ -337,18 +337,18 @@
     jump_out[...] = jump
     payload[0] = jnp.where(is_low, own[0], mate[0]) + pair_c[1] * q_mid
     payload[1] = jnp.where(is_low, mate[1], own[1]) - pair_c[2] * q_mid
-    for k in range(3):
-        payload[2 + k] = chip_c[k]
 
 
 def make_flux_kernel(chips):
     def kernel(*refs):
-        parts = refs[:chips]
-        pair_c, jump, mine, theirs, slots, flux = refs[chips:]
+        parts, coefs = refs[:chips], refs[chips:2 * chips]
+        pair_c, jump, mine, theirs, slots, flux = refs[2 * chips:]
         chip = lax.div(lax.axis_index("gz"), 2)
         is_low = lax.rem(lax.axis_index("gz"), 2) == 0
         for k in range(chips):
-            slots[jnp.bitwise_xor(chip, k)] = parts[k][...]
+            at = jnp.bitwise_xor(chip, k)
+            slots[at, :2] = parts[k][...]
+            slots[at, 2:] = coefs[k][...]
         flux[0] = jnp.zeros_like(jump)
         flux[chips] = jnp.zeros_like(jump)
         lower, right = [], None
@@ -465,14 +465,16 @@
     )(*parts, w, gf_x, gl_x, vel, c_y, n_y, gf_y, gl_y, al_y, ga_y, inv_y, c_z, n_z)
 
     mate = lax.ppermute(give, "gz", pair_route)
-    chip_ends, jump = call(pair_kernel, [(5,) + half, half], [VMEM] * 4, (), size, size)(
-        keep, mate, pair_c, chip_c
+    coefs = [chip_c] + [lax.ppermute(chip_c, "gz", to_chip(k)) for k in range(1, chips)]
+    mate, *coefs = lax.optimization_barrier((mate, *coefs))
+    chip_ends, jump = call(pair_kernel, [(2,) + half, half], [VMEM] * 3, (), size, size)(
+        keep, mate, pair_c
     )
     others = [chip_ends] + [lax.ppermute(chip_ends, "gz", to_chip(k)) for k in range(1, chips)]
     mine, theirs = call(
-        make_flux_kernel(chips), [(2,) + half] * 2, [VMEM] * (chips + 2),
+        make_flux_kernel(chips), [(2,) + half] * 2, [VMEM] * (2 * chips + 2),
         [pltpu.VMEM((chips, 5) + half, F32), pltpu.VMEM((chips + 1,) + half, F32)], size, size,
-    )(*others, pair_c, jump)
+    )(*others, *coefs, pair_c, jump)
     got = lax.ppermute(theirs, "gz", pair_route)
     return call(
         final_kernel, [volume], [VMEM] * 5,

time: 36.1 us -> 33.4 us (0.925)
  waiting for transfers between devices: 14.8 us -> 9.13 us
  starting transfers between devices: 14.1 us -> 17 us
    ppermute x3, waiting for transfers between devices: 7.74 us -> 3.89 us  [local(): lax.ppermute(chip_ends, 'gz', to_chip(k))]
    ppermute x0 -> x3, starting transfers between devices: none -> 3.75 us  [local(): lax.ppermute(chip_c, 'gz', to_chip(k))]
    ppermute x3, waiting for transfers between devices: 4.59 us -> 1.36 us  [local(): lax.ppermute(payload, 'gx', [(i, i ^ k) for i in range(nx)])]
    ppermute x0 -> x3, waiting for transfers between devices: none -> 2.63 us  [local(): lax.ppermute(chip_c, 'gz', to_chip(k))]
    ppermute x1, waiting for transfers between devices: 1.17 us -> 0.01 us  [local(): mate = lax.ppermute(give, 'gz', pair_route)]
    ppermute x3, starting transfers between devices: 4.27 us -> 3.55 us  [local(): lax.ppermute(chip_ends, 'gz', to_chip(k))]
  transfers between devices with their start and end apart: 11 -> 14, of which waited for: 7 -> 7; matrix products, arithmetic and copies ran while one was open for 0% -> 0% of each run, Pallas kernels for 13% -> 15%
where the time goes in v5:
time: 33.4 us; the launch traced here: 33.2 us
  starting transfers between devices  17 us (51%)
  waiting for transfers between devices  9.13 us (27%)
  Pallas kernels  6.96 us (21%)
    ppermute x3, starting transfers between devices, local(): lax.ppermute(payload, 'gx', [(i, i ^ k) for i in range(nx)])  4.45 us
    ppermute x1, starting transfers between devices, local(): pair = lax.ppermute(near, 'gz', pair_route)  4.32 us
    ppermute x3, waiting for transfers between devices, local(): lax.ppermute(chip_ends, 'gz', to_chip(k))  3.89 us
    ppermute x3, starting transfers between devices, local(): lax.ppermute(chip_c, 'gz', to_chip(k))  3.75 us
    ppermute x3, starting transfers between devices, local(): lax.ppermute(chip_ends, 'gz', to_chip(k))  3.55 us
    ppermute x3, waiting for transfers between devices, local(): lax.ppermute(chip_c, 'gz', to_chip(k))  2.63 us
    pallas_call x1, Pallas kernels, local(): call(x_factor_kernel, [volume] * 4 + [(5,) + plane, volume], [VMEM, VMEM,...  1.52 us
    pallas_call x1, Pallas kernels, local(): call(load_kernel, [volume, volume, zmajor, (2,) + slab], [HBM, HBM], [plt...  1.38 us
  transfers between devices with their start and end apart: 14, of which 7 were waited for; matrix products, arithmetic and copies ran while one was open for 0% of the time, Pallas kernels for 15%

profile of v5, /device:TPU:0, one launch (start us, length us, event | category | flops | bytes accessed | tf_op | source)
XLA Modules:
  0.0 33.2 jit_solution(10068884135272523097)
XLA Ops:
  0.0 0.9 %shard_map.39.far = f32[2,64,256]{2,1,0:T(8,128)S(1)} custom-call(f32[64,8,256]{2,1,0:T(8,128)} %visc_hbm.3, f32[64,8,256]{2,1,0:T(8,128)} %vel_hbm.3), custom_call_target="tpu_custom_call" | custom-call | bytes 524288 | tf_op jit(solution)/shard_map/pallas_call | solution.py:422
  0.9 0.7 %collective-permute-start.1 = (f32[2,64,256]{2,1,0:T(8,128)S(1)}, f32[2,64,256]{2,1,0:T(8,128)S(1)}, u32[]{:S(2)}, u32[]{:S(2)}) collective-permute-start(f32[2,64,256]{2,1,0:T(8,128)S(1)} %shard_map.39.far), channel_id=1, source_target_pairs={{1,2},{2,1},{3,4},{4,3},{5,6},{6,5},{9,10},{10,9},{11,12},{12,11},... | collective-permute-start | bytes 393224 | tf_op jit(solution)/shard_map/ppermute | solution.py:430
  1.6 1.4 %shard_map.37 = (f32[64,8,256]{2,1,0:T(8,128)S(1)}, f32[64,8,256]{2,1,0:T(8,128)S(1)}, f32[8,64,256]{2,1,0:T(8,128)S(1)}, f32[2,64,256]{2,1,0:T(8,128)S(1)}) custom-call(f32[64,8,256]{2,1,0:T(8,128)} %visc_hbm.3, f32[64,8,256]{2,1,0:T(8,128)} %vel_hbm.3), custom_call_target="tpu_custom_call" | custom-call | flops 131072 | bytes 3145728 | tf_op jit(solution)/shard_map/pallas_call | solution.py:425
  3.0 0.0 copy-start
  3.0 4.3 %collective-permute-start = (f32[2,64,256]{2,1,0:T(8,128)S(1)}, f32[2,64,256]{2,1,0:T(8,128)S(1)}, u32[]{:S(2)}, u32[]{:S(2)}) collective-permute-start(f32[2,64,256]{2,1,0:T(8,128)S(1)} %get-tuple-element.50.near), channel_id=1, source_target_pairs={{0,1},{1,0},{2,3},{3,2},{4,5},{5,4},{6,7},{7,6},{8,9},{9,8},{10,11... | collective-permute-start | bytes 393224 | tf_op jit(solution)/shard_map/ppermute | solution.py:429
  7.3 0.4 %shard_map.43 = (f32[8,64,256]{2,1,0:T(8,128)S(1)}, f32[8,64,256]{2,1,0:T(8,128)S(1)}, f32[8,64,256]{2,1,0:T(8,128)S(1)}, f32[8,64,256]{2,1,0:T(8,128)S(1)}, f32...) custom-call(f32[8,64,256]{2,1,0:T(8,128)S(1)} %get-tuple-element.62.visc_z), custom_call_target="tpu_custom_call" | custom-call | flops 2621440 | bytes 2621440 | tf_op jit(solution)/shard_map/pallas_call | solution.py:433
  7.7 0.1 collective-permute-start.6
  7.8 0.0 copy-done
  7.8 1.5 %shard_map.38 = (f32[64,8,256]{2,1,0:T(8,128)S(1)}, f32[64,8,256]{2,1,0:T(8,128)S(1)}, f32[64,8,256]{2,1,0:T(8,128)S(1)}, f32[64,8,256]{2,1,0:T(8,128)S(1)}, f32...) custom-call(f32[64,8,256]{2,1,0:T(8,128)S(1)} %get-tuple-element.44.visc, ...), custom_call_target="tpu_custom_call" | custom-call | flops 7864320 | bytes 4718592 | tf_op jit(solution)/shard_map/pallas_call | solution.py:437
  9.3 0.0 collective-permute-done.1.cross
  9.4 0.0 collective-permute-done.pair
  9.4 0.3 shard_map.41
  9.6 1.6 %collective-permute-start.2 = (f32[7,8,256]{2,1,0:T(8,128)S(1)}, f32[7,8,256]{2,1,0:T(8,128)S(1)}, u32[]{:S(2)}, u32[]{:S(2)}) collective-permute-start(f32[7,8,256]{2,1,0:T(8,128)S(1)} %get-tuple-element.51.refs_0_), channel_id=1, source_target_pairs={{0,8},{8,0},{16,24},{24,16},{1,9},{9,1},{17,25},{25,17},{2,10},{10... | collective-permute-start | bytes 172040 | tf_op jit(solution)/shard_map/ppermute | solution.py:457
  11.3 2.6 %collective-permute-start.3 = (f32[7,8,256]{2,1,0:T(8,128)S(1)}, f32[7,8,256]{2,1,0:T(8,128)S(1)}, u32[]{:S(2)}, u32[]{:S(2)}) collective-permute-start(f32[7,8,256]{2,1,0:T(8,128)S(1)} %get-tuple-element.51.refs_0_), channel_id=1, source_target_pairs={{0,16},{8,24},{16,0},{24,8},{1,17},{9,25},{17,1},{25,9},{2,18},{10... | collective-permute-start | bytes 172040 | tf_op jit(solution)/shard_map/ppermute | solution.py:457
  13.9 0.2 collective-permute-start.4
  14.1 0.0 collective-permute-done.6.mate
  14.2 1.6 %collective-permute-start.7 = (f32[3,32,256]{2,1,0:T(8,128)S(1)}, f32[3,32,256]{2,1,0:T(8,128)S(1)}, u32[]{:S(2)}, u32[]{:S(2)}) collective-permute-start(f32[3,32,256]{2,1,0:T(8,128)S(1)} %get-tuple-element.73.refs_4_), channel_id=1, source_target_pairs={{0,2},{1,3},{2,0},{3,1},{4,6},{5,7},{6,4},{7,5},{8,10},{9,11},{10,... | collective-permute-start | bytes 294920 | tf_op jit(solution)/shard_map/ppermute | solution.py:468
  15.7 2.2 %collective-permute-start.8 = (f32[3,32,256]{2,1,0:T(8,128)S(1)}, f32[3,32,256]{2,1,0:T(8,128)S(1)}, u32[]{:S(2)}, u32[]{:S(2)}) collective-permute-start(f32[3,32,256]{2,1,0:T(8,128)S(1)} %get-tuple-element.73.refs_4_), channel_id=1, source_target_pairs={{0,4},{1,5},{2,6},{3,7},{4,0},{5,1},{6,2},{7,3},{8,12},{9,13},{10,... | collective-permute-start | bytes 294920 | tf_op jit(solution)/shard_map/ppermute | solution.py:468
  17.9 0.0 collective-permute-done.2.refs_1_
  17.9 0.0 collective-permute-start.9
  17.9 0.6 %shard_map.42 = (f32[32,8,512]{2,1,0:T(8,128)S(1)}, f32[32,8,512]{2,1,0:T(8,128)S(1)}, f32[32,8,512]{2,1,0:T(8,128)S(1)}, f32[32,8,512]{2,1,0:T(8,128)S(1)}, f32...) custom-call(f32[64,8,256]{2,1,0:T(8,128)S(1)} %get-tuple-element.44.visc), custom_call_target="tpu_custom_call" | custom-call | flops 3932160 | bytes 3145728 | tf_op jit(solution)/shard_map/pallas_call | solution.py:441
  18.5 0.0 collective-permute-done.3.refs_2_
  18.6 1.4 %collective-permute-done.4.refs_3_ = f32[7,8,256]{2,1,0:T(8,128)S(1)} collective-permute-done((f32[7,8,256]{2,1,0:T(8,128)S(1)}, f32[7,8,256]{2,1,0:T(8,128)S(1)}, u32[]{:S(2)}, u32[]{:S(2)}) %collective-permute-start.4) | collective-permute-done | bytes 57376 | tf_op jit(solution)/shard_map/ppermute | solution.py:457
  19.9 0.8 %shard_map.44 = (f32[8,64,256]{2,1,0:T(8,128)S(1)}, f32[2,32,256]{2,1,0:T(8,128)S(1)}, f32[2,32,256]{2,1,0:T(8,128)S(1)}) custom-call(f32[7,8,256]{2,1,0:T(8,128)S(1)} %get-tuple-element.51.refs_0_, f32[7,8,256]{2,1,0:T(8,128)S(1)} %collective-permute-done.2.refs_1_, f32[7,8,256]{2,1,0:T(8,128)S(1)} %collective-permute-done.3.refs_2_, ...), custom_call_target="tpu_custom_call" | custom-call | flops 7864320 | bytes 7340032 | tf_op jit(solution)/shard_map/pallas_call | solution.py:459
  20.7 0.1 collective-permute-start.5
  20.8 0.0 collective-permute-done.7.refs_5_
  20.8 1.2 %collective-permute-done.8.refs_6_ = f32[3,32,256]{2,1,0:T(8,128)S(1)} collective-permute-done((f32[3,32,256]{2,1,0:T(8,128)S(1)}, f32[3,32,256]{2,1,0:T(8,128)S(1)}, u32[]{:S(2)}, u32[]{:S(2)}) %collective-permute-start.8) | collective-permute-done | bytes 98336 | tf_op jit(solution)/shard_map/ppermute | solution.py:468
  22.0 1.4 %collective-permute-done.9.refs_7_ = f32[3,32,256]{2,1,0:T(8,128)S(1)} collective-permute-done((f32[3,32,256]{2,1,0:T(8,128)S(1)}, f32[3,32,256]{2,1,0:T(8,128)S(1)}, u32[]{:S(2)}, u32[]{:S(2)}) %collective-permute-start.9) | collective-permute-done | bytes 98336 | tf_op jit(solution)/shard_map/ppermute | solution.py:468
  23.4 0.0 collective-permute-done.5.mate
  23.4 0.7 %collective-permute-start.10 = (f32[2,32,256]{2,1,0:T(8,128)S(1)}, f32[2,32,256]{2,1,0:T(8,128)S(1)}, u32[]{:S(2)}, u32[]{:S(2)}) collective-permute-start(f32[2,32,256]{2,1,0:T(8,128)S(1)} %get-tuple-element.72.refs_0_), channel_id=1, source_target_pairs={{0,2},{1,3},{2,0},{3,1},{4,6},{5,7},{6,4},{7,5},{8,10},{9,11},{10,... | collective-permute-start | bytes 196616 | tf_op jit(solution)/shard_map/ppermute | solution.py:473
  24.1 1.6 %collective-permute-start.11 = (f32[2,32,256]{2,1,0:T(8,128)S(1)}, f32[2,32,256]{2,1,0:T(8,128)S(1)}, u32[]{:S(2)}, u32[]{:S(2)}) collective-permute-start(f32[2,32,256]{2,1,0:T(8,128)S(1)} %get-tuple-element.72.refs_0_), channel_id=1, source_target_pairs={{0,4},{1,5},{2,6},{3,7},{4,0},{5,1},{6,2},{7,3},{8,12},{9,13},{10,... | collective-permute-start | bytes 196616 | tf_op jit(solution)/shard_map/ppermute | solution.py:473
  25.7 1.3 %collective-permute-start.12 = (f32[2,32,256]{2,1,0:T(8,128)S(1)}, f32[2,32,256]{2,1,0:T(8,128)S(1)}, u32[]{:S(2)}, u32[]{:S(2)}) collective-permute-start(f32[2,32,256]{2,1,0:T(8,128)S(1)} %get-tuple-element.72.refs_0_), channel_id=1, source_target_pairs={{0,6},{1,7},{2,4},{3,5},{4,2},{5,3},{6,0},{7,1},{8,14},{9,15},{10,... | collective-permute-start | bytes 196616 | tf_op jit(solution)/shard_map/ppermute | solution.py:473
  27.0 0.8 %collective-permute-done.10.refs_1_ = f32[2,32,256]{2,1,0:T(8,128)S(1)} collective-permute-done((f32[2,32,256]{2,1,0:T(8,128)S(1)}, f32[2,32,256]{2,1,0:T(8,128)S(1)}, u32[]{:S(2)}, u32[]{:S(2)}) %collective-permute-start.10) | collective-permute-done | bytes 65568 | tf_op jit(solution)/shard_map/ppermute | solution.py:473
  27.8 0.6 %collective-permute-done.11.refs_2_ = f32[2,32,256]{2,1,0:T(8,128)S(1)} collective-permute-done((f32[2,32,256]{2,1,0:T(8,128)S(1)}, f32[2,32,256]{2,1,0:T(8,128)S(1)}, u32[]{:S(2)}, u32[]{:S(2)}) %collective-permute-start.11) | collective-permute-done | bytes 65568 | tf_op jit(solution)/shard_map/ppermute | solution.py:473
  28.4 2.5 %collective-permute-done.12.refs_3_ = f32[2,32,256]{2,1,0:T(8,128)S(1)} collective-permute-done((f32[2,32,256]{2,1,0:T(8,128)S(1)}, f32[2,32,256]{2,1,0:T(8,128)S(1)}, u32[]{:S(2)}, u32[]{:S(2)}) %collective-permute-start.12) | collective-permute-done | bytes 65568 | tf_op jit(solution)/shard_map/ppermute | solution.py:473
  30.9 0.1 shard_map.47
  31.0 0.1 collective-permute-start.13
  31.1 1.2 %collective-permute-done.13.got = f32[2,32,256]{2,1,0:T(8,128)S(1)} collective-permute-done((f32[2,32,256]{2,1,0:T(8,128)S(1)}, f32[2,32,256]{2,1,0:T(8,128)S(1)}, u32[]{:S(2)}, u32[]{:S(2)}) %collective-permute-start.13) | collective-permute-done | bytes 65568 | tf_op jit(solution)/shard_map/ppermute | solution.py:478
  32.3 0.9 %shard_map.48 = f32[64,8,256]{2,1,0:T(8,128)} custom-call(f32[2,32,256]{2,1,0:T(8,128)S(1)} %get-tuple-element.78.mine, f32[2,32,256]{2,1,0:T(8,128)S(1)} %collective-permute-done.13.got, f32[8,64,256]{2,1,0:T(8,128)S(1)} %get-tuple-element.80.dz, f32[8,64,256]{2,1,0:T(8,128)S(1)} %get-tuple-element.81.gf, f32[8,64,256]{2,1,0:T(8,128)S(1)} %get-tuple-element.82.gl), custom_call_target="tpu_custom_call" | custom-call | flops 524288 | bytes 2097152 | tf_op jit(solution)/shard_map/pallas_call | solution.py:479
  (3 shorter events, 0.1 us)
Async XLA Ops:
  0.9 8.4 %collective-permute-start.1 = (f32[2,64,256]{2,1,0:T(8,128)S(1)}, f32[2,64,256]{2,1,0:T(8,128)S(1)}, u32[]{:S(2)}, u32[]{:S(2)}) collective-permute-start(f32[2,64,256]{2,1,0:T(8,128)S(1)} %shard_map.39.far), channel_id=1, source_target_pairs={{1,2},{2,1},{3,4},{4,3},{5,6},{6,5},{9,10},{10,9},{11,12},{12,11},... | collective-permute-start | bytes 393224 | tf_op jit(solution)/shard_map/ppermute | solution.py:430
  3.0 4.8 %copy-start = (f32[64,8,256]{2,1,0:T(8,128)S(1)}, f32[64,8,256]{2,1,0:T(8,128)}, u32[]{:S(2)}) copy-start(f32[64,8,256]{2,1,0:T(8,128)} %force_hbm.1) | copy-start | bytes 1572868
  3.0 6.4 %collective-permute-start = (f32[2,64,256]{2,1,0:T(8,128)S(1)}, f32[2,64,256]{2,1,0:T(8,128)S(1)}, u32[]{:S(2)}, u32[]{:S(2)}) collective-permute-start(f32[2,64,256]{2,1,0:T(8,128)S(1)} %get-tuple-element.50.near), channel_id=1, source_target_pairs={{0,1},{1,0},{2,3},{3,2},{4,5},{5,4},{6,7},{7,6},{8,9},{9,8},{10,11... | collective-permute-start | bytes 393224 | tf_op jit(solution)/shard_map/ppermute | solution.py:429
  7.7 6.4 %collective-permute-start.6 = (f32[3,32,256]{2,1,0:T(8,128)S(1)}, f32[3,32,256]{2,1,0:T(8,128)S(1)}, u32[]{:S(2)}, u32[]{:S(2)}) collective-permute-start(f32[3,32,256]{2,1,0:T(8,128)S(1)} %get-tuple-element.68), channel_id=1, source_target_pairs={{0,1},{1,0},{2,3},{3,2},{4,5},{5,4},{6,7},{7,6},{8,9},{9,8},{10,11... | collective-permute-start | bytes 294920 | tf_op jit(solution)/shard_map/ppermute | solution.py:446
  9.6 8.2 %collective-permute-start.2 = (f32[7,8,256]{2,1,0:T(8,128)S(1)}, f32[7,8,256]{2,1,0:T(8,128)S(1)}, u32[]{:S(2)}, u32[]{:S(2)}) collective-permute-start(f32[7,8,256]{2,1,0:T(8,128)S(1)} %get-tuple-element.51.refs_0_), channel_id=1, source_target_pairs={{0,8},{8,0},{16,24},{24,16},{1,9},{9,1},{17,25},{25,17},{2,10},{10... | collective-permute-start | bytes 172040 | tf_op jit(solution)/shard_map/ppermute | solution.py:457
  11.3 7.3 %collective-permute-start.3 = (f32[7,8,256]{2,1,0:T(8,128)S(1)}, f32[7,8,256]{2,1,0:T(8,128)S(1)}, u32[]{:S(2)}, u32[]{:S(2)}) collective-permute-start(f32[7,8,256]{2,1,0:T(8,128)S(1)} %get-tuple-element.51.refs_0_), channel_id=1, source_target_pairs={{0,16},{8,24},{16,0},{24,8},{1,17},{9,25},{17,1},{25,9},{2,18},{10... | collective-permute-start | bytes 172040 | tf_op jit(solution)/shard_map/ppermute | solution.py:457
  13.9 6.0 %collective-permute-start.4 = (f32[7,8,256]{2,1,0:T(8,128)S(1)}, f32[7,8,256]{2,1,0:T(8,128)S(1)}, u32[]{:S(2)}, u32[]{:S(2)}) collective-permute-start(f32[7,8,256]{2,1,0:T(8,128)S(1)} %get-tuple-element.51.refs_0_), channel_id=1, source_target_pairs={{0,24},{8,16},{16,8},{24,0},{1,25},{9,17},{17,9},{25,1},{2,26},{10... | collective-permute-start | bytes 172040 | tf_op jit(solution)/shard_map/ppermute | solution.py:457
  14.2 6.6 %collective-permute-start.7 = (f32[3,32,256]{2,1,0:T(8,128)S(1)}, f32[3,32,256]{2,1,0:T(8,128)S(1)}, u32[]{:S(2)}, u32[]{:S(2)}) collective-permute-start(f32[3,32,256]{2,1,0:T(8,128)S(1)} %get-tuple-element.73.refs_4_), channel_id=1, source_target_pairs={{0,2},{1,3},{2,0},{3,1},{4,6},{5,7},{6,4},{7,5},{8,10},{9,11},{10,... | collective-permute-start | bytes 294920 | tf_op jit(solution)/shard_map/ppermute | solution.py:468
  15.7 6.3 %collective-permute-start.8 = (f32[3,32,256]{2,1,0:T(8,128)S(1)}, f32[3,32,256]{2,1,0:T(8,128)S(1)}, u32[]{:S(2)}, u32[]{:S(2)}) collective-permute-start(f32[3,32,256]{2,1,0:T(8,128)S(1)} %get-tuple-element.73.refs_4_), channel_id=1, source_target_pairs={{0,4},{1,5},{2,6},{3,7},{4,0},{5,1},{6,2},{7,3},{8,12},{9,13},{10,... | collective-permute-start | bytes 294920 | tf_op jit(solution)/shard_map/ppermute | solution.py:468
  17.9 5.5 %collective-permute-start.9 = (f32[3,32,256]{2,1,0:T(8,128)S(1)}, f32[3,32,256]{2,1,0:T(8,128)S(1)}, u32[]{:S(2)}, u32[]{:S(2)}) collective-permute-start(f32[3,32,256]{2,1,0:T(8,128)S(1)} %get-tuple-element.73.refs_4_), channel_id=1, source_target_pairs={{0,6},{1,7},{2,4},{3,5},{4,2},{5,3},{6,0},{7,1},{8,14},{9,15},{10,... | collective-permute-start | bytes 294920 | tf_op jit(solution)/shard_map/ppermute | solution.py:468
  20.7 2.7 %collective-permute-start.5 = (f32[2,32,256]{2,1,0:T(8,128)S(1)}, f32[2,32,256]{2,1,0:T(8,128)S(1)}, u32[]{:S(2)}, u32[]{:S(2)}) collective-permute-start(f32[2,32,256]{2,1,0:T(8,128)S(1)} %get-tuple-element.66), channel_id=1, source_target_pairs={{0,1},{1,0},{2,3},{3,2},{4,5},{5,4},{6,7},{7,6},{8,9},{9,8},{10,11... | collective-permute-start | bytes 196616 | tf_op jit(solution)/shard_map/ppermute | solution.py:467
  23.4 4.3 %collective-permute-start.10 = (f32[2,32,256]{2,1,0:T(8,128)S(1)}, f32[2,32,256]{2,1,0:T(8,128)S(1)}, u32[]{:S(2)}, u32[]{:S(2)}) collective-permute-start(f32[2,32,256]{2,1,0:T(8,128)S(1)} %get-tuple-element.72.refs_0_), channel_id=1, source_target_pairs={{0,2},{1,3},{2,0},{3,1},{4,6},{5,7},{6,4},{7,5},{8,10},{9,11},{10,... | collective-permute-start | bytes 196616 | tf_op jit(solution)/shard_map/ppermute | solution.py:473
  24.1 4.3 %collective-permute-start.11 = (f32[2,32,256]{2,1,0:T(8,128)S(1)}, f32[2,32,256]{2,1,0:T(8,128)S(1)}, u32[]{:S(2)}, u32[]{:S(2)}) collective-permute-start(f32[2,32,256]{2,1,0:T(8,128)S(1)} %get-tuple-element.72.refs_0_), channel_id=1, source_target_pairs={{0,4},{1,5},{2,6},{3,7},{4,0},{5,1},{6,2},{7,3},{8,12},{9,13},{10,... | collective-permute-start | bytes 196616 | tf_op jit(solution)/shard_map/ppermute | solution.py:473
  25.7 5.2 %collective-permute-start.12 = (f32[2,32,256]{2,1,0:T(8,128)S(1)}, f32[2,32,256]{2,1,0:T(8,128)S(1)}, u32[]{:S(2)}, u32[]{:S(2)}) collective-permute-start(f32[2,32,256]{2,1,0:T(8,128)S(1)} %get-tuple-element.72.refs_0_), channel_id=1, source_target_pairs={{0,6},{1,7},{2,4},{3,5},{4,2},{5,3},{6,0},{7,1},{8,14},{9,15},{10,... | collective-permute-start | bytes 196616 | tf_op jit(solution)/shard_map/ppermute | solution.py:473
  31.0 1.3 %collective-permute-start.13 = (f32[2,32,256]{2,1,0:T(8,128)S(1)}, f32[2,32,256]{2,1,0:T(8,128)S(1)}, u32[]{:S(2)}, u32[]{:S(2)}) collective-permute-start(f32[2,32,256]{2,1,0:T(8,128)S(1)} %get-tuple-element.79), channel_id=1, source_target_pairs={{0,1},{1,0},{2,3},{3,2},{4,5},{5,4},{6,7},{7,6},{8,9},{9,8},{10,11... | collective-permute-start | bytes 196616 | tf_op jit(solution)/shard_map/ppermute | solution.py:478

commit v6 on v5

--- a/solution.py
+++ b/solution.py
@@ -27,6 +27,10 @@
             flops=flops, bytes_accessed=4 * touched, transcendentals=0
         ),
     )
+
+
+def partners(n):
+    return [0, *range(n - 1, 0, -1)]
 
 
 def iota(shape, dim):
@@ -258,8 +262,8 @@
          dz, keep, give, slots, flux, src, sol, turned, ends) = refs[parts_n:]
         rows, depth, width = w.shape
         me = lax.axis_index("gx")
-        for k in range(parts_n):
-            slots[jnp.bitwise_xor(me, k)] = parts[k][...]
+        for k, part in zip(partners(parts_n), parts):
+            slots[jnp.bitwise_xor(me, k)] = part[...]
         zero = jnp.zeros((depth, width), F32)
         flux[0] = zero
         flux[parts_n] = zero
@@ -346,9 +350,9 @@
         chip = lax.div(lax.axis_index("gz"), 2)
         is_low = lax.rem(lax.axis_index("gz"), 2) == 0
         for k in range(chips):
-            at = jnp.bitwise_xor(chip, k)
-            slots[at, :2] = parts[k][...]
-            slots[at, 2:] = coefs[k][...]
+            slots[jnp.bitwise_xor(chip, k), 2:] = coefs[k][...]
+        for k, part in zip(partners(chips), parts):
+            slots[jnp.bitwise_xor(chip, k), :2] = part[...]
         flux[0] = jnp.zeros_like(jump)
         flux[chips] = jnp.zeros_like(jump)
         lower, right = [], None
@@ -462,7 +466,7 @@
          pltpu.VMEM(lines, F32), pltpu.VMEM(lines, F32), pltpu.VMEM(zmajor, F32),
          pltpu.VMEM((2,) + slab, F32)],
         60 * size, 14 * size,
-    )(*parts, w, gf_x, gl_x, vel, c_y, n_y, gf_y, gl_y, al_y, ga_y, inv_y, c_z, n_z)
+    )(*[parts[k] for k in partners(nx)], w, gf_x, gl_x, vel, c_y, n_y, gf_y, gl_y, al_y, ga_y, inv_y, c_z, n_z)
 
     mate = lax.ppermute(give, "gz", pair_route)
     coefs = [chip_c] + [lax.ppermute(chip_c, "gz", to_chip(k)) for k in range(1, chips)]
@@ -474,7 +478,7 @@
     mine, theirs = call(
         make_flux_kernel(chips), [(2,) + half] * 2, [VMEM] * (2 * chips + 2),
         [pltpu.VMEM((chips, 5) + half, F32), pltpu.VMEM((chips + 1,) + half, F32)], size, size,
-    )(*others, *coefs, pair_c, jump)
+    )(*[others[k] for k in partners(chips)], *coefs, pair_c, jump)
     got = lax.ppermute(theirs, "gz", pair_route)
     return call(
         final_kernel, [volume], [VMEM] * 5,

time: 33.4 us -> 32.4 us (0.970)
  waiting for transfers between devices: 9.13 us -> 7.11 us
  starting transfers between devices: 17 us -> 18 us
    ppermute x3, waiting for transfers between devices: 1.36 us -> 0.01 us  [local(): lax.ppermute(payload, 'gx', [(i, i ^ k) for i in range(nx)])]
    ppermute x3, waiting for transfers between devices: 3.89 us -> 2.88 us  [local(): lax.ppermute(chip_ends, 'gz', to_chip(k))]
    ppermute x3, starting transfers between devices: 3.75 us -> 4.74 us  [local(): lax.ppermute(chip_c, 'gz', to_chip(k))]
    ppermute x3, waiting for transfers between devices: 2.63 us -> 2.97 us  [local(): lax.ppermute(chip_c, 'gz', to_chip(k))]
  transfers between devices with their start and end apart: 14 -> 14, of which waited for: 7 -> 6; matrix products, arithmetic and copies ran while one was open for 0% -> 0% of each run, Pallas kernels for 15% -> 16%
where the time goes in v6:
time: 32.4 us; the launch traced here: 32.2 us
  starting transfers between devices  18 us (56%)
  waiting for transfers between devices  7.11 us (22%)
  Pallas kernels  6.97 us (22%)
    ppermute x3, starting transfers between devices, local(): lax.ppermute(chip_c, 'gz', to_chip(k))  4.74 us
    ppermute x3, starting transfers between devices, local(): lax.ppermute(payload, 'gx', [(i, i ^ k) for i in range(nx)])  4.45 us
    ppermute x1, starting transfers between devices, local(): pair = lax.ppermute(near, 'gz', pair_route)  4.32 us
    ppermute x3, starting transfers between devices, local(): lax.ppermute(chip_ends, 'gz', to_chip(k))  3.55 us
    ppermute x3, waiting for transfers between devices, local(): lax.ppermute(chip_c, 'gz', to_chip(k))  2.97 us
    ppermute x3, waiting for transfers between devices, local(): lax.ppermute(chip_ends, 'gz', to_chip(k))  2.88 us
    pallas_call x1, Pallas kernels, local(): call(x_factor_kernel, [volume] * 4 + [(5,) + plane, volume], [VMEM, VMEM,...  1.52 us
    pallas_call x1, Pallas kernels, local(): call(load_kernel, [volume, volume, zmajor, (2,) + slab], [HBM, HBM], [plt...  1.38 us
  transfers between devices with their start and end apart: 14, of which 6 were waited for; matrix products, arithmetic and copies ran while one was open for 0% of the time, Pallas kernels for 16%

profile of v6, /device:TPU:0, one launch (start us, length us, event | category | flops | bytes accessed | tf_op | source)
XLA Modules:
  0.0 32.2 jit_solution(4685717936030964659)
XLA Ops:
  0.0 0.9 %shard_map.39.far = f32[2,64,256]{2,1,0:T(8,128)S(1)} custom-call(f32[64,8,256]{2,1,0:T(8,128)} %visc_hbm.3, f32[64,8,256]{2,1,0:T(8,128)} %vel_hbm.3), custom_call_target="tpu_custom_call" | custom-call | bytes 524288 | tf_op jit(solution)/shard_map/pallas_call | solution.py:426
  0.9 0.7 %collective-permute-start.1 = (f32[2,64,256]{2,1,0:T(8,128)S(1)}, f32[2,64,256]{2,1,0:T(8,128)S(1)}, u32[]{:S(2)}, u32[]{:S(2)}) collective-permute-start(f32[2,64,256]{2,1,0:T(8,128)S(1)} %shard_map.39.far), channel_id=1, source_target_pairs={{1,2},{2,1},{3,4},{4,3},{5,6},{6,5},{9,10},{10,9},{11,12},{12,11},... | collective-permute-start | bytes 393224 | tf_op jit(solution)/shard_map/ppermute | solution.py:434
  1.6 1.4 %shard_map.37 = (f32[64,8,256]{2,1,0:T(8,128)S(1)}, f32[64,8,256]{2,1,0:T(8,128)S(1)}, f32[8,64,256]{2,1,0:T(8,128)S(1)}, f32[2,64,256]{2,1,0:T(8,128)S(1)}) custom-call(f32[64,8,256]{2,1,0:T(8,128)} %visc_hbm.3, f32[64,8,256]{2,1,0:T(8,128)} %vel_hbm.3), custom_call_target="tpu_custom_call" | custom-call | flops 131072 | bytes 3145728 | tf_op jit(solution)/shard_map/pallas_call | solution.py:429
  3.0 0.0 copy-start
  3.0 4.3 %collective-permute-start = (f32[2,64,256]{2,1,0:T(8,128)S(1)}, f32[2,64,256]{2,1,0:T(8,128)S(1)}, u32[]{:S(2)}, u32[]{:S(2)}) collective-permute-start(f32[2,64,256]{2,1,0:T(8,128)S(1)} %get-tuple-element.50.near), channel_id=1, source_target_pairs={{0,1},{1,0},{2,3},{3,2},{4,5},{5,4},{6,7},{7,6},{8,9},{9,8},{10,11... | collective-permute-start | bytes 393224 | tf_op jit(solution)/shard_map/ppermute | solution.py:433
  7.3 0.4 %shard_map.43 = (f32[8,64,256]{2,1,0:T(8,128)S(1)}, f32[8,64,256]{2,1,0:T(8,128)S(1)}, f32[8,64,256]{2,1,0:T(8,128)S(1)}, f32[8,64,256]{2,1,0:T(8,128)S(1)}, f32...) custom-call(f32[8,64,256]{2,1,0:T(8,128)S(1)} %get-tuple-element.62.visc_z), custom_call_target="tpu_custom_call" | custom-call | flops 2621440 | bytes 2621440 | tf_op jit(solution)/shard_map/pallas_call | solution.py:437
  7.7 0.1 collective-permute-start.6
  7.8 0.0 copy-done
  7.8 1.5 %shard_map.38 = (f32[64,8,256]{2,1,0:T(8,128)S(1)}, f32[64,8,256]{2,1,0:T(8,128)S(1)}, f32[64,8,256]{2,1,0:T(8,128)S(1)}, f32[64,8,256]{2,1,0:T(8,128)S(1)}, f32...) custom-call(f32[64,8,256]{2,1,0:T(8,128)S(1)} %get-tuple-element.44.visc, ...), custom_call_target="tpu_custom_call" | custom-call | flops 7864320 | bytes 4718592 | tf_op jit(solution)/shard_map/pallas_call | solution.py:441
  9.3 0.0 collective-permute-done.1.cross
  9.4 0.0 collective-permute-done.pair
  9.4 0.3 shard_map.41
  9.6 3.7 %collective-permute-start.2 = (f32[7,8,256]{2,1,0:T(8,128)S(1)}, f32[7,8,256]{2,1,0:T(8,128)S(1)}, u32[]{:S(2)}, u32[]{:S(2)}) collective-permute-start(f32[7,8,256]{2,1,0:T(8,128)S(1)} %get-tuple-element.51.refs_0_), channel_id=1, source_target_pairs={{0,24},{8,16},{16,8},{24,0},{1,25},{9,17},{17,9},{25,1},{2,26},{10... | collective-permute-start | bytes 172040 | tf_op jit(solution)/shard_map/ppermute | solution.py:461
  13.3 0.0 collective-permute-start.3
  13.3 0.8 %collective-permute-start.4 = (f32[7,8,256]{2,1,0:T(8,128)S(1)}, f32[7,8,256]{2,1,0:T(8,128)S(1)}, u32[]{:S(2)}, u32[]{:S(2)}) collective-permute-start(f32[7,8,256]{2,1,0:T(8,128)S(1)} %get-tuple-element.51.refs_0_), channel_id=1, source_target_pairs={{0,8},{8,0},{16,24},{24,16},{1,9},{9,1},{17,25},{25,17},{2,10},{10... | collective-permute-start | bytes 172040 | tf_op jit(solution)/shard_map/ppermute | solution.py:461
  14.1 0.0 collective-permute-done.6.mate
  14.2 1.6 %collective-permute-start.7 = (f32[3,32,256]{2,1,0:T(8,128)S(1)}, f32[3,32,256]{2,1,0:T(8,128)S(1)}, u32[]{:S(2)}, u32[]{:S(2)}) collective-permute-start(f32[3,32,256]{2,1,0:T(8,128)S(1)} %get-tuple-element.73.refs_4_), channel_id=1, source_target_pairs={{0,2},{1,3},{2,0},{3,1},{4,6},{5,7},{6,4},{7,5},{8,10},{9,11},{10,... | collective-permute-start | bytes 294920 | tf_op jit(solution)/shard_map/ppermute | solution.py:472
  15.7 2.2 %collective-permute-start.8 = (f32[3,32,256]{2,1,0:T(8,128)S(1)}, f32[3,32,256]{2,1,0:T(8,128)S(1)}, u32[]{:S(2)}, u32[]{:S(2)}) collective-permute-start(f32[3,32,256]{2,1,0:T(8,128)S(1)} %get-tuple-element.73.refs_4_), channel_id=1, source_target_pairs={{0,4},{1,5},{2,6},{3,7},{4,0},{5,1},{6,2},{7,3},{8,12},{9,13},{10,... | collective-permute-start | bytes 294920 | tf_op jit(solution)/shard_map/ppermute | solution.py:472
  17.9 0.0 collective-permute-done.2.refs_1_
  17.9 1.0 %collective-permute-start.9 = (f32[3,32,256]{2,1,0:T(8,128)S(1)}, f32[3,32,256]{2,1,0:T(8,128)S(1)}, u32[]{:S(2)}, u32[]{:S(2)}) collective-permute-start(f32[3,32,256]{2,1,0:T(8,128)S(1)} %get-tuple-element.73.refs_4_), channel_id=1, source_target_pairs={{0,6},{1,7},{2,4},{3,5},{4,2},{5,3},{6,0},{7,1},{8,14},{9,15},{10,... | collective-permute-start | bytes 294920 | tf_op jit(solution)/shard_map/ppermute | solution.py:472
  18.9 0.6 %shard_map.42 = (f32[32,8,512]{2,1,0:T(8,128)S(1)}, f32[32,8,512]{2,1,0:T(8,128)S(1)}, f32[32,8,512]{2,1,0:T(8,128)S(1)}, f32[32,8,512]{2,1,0:T(8,128)S(1)}, f32...) custom-call(f32[64,8,256]{2,1,0:T(8,128)S(1)} %get-tuple-element.44.visc), custom_call_target="tpu_custom_call" | custom-call | flops 3932160 | bytes 3145728 | tf_op jit(solution)/shard_map/pallas_call | solution.py:445
  19.5 0.0 collective-permute-done.3.refs_2_
  19.5 0.0 collective-permute-done.4.refs_3_
  19.6 0.8 %shard_map.44 = (f32[8,64,256]{2,1,0:T(8,128)S(1)}, f32[2,32,256]{2,1,0:T(8,128)S(1)}, f32[2,32,256]{2,1,0:T(8,128)S(1)}) custom-call(f32[7,8,256]{2,1,0:T(8,128)S(1)} %get-tuple-element.51.refs_0_, f32[7,8,256]{2,1,0:T(8,128)S(1)} %collective-permute-done.2.refs_1_, f32[7,8,256]{2,1,0:T(8,128)S(1)} %collective-permute-done.3.refs_2_, ...), custom_call_target="tpu_custom_call" | custom-call | flops 7864320 | bytes 7340032 | tf_op jit(solution)/shard_map/pallas_call | solution.py:463
  20.3 0.1 collective-permute-start.5
  20.4 0.0 collective-permute-done.7.refs_5_
  20.4 1.7 %collective-permute-done.8.refs_6_ = f32[3,32,256]{2,1,0:T(8,128)S(1)} collective-permute-done((f32[3,32,256]{2,1,0:T(8,128)S(1)}, f32[3,32,256]{2,1,0:T(8,128)S(1)}, u32[]{:S(2)}, u32[]{:S(2)}) %collective-permute-start.8) | collective-permute-done | bytes 98336 | tf_op jit(solution)/shard_map/ppermute | solution.py:472
  22.1 1.3 %collective-permute-done.9.refs_7_ = f32[3,32,256]{2,1,0:T(8,128)S(1)} collective-permute-done((f32[3,32,256]{2,1,0:T(8,128)S(1)}, f32[3,32,256]{2,1,0:T(8,128)S(1)}, u32[]{:S(2)}, u32[]{:S(2)}) %collective-permute-start.9) | collective-permute-done | bytes 98336 | tf_op jit(solution)/shard_map/ppermute | solution.py:472
  23.4 0.0 collective-permute-done.5.mate
  23.4 1.3 %collective-permute-start.10 = (f32[2,32,256]{2,1,0:T(8,128)S(1)}, f32[2,32,256]{2,1,0:T(8,128)S(1)}, u32[]{:S(2)}, u32[]{:S(2)}) collective-permute-start(f32[2,32,256]{2,1,0:T(8,128)S(1)} %get-tuple-element.72.refs_0_), channel_id=1, source_target_pairs={{0,6},{1,7},{2,4},{3,5},{4,2},{5,3},{6,0},{7,1},{8,14},{9,15},{10,... | collective-permute-start | bytes 196616 | tf_op jit(solution)/shard_map/ppermute | solution.py:477
  24.7 0.9 %collective-permute-start.11 = (f32[2,32,256]{2,1,0:T(8,128)S(1)}, f32[2,32,256]{2,1,0:T(8,128)S(1)}, u32[]{:S(2)}, u32[]{:S(2)}) collective-permute-start(f32[2,32,256]{2,1,0:T(8,128)S(1)} %get-tuple-element.72.refs_0_), channel_id=1, source_target_pairs={{0,4},{1,5},{2,6},{3,7},{4,0},{5,1},{6,2},{7,3},{8,12},{9,13},{10,... | collective-permute-start | bytes 196616 | tf_op jit(solution)/shard_map/ppermute | solution.py:477
  25.6 1.4 %collective-permute-start.12 = (f32[2,32,256]{2,1,0:T(8,128)S(1)}, f32[2,32,256]{2,1,0:T(8,128)S(1)}, u32[]{:S(2)}, u32[]{:S(2)}) collective-permute-start(f32[2,32,256]{2,1,0:T(8,128)S(1)} %get-tuple-element.72.refs_0_), channel_id=1, source_target_pairs={{0,2},{1,3},{2,0},{3,1},{4,6},{5,7},{6,4},{7,5},{8,10},{9,11},{10,... | collective-permute-start | bytes 196616 | tf_op jit(solution)/shard_map/ppermute | solution.py:477
  27.0 1.8 %collective-permute-done.10.refs_1_ = f32[2,32,256]{2,1,0:T(8,128)S(1)} collective-permute-done((f32[2,32,256]{2,1,0:T(8,128)S(1)}, f32[2,32,256]{2,1,0:T(8,128)S(1)}, u32[]{:S(2)}, u32[]{:S(2)}) %collective-permute-start.10) | collective-permute-done | bytes 65568 | tf_op jit(solution)/shard_map/ppermute | solution.py:477
  28.8 0.7 %collective-permute-done.11.refs_2_ = f32[2,32,256]{2,1,0:T(8,128)S(1)} collective-permute-done((f32[2,32,256]{2,1,0:T(8,128)S(1)}, f32[2,32,256]{2,1,0:T(8,128)S(1)}, u32[]{:S(2)}, u32[]{:S(2)}) %collective-permute-start.11) | collective-permute-done | bytes 65568 | tf_op jit(solution)/shard_map/ppermute | solution.py:477
  29.5 0.4 %collective-permute-done.12.refs_3_ = f32[2,32,256]{2,1,0:T(8,128)S(1)} collective-permute-done((f32[2,32,256]{2,1,0:T(8,128)S(1)}, f32[2,32,256]{2,1,0:T(8,128)S(1)}, u32[]{:S(2)}, u32[]{:S(2)}) %collective-permute-start.12) | collective-permute-done | bytes 65568 | tf_op jit(solution)/shard_map/ppermute | solution.py:477
  29.9 0.1 shard_map.47
  30.0 0.1 collective-permute-start.13
  30.1 1.2 %collective-permute-done.13.got = f32[2,32,256]{2,1,0:T(8,128)S(1)} collective-permute-done((f32[2,32,256]{2,1,0:T(8,128)S(1)}, f32[2,32,256]{2,1,0:T(8,128)S(1)}, u32[]{:S(2)}, u32[]{:S(2)}) %collective-permute-start.13) | collective-permute-done | bytes 65568 | tf_op jit(solution)/shard_map/ppermute | solution.py:482
  31.3 0.9 %shard_map.48 = f32[64,8,256]{2,1,0:T(8,128)} custom-call(f32[2,32,256]{2,1,0:T(8,128)S(1)} %get-tuple-element.78.mine, f32[2,32,256]{2,1,0:T(8,128)S(1)} %collective-permute-done.13.got, f32[8,64,256]{2,1,0:T(8,128)S(1)} %get-tuple-element.80.dz, f32[8,64,256]{2,1,0:T(8,128)S(1)} %get-tuple-element.81.gf, f32[8,64,256]{2,1,0:T(8,128)S(1)} %get-tuple-element.82.gl), custom_call_target="tpu_custom_call" | custom-call | flops 524288 | bytes 2097152 | tf_op jit(solution)/shard_map/pallas_call | solution.py:483
  (3 shorter events, 0.1 us)
Async XLA Ops:
  0.9 8.4 %collective-permute-start.1 = (f32[2,64,256]{2,1,0:T(8,128)S(1)}, f32[2,64,256]{2,1,0:T(8,128)S(1)}, u32[]{:S(2)}, u32[]{:S(2)}) collective-permute-start(f32[2,64,256]{2,1,0:T(8,128)S(1)} %shard_map.39.far), channel_id=1, source_target_pairs={{1,2},{2,1},{3,4},{4,3},{5,6},{6,5},{9,10},{10,9},{11,12},{12,11},... | collective-permute-start | bytes 393224 | tf_op jit(solution)/shard_map/ppermute | solution.py:434
  3.0 4.8 %copy-start = (f32[64,8,256]{2,1,0:T(8,128)S(1)}, f32[64,8,256]{2,1,0:T(8,128)}, u32[]{:S(2)}) copy-start(f32[64,8,256]{2,1,0:T(8,128)} %force_hbm.1) | copy-start | bytes 1572868
  3.0 6.4 %collective-permute-start = (f32[2,64,256]{2,1,0:T(8,128)S(1)}, f32[2,64,256]{2,1,0:T(8,128)S(1)}, u32[]{:S(2)}, u32[]{:S(2)}) collective-permute-start(f32[2,64,256]{2,1,0:T(8,128)S(1)} %get-tuple-element.50.near), channel_id=1, source_target_pairs={{0,1},{1,0},{2,3},{3,2},{4,5},{5,4},{6,7},{7,6},{8,9},{9,8},{10,11... | collective-permute-start | bytes 393224 | tf_op jit(solution)/shard_map/ppermute | solution.py:433
  7.7 6.4 %collective-permute-start.6 = (f32[3,32,256]{2,1,0:T(8,128)S(1)}, f32[3,32,256]{2,1,0:T(8,128)S(1)}, u32[]{:S(2)}, u32[]{:S(2)}) collective-permute-start(f32[3,32,256]{2,1,0:T(8,128)S(1)} %get-tuple-element.68), channel_id=1, source_target_pairs={{0,1},{1,0},{2,3},{3,2},{4,5},{5,4},{6,7},{7,6},{8,9},{9,8},{10,11... | collective-permute-start | bytes 294920 | tf_op jit(solution)/shard_map/ppermute | solution.py:450
  9.6 8.2 %collective-permute-start.2 = (f32[7,8,256]{2,1,0:T(8,128)S(1)}, f32[7,8,256]{2,1,0:T(8,128)S(1)}, u32[]{:S(2)}, u32[]{:S(2)}) collective-permute-start(f32[7,8,256]{2,1,0:T(8,128)S(1)} %get-tuple-element.51.refs_0_), channel_id=1, source_target_pairs={{0,24},{8,16},{16,8},{24,0},{1,25},{9,17},{17,9},{25,1},{2,26},{10... | collective-permute-start | bytes 172040 | tf_op jit(solution)/shard_map/ppermute | solution.py:461
  13.3 6.2 %collective-permute-start.3 = (f32[7,8,256]{2,1,0:T(8,128)S(1)}, f32[7,8,256]{2,1,0:T(8,128)S(1)}, u32[]{:S(2)}, u32[]{:S(2)}) collective-permute-start(f32[7,8,256]{2,1,0:T(8,128)S(1)} %get-tuple-element.51.refs_0_), channel_id=1, source_target_pairs={{0,16},{8,24},{16,0},{24,8},{1,17},{9,25},{17,1},{25,9},{2,18},{10... | collective-permute-start | bytes 172040 | tf_op jit(solution)/shard_map/ppermute | solution.py:461
  13.3 6.2 %collective-permute-start.4 = (f32[7,8,256]{2,1,0:T(8,128)S(1)}, f32[7,8,256]{2,1,0:T(8,128)S(1)}, u32[]{:S(2)}, u32[]{:S(2)}) collective-permute-start(f32[7,8,256]{2,1,0:T(8,128)S(1)} %get-tuple-element.51.refs_0_), channel_id=1, source_target_pairs={{0,8},{8,0},{16,24},{24,16},{1,9},{9,1},{17,25},{25,17},{2,10},{10... | collective-permute-start | bytes 172040 | tf_op jit(solution)/shard_map/ppermute | solution.py:461
  14.2 6.3 %collective-permute-start.7 = (f32[3,32,256]{2,1,0:T(8,128)S(1)}, f32[3,32,256]{2,1,0:T(8,128)S(1)}, u32[]{:S(2)}, u32[]{:S(2)}) collective-permute-start(f32[3,32,256]{2,1,0:T(8,128)S(1)} %get-tuple-element.73.refs_4_), channel_id=1, source_target_pairs={{0,2},{1,3},{2,0},{3,1},{4,6},{5,7},{6,4},{7,5},{8,10},{9,11},{10,... | collective-permute-start | bytes 294920 | tf_op jit(solution)/shard_map/ppermute | solution.py:472
  15.7 6.4 %collective-permute-start.8 = (f32[3,32,256]{2,1,0:T(8,128)S(1)}, f32[3,32,256]{2,1,0:T(8,128)S(1)}, u32[]{:S(2)}, u32[]{:S(2)}) collective-permute-start(f32[3,32,256]{2,1,0:T(8,128)S(1)} %get-tuple-element.73.refs_4_), channel_id=1, source_target_pairs={{0,4},{1,5},{2,6},{3,7},{4,0},{5,1},{6,2},{7,3},{8,12},{9,13},{10,... | collective-permute-start | bytes 294920 | tf_op jit(solution)/shard_map/ppermute | solution.py:472
  17.9 5.5 %collective-permute-start.9 = (f32[3,32,256]{2,1,0:T(8,128)S(1)}, f32[3,32,256]{2,1,0:T(8,128)S(1)}, u32[]{:S(2)}, u32[]{:S(2)}) collective-permute-start(f32[3,32,256]{2,1,0:T(8,128)S(1)} %get-tuple-element.73.refs_4_), channel_id=1, source_target_pairs={{0,6},{1,7},{2,4},{3,5},{4,2},{5,3},{6,0},{7,1},{8,14},{9,15},{10,... | collective-permute-start | bytes 294920 | tf_op jit(solution)/shard_map/ppermute | solution.py:472
  20.3 3.1 %collective-permute-start.5 = (f32[2,32,256]{2,1,0:T(8,128)S(1)}, f32[2,32,256]{2,1,0:T(8,128)S(1)}, u32[]{:S(2)}, u32[]{:S(2)}) collective-permute-start(f32[2,32,256]{2,1,0:T(8,128)S(1)} %get-tuple-element.66), channel_id=1, source_target_pairs={{0,1},{1,0},{2,3},{3,2},{4,5},{5,4},{6,7},{7,6},{8,9},{9,8},{10,11... | collective-permute-start | bytes 196616 | tf_op jit(solution)/shard_map/ppermute | solution.py:471
  23.4 5.4 %collective-permute-start.10 = (f32[2,32,256]{2,1,0:T(8,128)S(1)}, f32[2,32,256]{2,1,0:T(8,128)S(1)}, u32[]{:S(2)}, u32[]{:S(2)}) collective-permute-start(f32[2,32,256]{2,1,0:T(8,128)S(1)} %get-tuple-element.72.refs_0_), channel_id=1, source_target_pairs={{0,6},{1,7},{2,4},{3,5},{4,2},{5,3},{6,0},{7,1},{8,14},{9,15},{10,... | collective-permute-start | bytes 196616 | tf_op jit(solution)/shard_map/ppermute | solution.py:477
  24.7 4.7 %collective-permute-start.11 = (f32[2,32,256]{2,1,0:T(8,128)S(1)}, f32[2,32,256]{2,1,0:T(8,128)S(1)}, u32[]{:S(2)}, u32[]{:S(2)}) collective-permute-start(f32[2,32,256]{2,1,0:T(8,128)S(1)} %get-tuple-element.72.refs_0_), channel_id=1, source_target_pairs={{0,4},{1,5},{2,6},{3,7},{4,0},{5,1},{6,2},{7,3},{8,12},{9,13},{10,... | collective-permute-start | bytes 196616 | tf_op jit(solution)/shard_map/ppermute | solution.py:477
  25.6 4.3 %collective-permute-start.12 = (f32[2,32,256]{2,1,0:T(8,128)S(1)}, f32[2,32,256]{2,1,0:T(8,128)S(1)}, u32[]{:S(2)}, u32[]{:S(2)}) collective-permute-start(f32[2,32,256]{2,1,0:T(8,128)S(1)} %get-tuple-element.72.refs_0_), channel_id=1, source_target_pairs={{0,2},{1,3},{2,0},{3,1},{4,6},{5,7},{6,4},{7,5},{8,10},{9,11},{10,... | collective-permute-start | bytes 196616 | tf_op jit(solution)/shard_map/ppermute | solution.py:477
  30.0 1.3 %collective-permute-start.13 = (f32[2,32,256]{2,1,0:T(8,128)S(1)}, f32[2,32,256]{2,1,0:T(8,128)S(1)}, u32[]{:S(2)}, u32[]{:S(2)}) collective-permute-start(f32[2,32,256]{2,1,0:T(8,128)S(1)} %get-tuple-element.79), channel_id=1, source_target_pairs={{0,1},{1,0},{2,3},{3,2},{4,5},{5,4},{6,7},{7,6},{8,9},{9,8},{10,11... | collective-permute-start | bytes 196616 | tf_op jit(solution)/shard_map/ppermute | solution.py:482

commit v7 on v6

--- a/solution.py
+++ b/solution.py
@@ -349,10 +349,9 @@
         pair_c, jump, mine, theirs, slots, flux = refs[2 * chips:]
         chip = lax.div(lax.axis_index("gz"), 2)
         is_low = lax.rem(lax.axis_index("gz"), 2) == 0
-        for k in range(chips):
-            slots[jnp.bitwise_xor(chip, k), 2:] = coefs[k][...]
-        for k, part in zip(partners(chips), parts):
+        for k, part, coef in zip(partners(chips), parts, coefs):
             slots[jnp.bitwise_xor(chip, k), :2] = part[...]
+            slots[jnp.bitwise_xor(chip, k), 2:] = coef[...]
         flux[0] = jnp.zeros_like(jump)
         flux[chips] = jnp.zeros_like(jump)
         lower, right = [], None
@@ -469,7 +468,7 @@
     )(*[parts[k] for k in partners(nx)], w, gf_x, gl_x, vel, c_y, n_y, gf_y, gl_y, al_y, ga_y, inv_y, c_z, n_z)
 
     mate = lax.ppermute(give, "gz", pair_route)
-    coefs = [chip_c] + [lax.ppermute(chip_c, "gz", to_chip(k)) for k in range(1, chips)]
+    coefs = [chip_c] + [lax.ppermute(chip_c, "gz", to_chip(k)) for k in partners(chips)[1:]]
     mate, *coefs = lax.optimization_barrier((mate, *coefs))
     chip_ends, jump = call(pair_kernel, [(2,) + half, half], [VMEM] * 3, (), size, size)(
         keep, mate, pair_c

time: 32.4 us -> 31.8 us (0.981)
  starting transfers between devices: 18 us -> 17 us
  waiting for transfers between devices: 7.11 us -> 7.53 us
    ppermute x3, starting transfers between devices: 4.74 us -> 3.81 us  [local(): lax.ppermute(chip_c, 'gz', to_chip(k))]
  transfers between devices with their start and end apart: 14 -> 14, of which waited for: 6 -> 8; matrix products, arithmetic and copies ran while one was open for 0% -> 0% of each run, Pallas kernels for 16% -> 16%
where the time goes in v7:
time: 31.8 us; the launch traced here: 31.6 us
  starting transfers between devices  17 us (53%)
  waiting for transfers between devices  7.53 us (24%)
  Pallas kernels  6.96 us (22%)
    ppermute x3, starting transfers between devices, local(): lax.ppermute(payload, 'gx', [(i, i ^ k) for i in range(nx)])  4.45 us
    ppermute x1, starting transfers between devices, local(): pair = lax.ppermute(near, 'gz', pair_route)  4.32 us
    ppermute x3, starting transfers between devices, local(): lax.ppermute(chip_c, 'gz', to_chip(k))  3.81 us
    ppermute x3, starting transfers between devices, local(): lax.ppermute(chip_ends, 'gz', to_chip(k))  3.55 us
    ppermute x3, waiting for transfers between devices, local(): lax.ppermute(chip_ends, 'gz', to_chip(k))  3.15 us
    ppermute x3, waiting for transfers between devices, local(): lax.ppermute(chip_c, 'gz', to_chip(k))  3 us
    pallas_call x1, Pallas kernels, local(): call(x_factor_kernel, [volume] * 4 + [(5,) + plane, volume], [VMEM, VMEM,...  1.52 us
    pallas_call x1, Pallas kernels, local(): call(load_kernel, [volume, volume, zmajor, (2,) + slab], [HBM, HBM], [plt...  1.38 us
  transfers between devices with their start and end apart: 14, of which 8 were waited for; matrix products, arithmetic and copies ran while one was open for 0% of the time, Pallas kernels for 16%

profile of v7, /device:TPU:0, one launch (start us, length us, event | category | flops | bytes accessed | tf_op | source)
XLA Modules:
  0.0 31.6 jit_solution(10426200802535443318)
XLA Ops:
  0.0 0.9 %shard_map.39.far = f32[2,64,256]{2,1,0:T(8,128)S(1)} custom-call(f32[64,8,256]{2,1,0:T(8,128)} %visc_hbm.3, f32[64,8,256]{2,1,0:T(8,128)} %vel_hbm.3), custom_call_target="tpu_custom_call" | custom-call | bytes 524288 | tf_op jit(solution)/shard_map/pallas_call | solution.py:425
  0.9 0.7 %collective-permute-start.1 = (f32[2,64,256]{2,1,0:T(8,128)S(1)}, f32[2,64,256]{2,1,0:T(8,128)S(1)}, u32[]{:S(2)}, u32[]{:S(2)}) collective-permute-start(f32[2,64,256]{2,1,0:T(8,128)S(1)} %shard_map.39.far), channel_id=1, source_target_pairs={{1,2},{2,1},{3,4},{4,3},{5,6},{6,5},{9,10},{10,9},{11,12},{12,11},... | collective-permute-start | bytes 393224 | tf_op jit(solution)/shard_map/ppermute | solution.py:433
  1.6 1.4 %shard_map.37 = (f32[64,8,256]{2,1,0:T(8,128)S(1)}, f32[64,8,256]{2,1,0:T(8,128)S(1)}, f32[8,64,256]{2,1,0:T(8,128)S(1)}, f32[2,64,256]{2,1,0:T(8,128)S(1)}) custom-call(f32[64,8,256]{2,1,0:T(8,128)} %visc_hbm.3, f32[64,8,256]{2,1,0:T(8,128)} %vel_hbm.3), custom_call_target="tpu_custom_call" | custom-call | flops 131072 | bytes 3145728 | tf_op jit(solution)/shard_map/pallas_call | solution.py:428
  3.0 0.0 copy-start
  3.0 4.3 %collective-permute-start = (f32[2,64,256]{2,1,0:T(8,128)S(1)}, f32[2,64,256]{2,1,0:T(8,128)S(1)}, u32[]{:S(2)}, u32[]{:S(2)}) collective-permute-start(f32[2,64,256]{2,1,0:T(8,128)S(1)} %get-tuple-element.50.near), channel_id=1, source_target_pairs={{0,1},{1,0},{2,3},{3,2},{4,5},{5,4},{6,7},{7,6},{8,9},{9,8},{10,11... | collective-permute-start | bytes 393224 | tf_op jit(solution)/shard_map/ppermute | solution.py:432
  7.3 0.4 %shard_map.43 = (f32[8,64,256]{2,1,0:T(8,128)S(1)}, f32[8,64,256]{2,1,0:T(8,128)S(1)}, f32[8,64,256]{2,1,0:T(8,128)S(1)}, f32[8,64,256]{2,1,0:T(8,128)S(1)}, f32...) custom-call(f32[8,64,256]{2,1,0:T(8,128)S(1)} %get-tuple-element.62.visc_z), custom_call_target="tpu_custom_call" | custom-call | flops 2621440 | bytes 2621440 | tf_op jit(solution)/shard_map/pallas_call | solution.py:436
  7.7 0.1 collective-permute-start.6
  7.8 0.0 copy-done
  7.8 1.5 %shard_map.38 = (f32[64,8,256]{2,1,0:T(8,128)S(1)}, f32[64,8,256]{2,1,0:T(8,128)S(1)}, f32[64,8,256]{2,1,0:T(8,128)S(1)}, f32[64,8,256]{2,1,0:T(8,128)S(1)}, f32...) custom-call(f32[64,8,256]{2,1,0:T(8,128)S(1)} %get-tuple-element.44.visc, ...), custom_call_target="tpu_custom_call" | custom-call | flops 7864320 | bytes 4718592 | tf_op jit(solution)/shard_map/pallas_call | solution.py:440
  9.3 0.0 collective-permute-done.1.cross
  9.4 0.0 collective-permute-done.pair
  9.4 0.3 shard_map.41
  9.6 3.7 %collective-permute-start.2 = (f32[7,8,256]{2,1,0:T(8,128)S(1)}, f32[7,8,256]{2,1,0:T(8,128)S(1)}, u32[]{:S(2)}, u32[]{:S(2)}) collective-permute-start(f32[7,8,256]{2,1,0:T(8,128)S(1)} %get-tuple-element.51.refs_0_), channel_id=1, source_target_pairs={{0,24},{8,16},{16,8},{24,0},{1,25},{9,17},{17,9},{25,1},{2,26},{10... | collective-permute-start | bytes 172040 | tf_op jit(solution)/shard_map/ppermute | solution.py:460
  13.3 0.0 collective-permute-start.3
  13.3 0.8 %collective-permute-start.4 = (f32[7,8,256]{2,1,0:T(8,128)S(1)}, f32[7,8,256]{2,1,0:T(8,128)S(1)}, u32[]{:S(2)}, u32[]{:S(2)}) collective-permute-start(f32[7,8,256]{2,1,0:T(8,128)S(1)} %get-tuple-element.51.refs_0_), channel_id=1, source_target_pairs={{0,8},{8,0},{16,24},{24,16},{1,9},{9,1},{17,25},{25,17},{2,10},{10... | collective-permute-start | bytes 172040 | tf_op jit(solution)/shard_map/ppermute | solution.py:460
  14.1 0.0 collective-permute-done.6.mate
  14.2 3.2 %collective-permute-start.7 = (f32[3,32,256]{2,1,0:T(8,128)S(1)}, f32[3,32,256]{2,1,0:T(8,128)S(1)}, u32[]{:S(2)}, u32[]{:S(2)}) collective-permute-start(f32[3,32,256]{2,1,0:T(8,128)S(1)} %get-tuple-element.73.refs_4_), channel_id=1, source_target_pairs={{0,6},{1,7},{2,4},{3,5},{4,2},{5,3},{6,0},{7,1},{8,14},{9,15},{10,... | collective-permute-start | bytes 294920 | tf_op jit(solution)/shard_map/ppermute | solution.py:471
  17.3 0.0 collective-permute-start.8
  17.3 0.0 collective-permute-done.2.refs_1_
  17.3 0.6 %collective-permute-start.9 = (f32[3,32,256]{2,1,0:T(8,128)S(1)}, f32[3,32,256]{2,1,0:T(8,128)S(1)}, u32[]{:S(2)}, u32[]{:S(2)}) collective-permute-start(f32[3,32,256]{2,1,0:T(8,128)S(1)} %get-tuple-element.73.refs_4_), channel_id=1, source_target_pairs={{0,2},{1,3},{2,0},{3,1},{4,6},{5,7},{6,4},{7,5},{8,10},{9,11},{10,... | collective-permute-start | bytes 294920 | tf_op jit(solution)/shard_map/ppermute | solution.py:471
  18.0 0.6 %shard_map.42 = (f32[32,8,512]{2,1,0:T(8,128)S(1)}, f32[32,8,512]{2,1,0:T(8,128)S(1)}, f32[32,8,512]{2,1,0:T(8,128)S(1)}, f32[32,8,512]{2,1,0:T(8,128)S(1)}, f32...) custom-call(f32[64,8,256]{2,1,0:T(8,128)S(1)} %get-tuple-element.44.visc), custom_call_target="tpu_custom_call" | custom-call | flops 3932160 | bytes 3145728 | tf_op jit(solution)/shard_map/pallas_call | solution.py:444
  18.6 0.1 collective-permute-done.3.refs_2_
  18.7 0.0 collective-permute-done.4.refs_3_
  18.7 0.8 %shard_map.44 = (f32[8,64,256]{2,1,0:T(8,128)S(1)}, f32[2,32,256]{2,1,0:T(8,128)S(1)}, f32[2,32,256]{2,1,0:T(8,128)S(1)}) custom-call(f32[7,8,256]{2,1,0:T(8,128)S(1)} %get-tuple-element.51.refs_0_, f32[7,8,256]{2,1,0:T(8,128)S(1)} %collective-permute-done.2.refs_1_, f32[7,8,256]{2,1,0:T(8,128)S(1)} %collective-permute-done.3.refs_2_, ...), custom_call_target="tpu_custom_call" | custom-call | flops 7864320 | bytes 7340032 | tf_op jit(solution)/shard_map/pallas_call | solution.py:462
  19.5 0.1 collective-permute-start.5
  19.6 0.7 %collective-permute-done.7.refs_5_ = f32[3,32,256]{2,1,0:T(8,128)S(1)} collective-permute-done((f32[3,32,256]{2,1,0:T(8,128)S(1)}, f32[3,32,256]{2,1,0:T(8,128)S(1)}, u32[]{:S(2)}, u32[]{:S(2)}) %collective-permute-start.7) | collective-permute-done | bytes 98336 | tf_op jit(solution)/shard_map/ppermute | solution.py:471
  20.3 1.7 %collective-permute-done.8.refs_6_ = f32[3,32,256]{2,1,0:T(8,128)S(1)} collective-permute-done((f32[3,32,256]{2,1,0:T(8,128)S(1)}, f32[3,32,256]{2,1,0:T(8,128)S(1)}, u32[]{:S(2)}, u32[]{:S(2)}) %collective-permute-start.8) | collective-permute-done | bytes 98336 | tf_op jit(solution)/shard_map/ppermute | solution.py:471
  21.9 0.7 %collective-permute-done.9.refs_7_ = f32[3,32,256]{2,1,0:T(8,128)S(1)} collective-permute-done((f32[3,32,256]{2,1,0:T(8,128)S(1)}, f32[3,32,256]{2,1,0:T(8,128)S(1)}, u32[]{:S(2)}, u32[]{:S(2)}) %collective-permute-start.9) | collective-permute-done | bytes 98336 | tf_op jit(solution)/shard_map/ppermute | solution.py:471
  22.6 0.0 collective-permute-done.5.mate
  22.6 1.6 %collective-permute-start.10 = (f32[2,32,256]{2,1,0:T(8,128)S(1)}, f32[2,32,256]{2,1,0:T(8,128)S(1)}, u32[]{:S(2)}, u32[]{:S(2)}) collective-permute-start(f32[2,32,256]{2,1,0:T(8,128)S(1)} %get-tuple-element.72.refs_0_), channel_id=1, source_target_pairs={{0,6},{1,7},{2,4},{3,5},{4,2},{5,3},{6,0},{7,1},{8,14},{9,15},{10,... | collective-permute-start | bytes 196616 | tf_op jit(solution)/shard_map/ppermute | solution.py:476
  24.2 0.8 %collective-permute-start.11 = (f32[2,32,256]{2,1,0:T(8,128)S(1)}, f32[2,32,256]{2,1,0:T(8,128)S(1)}, u32[]{:S(2)}, u32[]{:S(2)}) collective-permute-start(f32[2,32,256]{2,1,0:T(8,128)S(1)} %get-tuple-element.72.refs_0_), channel_id=1, source_target_pairs={{0,4},{1,5},{2,6},{3,7},{4,0},{5,1},{6,2},{7,3},{8,12},{9,13},{10,... | collective-permute-start | bytes 196616 | tf_op jit(solution)/shard_map/ppermute | solution.py:476
  25.1 1.1 %collective-permute-start.12 = (f32[2,32,256]{2,1,0:T(8,128)S(1)}, f32[2,32,256]{2,1,0:T(8,128)S(1)}, u32[]{:S(2)}, u32[]{:S(2)}) collective-permute-start(f32[2,32,256]{2,1,0:T(8,128)S(1)} %get-tuple-element.72.refs_0_), channel_id=1, source_target_pairs={{0,2},{1,3},{2,0},{3,1},{4,6},{5,7},{6,4},{7,5},{8,10},{9,11},{10,... | collective-permute-start | bytes 196616 | tf_op jit(solution)/shard_map/ppermute | solution.py:476
  26.2 2.2 %collective-permute-done.10.refs_1_ = f32[2,32,256]{2,1,0:T(8,128)S(1)} collective-permute-done((f32[2,32,256]{2,1,0:T(8,128)S(1)}, f32[2,32,256]{2,1,0:T(8,128)S(1)}, u32[]{:S(2)}, u32[]{:S(2)}) %collective-permute-start.10) | collective-permute-done | bytes 65568 | tf_op jit(solution)/shard_map/ppermute | solution.py:476
  28.4 0.4 %collective-permute-done.11.refs_2_ = f32[2,32,256]{2,1,0:T(8,128)S(1)} collective-permute-done((f32[2,32,256]{2,1,0:T(8,128)S(1)}, f32[2,32,256]{2,1,0:T(8,128)S(1)}, u32[]{:S(2)}, u32[]{:S(2)}) %collective-permute-start.11) | collective-permute-done | bytes 65568 | tf_op jit(solution)/shard_map/ppermute | solution.py:476
  28.8 0.5 %collective-permute-done.12.refs_3_ = f32[2,32,256]{2,1,0:T(8,128)S(1)} collective-permute-done((f32[2,32,256]{2,1,0:T(8,128)S(1)}, f32[2,32,256]{2,1,0:T(8,128)S(1)}, u32[]{:S(2)}, u32[]{:S(2)}) %collective-permute-start.12) | collective-permute-done | bytes 65568 | tf_op jit(solution)/shard_map/ppermute | solution.py:476
  29.3 0.1 shard_map.47
  29.5 0.1 collective-permute-start.13
  29.5 1.2 %collective-permute-done.13.got = f32[2,32,256]{2,1,0:T(8,128)S(1)} collective-permute-done((f32[2,32,256]{2,1,0:T(8,128)S(1)}, f32[2,32,256]{2,1,0:T(8,128)S(1)}, u32[]{:S(2)}, u32[]{:S(2)}) %collective-permute-start.13) | collective-permute-done | bytes 65568 | tf_op jit(solution)/shard_map/ppermute | solution.py:481
  30.8 0.9 %shard_map.48 = f32[64,8,256]{2,1,0:T(8,128)} custom-call(f32[2,32,256]{2,1,0:T(8,128)S(1)} %get-tuple-element.78.mine, f32[2,32,256]{2,1,0:T(8,128)S(1)} %collective-permute-done.13.got, f32[8,64,256]{2,1,0:T(8,128)S(1)} %get-tuple-element.80.dz, f32[8,64,256]{2,1,0:T(8,128)S(1)} %get-tuple-element.81.gf, f32[8,64,256]{2,1,0:T(8,128)S(1)} %get-tuple-element.82.gl), custom_call_target="tpu_custom_call" | custom-call | flops 524288 | bytes 2097152 | tf_op jit(solution)/shard_map/pallas_call | solution.py:482
  (3 shorter events, 0.1 us)
Async XLA Ops:
  0.9 8.4 %collective-permute-start.1 = (f32[2,64,256]{2,1,0:T(8,128)S(1)}, f32[2,64,256]{2,1,0:T(8,128)S(1)}, u32[]{:S(2)}, u32[]{:S(2)}) collective-permute-start(f32[2,64,256]{2,1,0:T(8,128)S(1)} %shard_map.39.far), channel_id=1, source_target_pairs={{1,2},{2,1},{3,4},{4,3},{5,6},{6,5},{9,10},{10,9},{11,12},{12,11},... | collective-permute-start | bytes 393224 | tf_op jit(solution)/shard_map/ppermute | solution.py:433
  3.0 4.8 %copy-start = (f32[64,8,256]{2,1,0:T(8,128)S(1)}, f32[64,8,256]{2,1,0:T(8,128)}, u32[]{:S(2)}) copy-start(f32[64,8,256]{2,1,0:T(8,128)} %force_hbm.1) | copy-start | bytes 1572868
  3.0 6.4 %collective-permute-start = (f32[2,64,256]{2,1,0:T(8,128)S(1)}, f32[2,64,256]{2,1,0:T(8,128)S(1)}, u32[]{:S(2)}, u32[]{:S(2)}) collective-permute-start(f32[2,64,256]{2,1,0:T(8,128)S(1)} %get-tuple-element.50.near), channel_id=1, source_target_pairs={{0,1},{1,0},{2,3},{3,2},{4,5},{5,4},{6,7},{7,6},{8,9},{9,8},{10,11... | collective-permute-start | bytes 393224 | tf_op jit(solution)/shard_map/ppermute | solution.py:432
  7.7 6.4 %collective-permute-start.6 = (f32[3,32,256]{2,1,0:T(8,128)S(1)}, f32[3,32,256]{2,1,0:T(8,128)S(1)}, u32[]{:S(2)}, u32[]{:S(2)}) collective-permute-start(f32[3,32,256]{2,1,0:T(8,128)S(1)} %get-tuple-element.68), channel_id=1, source_target_pairs={{0,1},{1,0},{2,3},{3,2},{4,5},{5,4},{6,7},{7,6},{8,9},{9,8},{10,11... | collective-permute-start | bytes 294920 | tf_op jit(solution)/shard_map/ppermute | solution.py:449
  9.6 7.7 %collective-permute-start.2 = (f32[7,8,256]{2,1,0:T(8,128)S(1)}, f32[7,8,256]{2,1,0:T(8,128)S(1)}, u32[]{:S(2)}, u32[]{:S(2)}) collective-permute-start(f32[7,8,256]{2,1,0:T(8,128)S(1)} %get-tuple-element.51.refs_0_), channel_id=1, source_target_pairs={{0,24},{8,16},{16,8},{24,0},{1,25},{9,17},{17,9},{25,1},{2,26},{10... | collective-permute-start | bytes 172040 | tf_op jit(solution)/shard_map/ppermute | solution.py:460
  13.3 5.4 %collective-permute-start.3 = (f32[7,8,256]{2,1,0:T(8,128)S(1)}, f32[7,8,256]{2,1,0:T(8,128)S(1)}, u32[]{:S(2)}, u32[]{:S(2)}) collective-permute-start(f32[7,8,256]{2,1,0:T(8,128)S(1)} %get-tuple-element.51.refs_0_), channel_id=1, source_target_pairs={{0,16},{8,24},{16,0},{24,8},{1,17},{9,25},{17,1},{25,9},{2,18},{10... | collective-permute-start | bytes 172040 | tf_op jit(solution)/shard_map/ppermute | solution.py:460
  13.3 5.4 %collective-permute-start.4 = (f32[7,8,256]{2,1,0:T(8,128)S(1)}, f32[7,8,256]{2,1,0:T(8,128)S(1)}, u32[]{:S(2)}, u32[]{:S(2)}) collective-permute-start(f32[7,8,256]{2,1,0:T(8,128)S(1)} %get-tuple-element.51.refs_0_), channel_id=1, source_target_pairs={{0,8},{8,0},{16,24},{24,16},{1,9},{9,1},{17,25},{25,17},{2,10},{10... | collective-permute-start | bytes 172040 | tf_op jit(solution)/shard_map/ppermute | solution.py:460
  14.2 6.1 %collective-permute-start.7 = (f32[3,32,256]{2,1,0:T(8,128)S(1)}, f32[3,32,256]{2,1,0:T(8,128)S(1)}, u32[]{:S(2)}, u32[]{:S(2)}) collective-permute-start(f32[3,32,256]{2,1,0:T(8,128)S(1)} %get-tuple-element.73.refs_4_), channel_id=1, source_target_pairs={{0,6},{1,7},{2,4},{3,5},{4,2},{5,3},{6,0},{7,1},{8,14},{9,15},{10,... | collective-permute-start | bytes 294920 | tf_op jit(solution)/shard_map/ppermute | solution.py:471
  17.3 4.6 %collective-permute-start.8 = (f32[3,32,256]{2,1,0:T(8,128)S(1)}, f32[3,32,256]{2,1,0:T(8,128)S(1)}, u32[]{:S(2)}, u32[]{:S(2)}) collective-permute-start(f32[3,32,256]{2,1,0:T(8,128)S(1)} %get-tuple-element.73.refs_4_), channel_id=1, source_target_pairs={{0,4},{1,5},{2,6},{3,7},{4,0},{5,1},{6,2},{7,3},{8,12},{9,13},{10,... | collective-permute-start | bytes 294920 | tf_op jit(solution)/shard_map/ppermute | solution.py:471
  17.3 5.3 %collective-permute-start.9 = (f32[3,32,256]{2,1,0:T(8,128)S(1)}, f32[3,32,256]{2,1,0:T(8,128)S(1)}, u32[]{:S(2)}, u32[]{:S(2)}) collective-permute-start(f32[3,32,256]{2,1,0:T(8,128)S(1)} %get-tuple-element.73.refs_4_), channel_id=1, source_target_pairs={{0,2},{1,3},{2,0},{3,1},{4,6},{5,7},{6,4},{7,5},{8,10},{9,11},{10,... | collective-permute-start | bytes 294920 | tf_op jit(solution)/shard_map/ppermute | solution.py:471
  19.5 3.1 %collective-permute-start.5 = (f32[2,32,256]{2,1,0:T(8,128)S(1)}, f32[2,32,256]{2,1,0:T(8,128)S(1)}, u32[]{:S(2)}, u32[]{:S(2)}) collective-permute-start(f32[2,32,256]{2,1,0:T(8,128)S(1)} %get-tuple-element.66), channel_id=1, source_target_pairs={{0,1},{1,0},{2,3},{3,2},{4,5},{5,4},{6,7},{7,6},{8,9},{9,8},{10,11... | collective-permute-start | bytes 196616 | tf_op jit(solution)/shard_map/ppermute | solution.py:470
  22.6 5.7 %collective-permute-start.10 = (f32[2,32,256]{2,1,0:T(8,128)S(1)}, f32[2,32,256]{2,1,0:T(8,128)S(1)}, u32[]{:S(2)}, u32[]{:S(2)}) collective-permute-start(f32[2,32,256]{2,1,0:T(8,128)S(1)} %get-tuple-element.72.refs_0_), channel_id=1, source_target_pairs={{0,6},{1,7},{2,4},{3,5},{4,2},{5,3},{6,0},{7,1},{8,14},{9,15},{10,... | collective-permute-start | bytes 196616 | tf_op jit(solution)/shard_map/ppermute | solution.py:476
  24.2 4.5 %collective-permute-start.11 = (f32[2,32,256]{2,1,0:T(8,128)S(1)}, f32[2,32,256]{2,1,0:T(8,128)S(1)}, u32[]{:S(2)}, u32[]{:S(2)}) collective-permute-start(f32[2,32,256]{2,1,0:T(8,128)S(1)} %get-tuple-element.72.refs_0_), channel_id=1, source_target_pairs={{0,4},{1,5},{2,6},{3,7},{4,0},{5,1},{6,2},{7,3},{8,12},{9,13},{10,... | collective-permute-start | bytes 196616 | tf_op jit(solution)/shard_map/ppermute | solution.py:476
  25.1 4.3 %collective-permute-start.12 = (f32[2,32,256]{2,1,0:T(8,128)S(1)}, f32[2,32,256]{2,1,0:T(8,128)S(1)}, u32[]{:S(2)}, u32[]{:S(2)}) collective-permute-start(f32[2,32,256]{2,1,0:T(8,128)S(1)} %get-tuple-element.72.refs_0_), channel_id=1, source_target_pairs={{0,2},{1,3},{2,0},{3,1},{4,6},{5,7},{6,4},{7,5},{8,10},{9,11},{10,... | collective-permute-start | bytes 196616 | tf_op jit(solution)/shard_map/ppermute | solution.py:476
  29.5 1.3 %collective-permute-start.13 = (f32[2,32,256]{2,1,0:T(8,128)S(1)}, f32[2,32,256]{2,1,0:T(8,128)S(1)}, u32[]{:S(2)}, u32[]{:S(2)}) collective-permute-start(f32[2,32,256]{2,1,0:T(8,128)S(1)} %get-tuple-element.79), channel_id=1, source_target_pairs={{0,1},{1,0},{2,3},{3,2},{4,5},{5,4},{6,7},{7,6},{8,9},{9,8},{10,11... | collective-permute-start | bytes 196616 | tf_op jit(solution)/shard_map/ppermute | solution.py:481
